TPU v7x, 512 devices: a whole 4x8x8 slice. The times are simulated.
512 devices in a mesh: section: 4 (over x), strip: 128 (over z, y, core).
Axes of the slice: x: 4, y: 8, z: 8, core: 2. Of those that a mesh axis runs over, the one named last changes fastest.
Arguments:
- cotangent: bfloat16 [1, 8192, 2048], P(None, 'strip'), may hold values from -6 to 6
- activations: bfloat16 [4, 1, 8192, 2048], P('section', None, 'strip'), may hold values from -6 to 6
- weights: bfloat16 [4, 2, 3, 3, 64, 64], P('section'), may hold values from -0.25 to 0.25
- biases: float32 [4, 2, 64], P('section'), may hold values from -3 to 3
Outputs:
- noise_grad: bfloat16 [4, 1, 8192, 2048], P('section', None, 'strip')
- weight_grad: float32 [4, 2, 3, 3, 64, 64], P('section')
- bias_grad: float32 [4, 2, 64], P('section')
All inputs are finite; a program needn't handle non-finite values.
Results may differ from a plain program's by a relative error of at most 0.01.
Values may be sent and summed in bfloat16 or wider, within the bound.
A program may use at most 64 MiB of HBM per device.

v0:
```python
import jax
import jax.numpy as jnp
from jax import lax
from jax.sharding import PartitionSpec as P

LEAK = 0.05


def extended_2(cells, sides, width):
    for axis, dim in sides:
        count = lax.axis_size(axis)
        ends = count - 1
        head = lax.slice_in_dim(cells, 0, width, axis=dim)
        tail = lax.slice_in_dim(cells, cells.shape[dim] - width, cells.shape[dim], axis=dim)
        cells = jnp.concatenate(
            [
                lax.ppermute(tail, axis, [(i, (i + 1) % count) for i in range(ends)]),
                cells,
                lax.ppermute(head, axis, [((i + 1) % count, i) for i in range(ends)]),
            ],
            axis=dim,
        )
    return cells


def shifted_2(x, axis, by):
    peers = lax.axis_size(axis)
    pairs = [(i, i + by) for i in range(peers) if 0 <= i + by < peers]
    return lax.ppermute(x, axis, pairs)


def activate(value):
    return LEAK * value + (1.0 - LEAK) * jax.nn.softplus(value)


def steepness(value):
    return LEAK + (1.0 - LEAK) * jax.nn.sigmoid(value)


def conv_rows(field_in, kernel):
    return lax.conv_general_dilated(
        field_in,
        kernel,
        (1, 1),
        ((0, 0), (1, 1)),
        dimension_numbers=("NHWC", "HWIO", "NHWC"),
        preferred_element_type=jnp.float32,
    )


def flipped(kernel):
    return jnp.transpose(kernel[::-1, ::-1], (0, 1, 3, 2))


def weight_taps(extended, error):
    padded = jnp.pad(extended, ((0, 0), (0, 0), (1, 1), (0, 0)))
    height = error.shape[1]
    col_span = error.shape[2]
    channels = error.shape[3]
    tap_list = []
    for row_tap in range(3):
        for col_tap in range(3):
            window = padded[:, row_tap : row_tap + height, col_tap : col_tap + col_span]
            tap_list.append(
                lax.dot_general(
                    window,
                    error,
                    (((0, 1, 2), (0, 1, 2)), ((), ())),
                    preferred_element_type=jnp.float32,
                )
            )
    return jnp.stack(tap_list).reshape(3, 3, channels, channels)


def edge_rows(field_in, rim_depth, live_rows):
    upper_rows = field_in[:, :rim_depth]
    lower_rows = lax.dynamic_slice_in_dim(field_in, live_rows - rim_depth, rim_depth, 1)
    return jnp.concatenate([upper_rows, lower_rows], axis=1)


def attach(field_in, received, rim_depth, live_rows):
    upper_rows = received[:, :rim_depth]
    lower_rows = received[:, 3 * rim_depth :]
    filler = jnp.zeros_like(upper_rows)
    joined = jnp.concatenate([upper_rows, field_in, filler], axis=1)
    return lax.dynamic_update_slice_in_dim(joined, lower_rows, live_rows + rim_depth, 1)


def local(cotangent, activations, weights, biases):
    section_id = lax.axis_index("section")
    strip_id = lax.axis_index("strip")
    strip_count = lax.axis_size("strip")
    section_count = lax.axis_size("section")
    samples, row_count, flat_width = cotangent.shape
    channels = weights.shape[-1]
    col_count = flat_width // channels
    coarse_rows = row_count * 3 // 4
    coarse_cols = col_count * 3 // 4
    row_table = jnp.array(
        [
            row_count * 3**section_level // 4**section_level
            for section_level in range(section_count)
        ],
        jnp.int32,
    )
    col_table = jnp.array(
        [
            col_count * 3**section_level // 4**section_level
            for section_level in range(section_count)
        ],
        jnp.int32,
    )
    live_rows = row_table[section_id]
    live_cols = col_table[section_id]
    row_index = lax.iota(jnp.int32, row_count)
    col_index = lax.iota(jnp.int32, col_count)
    col_live = col_index < live_cols
    keep_mask = ((row_index < live_rows)[:, None, None] & col_live[None, :, None]).astype(
        jnp.float32
    )
    kernel_in = weights[0, 0]
    kernel_out = weights[0, 1]
    kernel_in_back = flipped(kernel_in)
    kernel_out_back = flipped(kernel_out)
    bias_in = biases[0, 0]
    bias_out = biases[0, 1]
    cot_grid = cotangent.reshape(samples, row_count, col_count, channels)
    act_grid = activations[0].reshape(samples, row_count, col_count, channels)
    group_count = samples // samples
    tick_count = group_count + section_count - 1

    def section_backward(grad_out, field_in):
        got_input = extended_2(edge_rows(field_in, 1, live_rows), (("strip", 1),), 1)
        input_ext = attach(field_in, got_input, 1, live_rows)
        pre_in = conv_rows(input_ext, kernel_in) + bias_in
        hidden = (activate(pre_in) * keep_mask).astype(jnp.bfloat16)
        got_hidden = extended_2(edge_rows(hidden, 1, live_rows), (("strip", 1),), 1)
        hidden_ext = attach(hidden, got_hidden, 1, live_rows)
        pre_out = conv_rows(hidden_ext, kernel_out) + bias_out
        error_out = (grad_out.astype(jnp.float32) * steepness(pre_out) * keep_mask).astype(
            jnp.bfloat16
        )
        got_error = extended_2(edge_rows(error_out, 1, live_rows), (("strip", 1),), 1)
        error_ext = attach(error_out, got_error, 1, live_rows)
        back_hidden = conv_rows(error_ext, kernel_out_back)
        error_in = (back_hidden * steepness(pre_in) * keep_mask).astype(jnp.bfloat16)
        got_inner = extended_2(edge_rows(error_in, 1, live_rows), (("strip", 1),), 1)
        inner_ext = attach(error_in, got_inner, 1, live_rows)
        back_input = conv_rows(inner_ext, kernel_in_back) * keep_mask
        noise_part = back_input.astype(jnp.bfloat16)
        grad_up = (grad_out.astype(jnp.float32) + back_input).astype(jnp.bfloat16)
        kernel_grads = jnp.stack(
            [weight_taps(input_ext, error_in), weight_taps(hidden_ext, error_out)]
        )
        bias_grads = jnp.stack(
            [
                jnp.sum(error_in, axis=(0, 1, 2), dtype=jnp.float32),
                jnp.sum(error_out, axis=(0, 1, 2), dtype=jnp.float32),
            ]
        )
        return (noise_part, grad_up, kernel_grads, bias_grads)

    def coarse_grad(grad_up, fine_level):
        coarse_level = jnp.minimum(fine_level + 1, section_count - 1)
        fine_height = row_table[fine_level]
        coarse_height = row_table[coarse_level]
        fine_width = col_table[fine_level]
        coarse_width = col_table[coarse_level]
        global_row = strip_id * fine_height + row_index
        row_num = jnp.maximum(6 * global_row - 1, 0)
        row_low = row_num // 8
        row_frac = (row_num - 8 * row_low).astype(jnp.float32) / 8.0
        row_high = jnp.minimum(row_low + 1, strip_count * coarse_height - 1)
        row_on = (row_index < fine_height).astype(jnp.float32)
        base_row = strip_id * coarse_height - 1
        target_row = lax.iota(jnp.int32, coarse_rows + 2)[:, None]
        row_matrix = (
            jnp.where(target_row == (row_low - base_row)[None, :], 1.0 - row_frac[None, :], 0.0)
            + jnp.where(target_row == (row_high - base_row)[None, :], row_frac[None, :], 0.0)
        ) * row_on[None, :]
        col_num = jnp.maximum((2 * col_index + 1) * coarse_width - fine_width, 0)
        col_den = 2 * fine_width
        col_low = col_num // col_den
        col_frac = (col_num - col_den * col_low).astype(jnp.float32) / col_den.astype(jnp.float32)
        col_high = jnp.minimum(col_low + 1, coarse_width - 1)
        col_on = (col_index < fine_width).astype(jnp.float32)
        target_col = lax.iota(jnp.int32, coarse_cols)[:, None]
        col_matrix = (
            jnp.where(target_col == col_low[None, :], 1.0 - col_frac[None, :], 0.0)
            + jnp.where(target_col == col_high[None, :], col_frac[None, :], 0.0)
        ) * col_on[None, :]
        wide_grad = grad_up.astype(jnp.float32)
        partial_cols = jnp.einsum(
            "gyxc,kx->gykc", wide_grad, col_matrix, precision=lax.Precision.HIGHEST
        )
        summed = jnp.einsum(
            "ry,gykc->grkc", row_matrix, partial_cols, precision=lax.Precision.HIGHEST
        )
        rim_pair = jnp.concatenate(
            [summed[:, :1], lax.dynamic_slice_in_dim(summed, coarse_height + 1, 1, 1)], axis=1
        )
        got_rims = extended_2(rim_pair, (("strip", 1),), 1)
        core_rows = summed[:, 1 : coarse_rows + 1]
        index_row = lax.iota(jnp.int32, coarse_rows)[None, :, None, None]
        core_rows = (
            core_rows
            + jnp.where(index_row == 0, got_rims[:, :1], 0.0)
            + jnp.where(index_row == coarse_height - 1, got_rims[:, 3:], 0.0)
        )
        coarse_mask = (
            (lax.iota(jnp.int32, coarse_rows) < coarse_height)[:, None, None]
            & (lax.iota(jnp.int32, coarse_cols) < coarse_width)[None, :, None]
        ).astype(jnp.float32)
        return (core_rows * coarse_mask).astype(jnp.bfloat16)

    def expand(coarse):
        return jnp.pad(
            coarse, ((0, 0), (0, row_count - coarse_rows), (0, col_count - coarse_cols), (0, 0))
        )

    def one_tick(tick_index, state_in):
        incoming, noise_acc, kernel_acc, bias_acc = state_in
        group_index = tick_index - section_id
        active = (group_index >= 0) & (group_index < group_count)
        start_row = jnp.clip(group_index, 0, group_count - 1) * samples
        grad_out = jnp.where(section_id == 0, cot_grid, incoming)
        field_in = (act_grid.astype(jnp.float32) * keep_mask).astype(jnp.bfloat16)
        noise_part, grad_up, kernel_grads, bias_grads = section_backward(grad_out, field_in)
        shifted = shifted_2(grad_up, "section", 1)
        next_in = expand(coarse_grad(shifted, jnp.maximum(section_id - 1, 0)))
        old_noise = noise_acc
        noise_acc = lax.dynamic_update_slice_in_dim(
            noise_acc, jnp.where(active, noise_part, old_noise), start_row, 0
        )
        weight_on = active.astype(jnp.float32)
        return (
            next_in,
            noise_acc,
            kernel_acc + weight_on * kernel_grads,
            bias_acc + weight_on * bias_grads,
        )

    initial = (
        jnp.zeros((samples, row_count, col_count, channels), jnp.bfloat16),
        jnp.zeros((samples, row_count, col_count, channels), jnp.bfloat16),
        jnp.zeros((2, 3, 3, channels, channels), jnp.float32),
        jnp.zeros((2, channels), jnp.float32),
    )
    final_state = lax.fori_loop(0, tick_count, one_tick, initial)
    noise_acc = final_state[1]
    kernel_sum, bias_sum = lax.psum((final_state[2], final_state[3]), "strip")
    pixel_count = (samples * strip_count * live_rows * live_cols).astype(jnp.float32)
    scale_back = 1.0 / jnp.sqrt(pixel_count)
    return (
        noise_acc.reshape(1, samples, row_count, flat_width),
        (kernel_sum * scale_back)[None],
        (bias_sum * scale_back)[None],
    )


def solution(mesh):
    return jax.shard_map(
        local,
        mesh=mesh,
        in_specs=(
            P(None, "strip", None),
            P("section", None, "strip", None),
            P("section", None, None, None, None, None),
            P("section", None, None),
        ),
        out_specs=(
            P("section", None, "strip", None),
            P("section", None, None, None, None, None),
            P("section", None, None),
        ),
        check_vma=False,
    )
```

profile of v0, /device:TPU:259, one launch (start us, length us, event | category | flops | bytes accessed | tf_op | source)
XLA Modules:
  0.0 627.0 jit_solution(17448121383241691999)
XLA Ops:
  13.2 3.8 collective-permute-start.11
  17.0 1.9 collective-permute-start.12
  30.3 3.8 dynamic_update_slice.63
  34.8 1.7 fusion.155
  37.5 3.6 collective-permute-start.13
  41.2 4.1 collective-permute-start.14
  45.6 1.6 copy.183
  50.8 312.7 %while.25 = (s32[]{:T(128)}, bf16[1,64,32,64]{3,1,2,0:T(8,128)(2,1)S(1)}, bf16[1,64,32,64]{3,2,1,0:T(8,128)(2,1)}, f32[2,3,3,64,64]{4,3,2,1,0:T(8,128)}, f32[2,6...) while((s32[]{:T(128)}, ...), condition=%wide.region_3.4_spmd.clone.clone, body=%wide.region_0.3_spmd.clone.clone.sunk | while | flops 787387328 | bytes 55671280 | solution.py:249
  51.9 1.9 collective-permute-start
  53.8 7.0 %collective-permute-start.1 = (bf16[1,1,32,64]{3,2,1,0:T(8,128)(2,1)S(1)}, bf16[1,1,32,64]{3,2,1,0:T(8,128)(2,1)S(1)}, u32[]{:S(2)}, u32[]{:S(2)}) collective-permute-start(bf16[1,1,32,64]{3,2,1,0:T(8,128)(2,1)S(1)} %get-tuple-element.1605), channel_id=1, source_target_pairs={{1,0},{2,1},{3,2},{4,3},{5,4},{6,5},{7,6},{8,7},{9,8},{10,9},{11,1... | collective-permute-start | bytes 12296 | tf_op jit(solution)/shard_map/while/body/eval_jaxpr/ppermute | solution.py:19
  66.6 2.0 convolution_select_fusion.6
  70.1 1.5 convert_reduce_fusion.5
  71.6 1.9 collective-permute-start.2
  73.6 1.9 collective-permute-start.3
  75.5 1.9 collective-permute-start.4
  77.4 7.0 %collective-permute-start.10 = (bf16[1,1,32,64]{3,2,1,0:T(8,128)(2,1)S(1)}, bf16[1,1,32,64]{3,2,1,0:T(8,128)(2,1)S(1)}, u32[]{:S(2)}, u32[]{:S(2)}) collective-permute-start(bf16[1,1,32,64]{3,2,1,0:T(8,128)(2,1)S(1)} %get-tuple-element.1624), channel_id=1, source_target_pairs={{1,0},{2,1},{3,2},{4,3},{5,4},{6,5},{7,6},{8,7},{9,8},{10,9},{11,1... | collective-permute-start | bytes 12296 | tf_op jit(solution)/shard_map/while/body/eval_jaxpr/ppermute | solution.py:19
  84.4 7.0 %collective-permute-start.9 = (bf16[1,1,32,64]{3,2,1,0:T(8,128)(2,1)S(1)}, bf16[1,1,32,64]{3,2,1,0:T(8,128)(2,1)S(1)}, u32[]{:S(2)}, u32[]{:S(2)}) collective-permute-start(bf16[1,1,32,64]{3,2,1,0:T(8,128)(2,1)S(1)} %get-tuple-element.1622), channel_id=1, source_target_pairs={{1,0},{2,1},{3,2},{4,3},{5,4},{6,5},{7,6},{8,7},{9,8},{10,9},{11,1... | collective-permute-start | bytes 12296 | tf_op jit(solution)/shard_map/while/body/eval_jaxpr/ppermute | solution.py:19
  91.4 2.4 collective-permute-start.5
  105.0 3.1 collective-permute-start.6
  109.1 9.5 %collective-permute-done.6 = bf16[1,64,32,64]{3,2,1,0:T(8,128)(2,1)S(1)} collective-permute-done((bf16[1,64,32,64]{3,2,1,0:T(8,128)(2,1)S(1)}, bf16[1,64,32,64]{3,2,1,0:T(8,128)(2,1)S(1)}, u32[]{:S(2)}, u32[]{:S(2)}) %collective-permute-start.6) | collective-permute-done | bytes 262176 | tf_op jit(solution)/shard_map/while/body/eval_jaxpr/ppermute | solution.py:29
  120.0 4.6 collective-permute-start.7
  124.6 1.9 collective-permute-start.8
  129.5 3.4 collective-permute-start
  132.9 6.2 collective-permute-start.1
  144.9 2.0 convolution_select_fusion.6
  149.9 1.9 collective-permute-start.2
  151.9 1.9 collective-permute-start.3
  153.8 1.9 collective-permute-start.4
  155.7 7.0 %collective-permute-start.10 = (bf16[1,1,32,64]{3,2,1,0:T(8,128)(2,1)S(1)}, bf16[1,1,32,64]{3,2,1,0:T(8,128)(2,1)S(1)}, u32[]{:S(2)}, u32[]{:S(2)}) collective-permute-start(bf16[1,1,32,64]{3,2,1,0:T(8,128)(2,1)S(1)} %get-tuple-element.1624), channel_id=1, source_target_pairs={{1,0},{2,1},{3,2},{4,3},{5,4},{6,5},{7,6},{8,7},{9,8},{10,9},{11,1... | collective-permute-start | bytes 12296 | tf_op jit(solution)/shard_map/while/body/eval_jaxpr/ppermute | solution.py:19
  162.7 7.0 %collective-permute-start.9 = (bf16[1,1,32,64]{3,2,1,0:T(8,128)(2,1)S(1)}, bf16[1,1,32,64]{3,2,1,0:T(8,128)(2,1)S(1)}, u32[]{:S(2)}, u32[]{:S(2)}) collective-permute-start(bf16[1,1,32,64]{3,2,1,0:T(8,128)(2,1)S(1)} %get-tuple-element.1622), channel_id=1, source_target_pairs={{1,0},{2,1},{3,2},{4,3},{5,4},{6,5},{7,6},{8,7},{9,8},{10,9},{11,1... | collective-permute-start | bytes 12296 | tf_op jit(solution)/shard_map/while/body/eval_jaxpr/ppermute | solution.py:19
  169.7 2.4 collective-permute-start.5
  183.3 3.1 collective-permute-start.6
  187.4 9.5 %collective-permute-done.6 = bf16[1,64,32,64]{3,2,1,0:T(8,128)(2,1)S(1)} collective-permute-done((bf16[1,64,32,64]{3,2,1,0:T(8,128)(2,1)S(1)}, bf16[1,64,32,64]{3,2,1,0:T(8,128)(2,1)S(1)}, u32[]{:S(2)}, u32[]{:S(2)}) %collective-permute-start.6) | collective-permute-done | bytes 262176 | tf_op jit(solution)/shard_map/while/body/eval_jaxpr/ppermute | solution.py:29
  198.3 4.6 collective-permute-start.7
  202.9 1.9 collective-permute-start.8
  207.8 3.4 collective-permute-start
  211.2 6.2 collective-permute-start.1
  223.2 2.0 convolution_select_fusion.6
  228.2 1.9 collective-permute-start.2
  230.2 1.9 collective-permute-start.3
  232.1 1.9 collective-permute-start.4
  234.0 7.0 %collective-permute-start.10 = (bf16[1,1,32,64]{3,2,1,0:T(8,128)(2,1)S(1)}, bf16[1,1,32,64]{3,2,1,0:T(8,128)(2,1)S(1)}, u32[]{:S(2)}, u32[]{:S(2)}) collective-permute-start(bf16[1,1,32,64]{3,2,1,0:T(8,128)(2,1)S(1)} %get-tuple-element.1624), channel_id=1, source_target_pairs={{1,0},{2,1},{3,2},{4,3},{5,4},{6,5},{7,6},{8,7},{9,8},{10,9},{11,1... | collective-permute-start | bytes 12296 | tf_op jit(solution)/shard_map/while/body/eval_jaxpr/ppermute | solution.py:19
  241.0 7.0 %collective-permute-start.9 = (bf16[1,1,32,64]{3,2,1,0:T(8,128)(2,1)S(1)}, bf16[1,1,32,64]{3,2,1,0:T(8,128)(2,1)S(1)}, u32[]{:S(2)}, u32[]{:S(2)}) collective-permute-start(bf16[1,1,32,64]{3,2,1,0:T(8,128)(2,1)S(1)} %get-tuple-element.1622), channel_id=1, source_target_pairs={{1,0},{2,1},{3,2},{4,3},{5,4},{6,5},{7,6},{8,7},{9,8},{10,9},{11,1... | collective-permute-start | bytes 12296 | tf_op jit(solution)/shard_map/while/body/eval_jaxpr/ppermute | solution.py:19
  248.0 2.4 collective-permute-start.5
  261.6 3.1 collective-permute-start.6
  265.7 9.5 %collective-permute-done.6 = bf16[1,64,32,64]{3,2,1,0:T(8,128)(2,1)S(1)} collective-permute-done((bf16[1,64,32,64]{3,2,1,0:T(8,128)(2,1)S(1)}, bf16[1,64,32,64]{3,2,1,0:T(8,128)(2,1)S(1)}, u32[]{:S(2)}, u32[]{:S(2)}) %collective-permute-start.6) | collective-permute-done | bytes 262176 | tf_op jit(solution)/shard_map/while/body/eval_jaxpr/ppermute | solution.py:29
  276.6 4.6 collective-permute-start.7
  281.2 1.9 collective-permute-start.8
  286.1 3.4 collective-permute-start
  289.5 6.2 collective-permute-start.1
  301.5 2.0 convolution_select_fusion.6
  306.5 1.9 collective-permute-start.2
  308.5 1.9 collective-permute-start.3
  310.4 1.9 collective-permute-start.4
  312.3 7.0 %collective-permute-start.10 = (bf16[1,1,32,64]{3,2,1,0:T(8,128)(2,1)S(1)}, bf16[1,1,32,64]{3,2,1,0:T(8,128)(2,1)S(1)}, u32[]{:S(2)}, u32[]{:S(2)}) collective-permute-start(bf16[1,1,32,64]{3,2,1,0:T(8,128)(2,1)S(1)} %get-tuple-element.1624), channel_id=1, source_target_pairs={{1,0},{2,1},{3,2},{4,3},{5,4},{6,5},{7,6},{8,7},{9,8},{10,9},{11,1... | collective-permute-start | bytes 12296 | tf_op jit(solution)/shard_map/while/body/eval_jaxpr/ppermute | solution.py:19
  319.3 7.0 %collective-permute-start.9 = (bf16[1,1,32,64]{3,2,1,0:T(8,128)(2,1)S(1)}, bf16[1,1,32,64]{3,2,1,0:T(8,128)(2,1)S(1)}, u32[]{:S(2)}, u32[]{:S(2)}) collective-permute-start(bf16[1,1,32,64]{3,2,1,0:T(8,128)(2,1)S(1)} %get-tuple-element.1622), channel_id=1, source_target_pairs={{1,0},{2,1},{3,2},{4,3},{5,4},{6,5},{7,6},{8,7},{9,8},{10,9},{11,1... | collective-permute-start | bytes 12296 | tf_op jit(solution)/shard_map/while/body/eval_jaxpr/ppermute | solution.py:19
  326.3 2.4 collective-permute-start.5
  339.9 3.1 collective-permute-start.6
  343.9 9.6 %collective-permute-done.6 = bf16[1,64,32,64]{3,2,1,0:T(8,128)(2,1)S(1)} collective-permute-done((bf16[1,64,32,64]{3,2,1,0:T(8,128)(2,1)S(1)}, bf16[1,64,32,64]{3,2,1,0:T(8,128)(2,1)S(1)}, u32[]{:S(2)}, u32[]{:S(2)}) %collective-permute-start.6) | collective-permute-done | bytes 262176 | tf_op jit(solution)/shard_map/while/body/eval_jaxpr/ppermute | solution.py:29
  354.9 4.6 collective-permute-start.7
  359.5 1.9 collective-permute-start.8
  363.5 2.2 reshape.737
  365.7 252.0 %psum.15 = f32[2,64]{1,0:T(2,128)S(1)} all-reduce(f32[2,64]{1,0:T(2,128)S(1)} %get-tuple-element.969), channel_id=1, replica_groups=mesh['section'=4,'strip'=128] {'strip'}, use_global_device_ids=true, to_apply=%region_5.6 | all-reduce | flops 128 | bytes 1024 | tf_op jit(solution)/shard_map/psum | solution.py:251
  618.2 1.9 multiply_bitcast_fusion
  (457 shorter events, 112.0 us)
Async XLA Ops:
  7.2 11.8 %copy-start.14 = (f32[1,2,64]{2,1,0:T(2,128)S(1)}, f32[1,2,64]{2,1,0:T(2,128)}, u32[]{:S(2)}) copy-start(f32[1,2,64]{2,1,0:T(2,128)} %param.11) | copy-start | bytes 1540
  7.2 11.8 %copy-start.11 = (bf16[1,2,3,3,64,64]{5,4,3,2,1,0:T(8,128)(2,1)S(1)}, bf16[1,2,3,3,64,64]{5,4,3,2,1,0:T(8,128)(2,1)}, u32[]{:S(2)}) copy-start(bf16[1,2,3,3,64,64]{5,4,3,2,1,0:T(8,128)(2,1)} %param.10) | copy-start | bytes 442372
  7.2 611.0 %all-reduce.5.cloned.1.call-start = ((), (), s32[]{:S(2)}) async-start(), calls=%async_computation | async-start | bytes 1179648 | tf_op jit(solution)/shard_map/psum | solution.py:251
  12.9 14.4 %copy-start.12 = (bf16[1,64,2048]{2,1,0:T(8,128)(2,1)S(1)}, bf16[1,64,2048]{2,1,0:T(8,128)(2,1)}, u32[]{:S(2)}) copy-start(bf16[1,64,2048]{2,1,0:T(8,128)(2,1)} %param.8) | copy-start | bytes 786436
  13.2 15.9 %collective-permute-start.11 = (bf16[1,1,32,64]{3,2,1,0:T(8,128)(2,1)S(1)}, bf16[1,1,32,64]{3,2,1,0:T(8,128)(2,1)S(1)}, u32[]{:S(2)}, u32[]{:S(2)}) collective-permute-start(bf16[1,1,32,64]{3,2,1,0:T(8,128)(2,1)S(1)} %get-tuple-element.1367), channel_id=1, source_target_pairs={{0,1},{1,2},{2,3},{3,4},{4,5},{5,6},{6,7},{7,8},{8,9},{9,10},{10,1... | collective-permute-start | bytes 12296 | tf_op jit(solution)/shard_map/while/body/eval_jaxpr/ppermute | solution.py:17
  17.0 12.9 %collective-permute-start.12 = (bf16[1,1,32,64]{3,2,1,0:T(8,128)(2,1)S(1)}, bf16[1,1,32,64]{3,2,1,0:T(8,128)(2,1)S(1)}, u32[]{:S(2)}, u32[]{:S(2)}) collective-permute-start(bf16[1,1,32,64]{3,2,1,0:T(8,128)(2,1)S(1)} %get-tuple-element.1366), channel_id=1, source_target_pairs={{1,0},{2,1},{3,2},{4,3},{5,4},{6,5},{7,6},{8,7},{9,8},{10,9},{11,1... | collective-permute-start | bytes 12296 | tf_op jit(solution)/shard_map/while/body/eval_jaxpr/ppermute | solution.py:19
  37.5 9.7 %collective-permute-start.13 = (bf16[1,1,32,64]{3,0,2,1:T(2,128)(2,1)S(1)}, bf16[1,1,32,64]{3,0,2,1:T(2,128)(2,1)S(1)}, u32[]{:S(2)}, u32[]{:S(2)}) collective-permute-start(bf16[1,1,32,64]{3,0,2,1:T(2,128)(2,1)S(1)} %constant_dynamic-slice_fusion.5), channel_id=1, source_target_pairs={{0,1},{1,2},{2,3},{3,4},{4,5},{5,6},{6,7},{7,8},{8,9},{9,10},{10,1... | collective-permute-start | bytes 12296 | tf_op jit(solution)/shard_map/while/body/eval_jaxpr/ppermute | solution.py:17
  41.2 6.3 collective-permute-start.14
  51.9 13.1 %collective-permute-start = (bf16[1,1,32,64]{3,2,1,0:T(8,128)(2,1)S(1)}, bf16[1,1,32,64]{3,2,1,0:T(8,128)(2,1)S(1)}, u32[]{:S(2)}, u32[]{:S(2)}) collective-permute-start(bf16[1,1,32,64]{3,2,1,0:T(8,128)(2,1)S(1)} %get-tuple-element.1604), channel_id=1, source_target_pairs={{0,1},{1,2},{2,3},{3,4},{4,5},{5,6},{6,7},{7,8},{8,9},{9,10},{10,1... | collective-permute-start | bytes 12296 | tf_op jit(solution)/shard_map/while/body/eval_jaxpr/ppermute | solution.py:17
  53.8 11.4 %collective-permute-start.1 = (bf16[1,1,32,64]{3,2,1,0:T(8,128)(2,1)S(1)}, bf16[1,1,32,64]{3,2,1,0:T(8,128)(2,1)S(1)}, u32[]{:S(2)}, u32[]{:S(2)}) collective-permute-start(bf16[1,1,32,64]{3,2,1,0:T(8,128)(2,1)S(1)} %get-tuple-element.1605), channel_id=1, source_target_pairs={{1,0},{2,1},{3,2},{4,3},{5,4},{6,5},{7,6},{8,7},{9,8},{10,9},{11,1... | collective-permute-start | bytes 12296 | tf_op jit(solution)/shard_map/while/body/eval_jaxpr/ppermute | solution.py:19
  71.6 19.8 %collective-permute-start.2 = (bf16[1,1,32,64]{3,2,1,0:T(8,128)(2,1)S(1)}, bf16[1,1,32,64]{3,2,1,0:T(8,128)(2,1)S(1)}, u32[]{:S(2)}, u32[]{:S(2)}) collective-permute-start(bf16[1,1,32,64]{3,2,1,0:T(8,128)(2,1)S(1)} %get-tuple-element.1607), channel_id=1, source_target_pairs={{0,1},{1,2},{2,3},{3,4},{4,5},{5,6},{6,7},{7,8},{8,9},{9,10},{10,1... | collective-permute-start | bytes 12296 | tf_op jit(solution)/shard_map/while/body/eval_jaxpr/ppermute | solution.py:17
  73.6 20.3 %collective-permute-start.3 = (bf16[1,1,32,64]{3,2,1,0:T(8,128)(2,1)S(1)}, bf16[1,1,32,64]{3,2,1,0:T(8,128)(2,1)S(1)}, u32[]{:S(2)}, u32[]{:S(2)}) collective-permute-start(bf16[1,1,32,64]{3,2,1,0:T(8,128)(2,1)S(1)} %get-tuple-element.1609), channel_id=1, source_target_pairs={{0,1},{1,2},{2,3},{3,4},{4,5},{5,6},{6,7},{7,8},{8,9},{9,10},{10,1... | collective-permute-start | bytes 12296 | tf_op jit(solution)/shard_map/while/body/eval_jaxpr/ppermute | solution.py:17
  75.5 18.3 %collective-permute-start.4 = (bf16[1,1,32,64]{3,2,1,0:T(8,128)(2,1)S(1)}, bf16[1,1,32,64]{3,2,1,0:T(8,128)(2,1)S(1)}, u32[]{:S(2)}, u32[]{:S(2)}) collective-permute-start(bf16[1,1,32,64]{3,2,1,0:T(8,128)(2,1)S(1)} %get-tuple-element.1611), channel_id=1, source_target_pairs={{0,1},{1,2},{2,3},{3,4},{4,5},{5,6},{6,7},{7,8},{8,9},{9,10},{10,1... | collective-permute-start | bytes 12296 | tf_op jit(solution)/shard_map/while/body/eval_jaxpr/ppermute | solution.py:17
  77.4 16.8 %collective-permute-start.10 = (bf16[1,1,32,64]{3,2,1,0:T(8,128)(2,1)S(1)}, bf16[1,1,32,64]{3,2,1,0:T(8,128)(2,1)S(1)}, u32[]{:S(2)}, u32[]{:S(2)}) collective-permute-start(bf16[1,1,32,64]{3,2,1,0:T(8,128)(2,1)S(1)} %get-tuple-element.1624), channel_id=1, source_target_pairs={{1,0},{2,1},{3,2},{4,3},{5,4},{6,5},{7,6},{8,7},{9,8},{10,9},{11,1... | collective-permute-start | bytes 12296 | tf_op jit(solution)/shard_map/while/body/eval_jaxpr/ppermute | solution.py:19
  84.4 12.8 %collective-permute-start.9 = (bf16[1,1,32,64]{3,2,1,0:T(8,128)(2,1)S(1)}, bf16[1,1,32,64]{3,2,1,0:T(8,128)(2,1)S(1)}, u32[]{:S(2)}, u32[]{:S(2)}) collective-permute-start(bf16[1,1,32,64]{3,2,1,0:T(8,128)(2,1)S(1)} %get-tuple-element.1622), channel_id=1, source_target_pairs={{1,0},{2,1},{3,2},{4,3},{5,4},{6,5},{7,6},{8,7},{9,8},{10,9},{11,1... | collective-permute-start | bytes 12296 | tf_op jit(solution)/shard_map/while/body/eval_jaxpr/ppermute | solution.py:19
  91.4 8.8 %collective-permute-start.5 = (bf16[1,1,32,64]{3,2,1,0:T(8,128)(2,1)S(1)}, bf16[1,1,32,64]{3,2,1,0:T(8,128)(2,1)S(1)}, u32[]{:S(2)}, u32[]{:S(2)}) collective-permute-start(bf16[1,1,32,64]{3,2,1,0:T(8,128)(2,1)S(1)} %get-tuple-element.1613), channel_id=1, source_target_pairs={{1,0},{2,1},{3,2},{4,3},{5,4},{6,5},{7,6},{8,7},{9,8},{10,9},{11,1... | collective-permute-start | bytes 12296 | tf_op jit(solution)/shard_map/while/body/eval_jaxpr/ppermute | solution.py:19
  105.0 13.6 %collective-permute-start.6 = (bf16[1,64,32,64]{3,2,1,0:T(8,128)(2,1)S(1)}, bf16[1,64,32,64]{3,2,1,0:T(8,128)(2,1)S(1)}, u32[]{:S(2)}, u32[]{:S(2)}) collective-permute-start(bf16[1,64,32,64]{3,2,1,0:T(8,128)(2,1)S(1)} %fusion.298), channel_id=1, source_target_pairs={{0,128},{128,256},{256,384},{1,129},{129,257},{257,385},{2,130},{1... | collective-permute-start | bytes 786440 | tf_op jit(solution)/shard_map/while/body/eval_jaxpr/ppermute | solution.py:29
  109.1 19.4 %copy-start.6 = (bf16[1,64,32,64]{3,2,1,0:T(8,128)(2,1)}, bf16[1,64,32,64]{3,2,1,0:T(8,128)(2,1)S(1)}, u32[]{:S(2)}) copy-start(bf16[1,64,32,64]{3,2,1,0:T(8,128)(2,1)S(1)} %fusion.301) | copy-start | bytes 786436 | tf_op jit(solution)/shard_map/while
  118.6 7.9 %copy-start.8 = (f32[9,64,64]{2,1,0:T(8,128)S(1)}, f32[9,64,64]{2,1,0:T(8,128)}, u32[]{:S(2)}) copy-start(f32[9,64,64]{2,1,0:T(8,128)} %copy-done.7) | copy-start | bytes 442372 | tf_op jit(solution)/shard_map/while
  118.6 7.9 %copy-start.10 = (f32[9,64,64]{2,1,0:T(8,128)S(1)}, f32[9,64,64]{2,1,0:T(8,128)}, u32[]{:S(2)}) copy-start(f32[9,64,64]{2,1,0:T(8,128)} %copy-done.9) | copy-start | bytes 442372 | tf_op jit(solution)/shard_map/while
  120.0 6.8 %collective-permute-start.7 = (f32[1,1,24,64]{3,1,2,0:T(1,128)S(1)}, f32[1,1,24,64]{3,1,2,0:T(1,128)S(1)}, u32[]{:S(2)}, u32[]{:S(2)}) collective-permute-start(f32[1,1,24,64]{3,1,2,0:T(1,128)S(1)} %slice.546), channel_id=1, source_target_pairs={{1,0},{2,1},{3,2},{4,3},{5,4},{6,5},{7,6},{8,7},{9,8},{10,9},{11,1... | collective-permute-start | bytes 18440 | tf_op jit(solution)/shard_map/while/body/eval_jaxpr/ppermute | solution.py:19
  124.6 3.5 collective-permute-start.8
  129.5 13.8 %collective-permute-start = (bf16[1,1,32,64]{3,2,1,0:T(8,128)(2,1)S(1)}, bf16[1,1,32,64]{3,2,1,0:T(8,128)(2,1)S(1)}, u32[]{:S(2)}, u32[]{:S(2)}) collective-permute-start(bf16[1,1,32,64]{3,2,1,0:T(8,128)(2,1)S(1)} %get-tuple-element.1604), channel_id=1, source_target_pairs={{0,1},{1,2},{2,3},{3,4},{4,5},{5,6},{6,7},{7,8},{8,9},{9,10},{10,1... | collective-permute-start | bytes 12296 | tf_op jit(solution)/shard_map/while/body/eval_jaxpr/ppermute | solution.py:17
  132.9 10.6 %collective-permute-start.1 = (bf16[1,1,32,64]{3,2,1,0:T(8,128)(2,1)S(1)}, bf16[1,1,32,64]{3,2,1,0:T(8,128)(2,1)S(1)}, u32[]{:S(2)}, u32[]{:S(2)}) collective-permute-start(bf16[1,1,32,64]{3,2,1,0:T(8,128)(2,1)S(1)} %get-tuple-element.1605), channel_id=1, source_target_pairs={{1,0},{2,1},{3,2},{4,3},{5,4},{6,5},{7,6},{8,7},{9,8},{10,9},{11,1... | collective-permute-start | bytes 12296 | tf_op jit(solution)/shard_map/while/body/eval_jaxpr/ppermute | solution.py:19
  149.9 19.8 %collective-permute-start.2 = (bf16[1,1,32,64]{3,2,1,0:T(8,128)(2,1)S(1)}, bf16[1,1,32,64]{3,2,1,0:T(8,128)(2,1)S(1)}, u32[]{:S(2)}, u32[]{:S(2)}) collective-permute-start(bf16[1,1,32,64]{3,2,1,0:T(8,128)(2,1)S(1)} %get-tuple-element.1607), channel_id=1, source_target_pairs={{0,1},{1,2},{2,3},{3,4},{4,5},{5,6},{6,7},{7,8},{8,9},{9,10},{10,1... | collective-permute-start | bytes 12296 | tf_op jit(solution)/shard_map/while/body/eval_jaxpr/ppermute | solution.py:17
  151.9 20.3 %collective-permute-start.3 = (bf16[1,1,32,64]{3,2,1,0:T(8,128)(2,1)S(1)}, bf16[1,1,32,64]{3,2,1,0:T(8,128)(2,1)S(1)}, u32[]{:S(2)}, u32[]{:S(2)}) collective-permute-start(bf16[1,1,32,64]{3,2,1,0:T(8,128)(2,1)S(1)} %get-tuple-element.1609), channel_id=1, source_target_pairs={{0,1},{1,2},{2,3},{3,4},{4,5},{5,6},{6,7},{7,8},{8,9},{9,10},{10,1... | collective-permute-start | bytes 12296 | tf_op jit(solution)/shard_map/while/body/eval_jaxpr/ppermute | solution.py:17
  153.8 18.3 %collective-permute-start.4 = (bf16[1,1,32,64]{3,2,1,0:T(8,128)(2,1)S(1)}, bf16[1,1,32,64]{3,2,1,0:T(8,128)(2,1)S(1)}, u32[]{:S(2)}, u32[]{:S(2)}) collective-permute-start(bf16[1,1,32,64]{3,2,1,0:T(8,128)(2,1)S(1)} %get-tuple-element.1611), channel_id=1, source_target_pairs={{0,1},{1,2},{2,3},{3,4},{4,5},{5,6},{6,7},{7,8},{8,9},{9,10},{10,1... | collective-permute-start | bytes 12296 | tf_op jit(solution)/shard_map/while/body/eval_jaxpr/ppermute | solution.py:17
  155.7 16.8 %collective-permute-start.10 = (bf16[1,1,32,64]{3,2,1,0:T(8,128)(2,1)S(1)}, bf16[1,1,32,64]{3,2,1,0:T(8,128)(2,1)S(1)}, u32[]{:S(2)}, u32[]{:S(2)}) collective-permute-start(bf16[1,1,32,64]{3,2,1,0:T(8,128)(2,1)S(1)} %get-tuple-element.1624), channel_id=1, source_target_pairs={{1,0},{2,1},{3,2},{4,3},{5,4},{6,5},{7,6},{8,7},{9,8},{10,9},{11,1... | collective-permute-start | bytes 12296 | tf_op jit(solution)/shard_map/while/body/eval_jaxpr/ppermute | solution.py:19
  162.7 12.8 %collective-permute-start.9 = (bf16[1,1,32,64]{3,2,1,0:T(8,128)(2,1)S(1)}, bf16[1,1,32,64]{3,2,1,0:T(8,128)(2,1)S(1)}, u32[]{:S(2)}, u32[]{:S(2)}) collective-permute-start(bf16[1,1,32,64]{3,2,1,0:T(8,128)(2,1)S(1)} %get-tuple-element.1622), channel_id=1, source_target_pairs={{1,0},{2,1},{3,2},{4,3},{5,4},{6,5},{7,6},{8,7},{9,8},{10,9},{11,1... | collective-permute-start | bytes 12296 | tf_op jit(solution)/shard_map/while/body/eval_jaxpr/ppermute | solution.py:19
  169.7 8.8 %collective-permute-start.5 = (bf16[1,1,32,64]{3,2,1,0:T(8,128)(2,1)S(1)}, bf16[1,1,32,64]{3,2,1,0:T(8,128)(2,1)S(1)}, u32[]{:S(2)}, u32[]{:S(2)}) collective-permute-start(bf16[1,1,32,64]{3,2,1,0:T(8,128)(2,1)S(1)} %get-tuple-element.1613), channel_id=1, source_target_pairs={{1,0},{2,1},{3,2},{4,3},{5,4},{6,5},{7,6},{8,7},{9,8},{10,9},{11,1... | collective-permute-start | bytes 12296 | tf_op jit(solution)/shard_map/while/body/eval_jaxpr/ppermute | solution.py:19
  183.3 13.6 %collective-permute-start.6 = (bf16[1,64,32,64]{3,2,1,0:T(8,128)(2,1)S(1)}, bf16[1,64,32,64]{3,2,1,0:T(8,128)(2,1)S(1)}, u32[]{:S(2)}, u32[]{:S(2)}) collective-permute-start(bf16[1,64,32,64]{3,2,1,0:T(8,128)(2,1)S(1)} %fusion.298), channel_id=1, source_target_pairs={{0,128},{128,256},{256,384},{1,129},{129,257},{257,385},{2,130},{1... | collective-permute-start | bytes 786440 | tf_op jit(solution)/shard_map/while/body/eval_jaxpr/ppermute | solution.py:29
  187.4 19.4 %copy-start.6 = (bf16[1,64,32,64]{3,2,1,0:T(8,128)(2,1)}, bf16[1,64,32,64]{3,2,1,0:T(8,128)(2,1)S(1)}, u32[]{:S(2)}) copy-start(bf16[1,64,32,64]{3,2,1,0:T(8,128)(2,1)S(1)} %fusion.301) | copy-start | bytes 786436 | tf_op jit(solution)/shard_map/while
  196.9 7.9 %copy-start.8 = (f32[9,64,64]{2,1,0:T(8,128)S(1)}, f32[9,64,64]{2,1,0:T(8,128)}, u32[]{:S(2)}) copy-start(f32[9,64,64]{2,1,0:T(8,128)} %copy-done.7) | copy-start | bytes 442372 | tf_op jit(solution)/shard_map/while
  196.9 7.9 %copy-start.10 = (f32[9,64,64]{2,1,0:T(8,128)S(1)}, f32[9,64,64]{2,1,0:T(8,128)}, u32[]{:S(2)}) copy-start(f32[9,64,64]{2,1,0:T(8,128)} %copy-done.9) | copy-start | bytes 442372 | tf_op jit(solution)/shard_map/while
  198.3 6.8 %collective-permute-start.7 = (f32[1,1,24,64]{3,1,2,0:T(1,128)S(1)}, f32[1,1,24,64]{3,1,2,0:T(1,128)S(1)}, u32[]{:S(2)}, u32[]{:S(2)}) collective-permute-start(f32[1,1,24,64]{3,1,2,0:T(1,128)S(1)} %slice.546), channel_id=1, source_target_pairs={{1,0},{2,1},{3,2},{4,3},{5,4},{6,5},{7,6},{8,7},{9,8},{10,9},{11,1... | collective-permute-start | bytes 18440 | tf_op jit(solution)/shard_map/while/body/eval_jaxpr/ppermute | solution.py:19
  202.9 3.5 collective-permute-start.8
  207.8 13.8 %collective-permute-start = (bf16[1,1,32,64]{3,2,1,0:T(8,128)(2,1)S(1)}, bf16[1,1,32,64]{3,2,1,0:T(8,128)(2,1)S(1)}, u32[]{:S(2)}, u32[]{:S(2)}) collective-permute-start(bf16[1,1,32,64]{3,2,1,0:T(8,128)(2,1)S(1)} %get-tuple-element.1604), channel_id=1, source_target_pairs={{0,1},{1,2},{2,3},{3,4},{4,5},{5,6},{6,7},{7,8},{8,9},{9,10},{10,1... | collective-permute-start | bytes 12296 | tf_op jit(solution)/shard_map/while/body/eval_jaxpr/ppermute | solution.py:17
  211.2 10.6 %collective-permute-start.1 = (bf16[1,1,32,64]{3,2,1,0:T(8,128)(2,1)S(1)}, bf16[1,1,32,64]{3,2,1,0:T(8,128)(2,1)S(1)}, u32[]{:S(2)}, u32[]{:S(2)}) collective-permute-start(bf16[1,1,32,64]{3,2,1,0:T(8,128)(2,1)S(1)} %get-tuple-element.1605), channel_id=1, source_target_pairs={{1,0},{2,1},{3,2},{4,3},{5,4},{6,5},{7,6},{8,7},{9,8},{10,9},{11,1... | collective-permute-start | bytes 12296 | tf_op jit(solution)/shard_map/while/body/eval_jaxpr/ppermute | solution.py:19
  228.2 19.8 %collective-permute-start.2 = (bf16[1,1,32,64]{3,2,1,0:T(8,128)(2,1)S(1)}, bf16[1,1,32,64]{3,2,1,0:T(8,128)(2,1)S(1)}, u32[]{:S(2)}, u32[]{:S(2)}) collective-permute-start(bf16[1,1,32,64]{3,2,1,0:T(8,128)(2,1)S(1)} %get-tuple-element.1607), channel_id=1, source_target_pairs={{0,1},{1,2},{2,3},{3,4},{4,5},{5,6},{6,7},{7,8},{8,9},{9,10},{10,1... | collective-permute-start | bytes 12296 | tf_op jit(solution)/shard_map/while/body/eval_jaxpr/ppermute | solution.py:17
  230.2 20.3 %collective-permute-start.3 = (bf16[1,1,32,64]{3,2,1,0:T(8,128)(2,1)S(1)}, bf16[1,1,32,64]{3,2,1,0:T(8,128)(2,1)S(1)}, u32[]{:S(2)}, u32[]{:S(2)}) collective-permute-start(bf16[1,1,32,64]{3,2,1,0:T(8,128)(2,1)S(1)} %get-tuple-element.1609), channel_id=1, source_target_pairs={{0,1},{1,2},{2,3},{3,4},{4,5},{5,6},{6,7},{7,8},{8,9},{9,10},{10,1... | collective-permute-start | bytes 12296 | tf_op jit(solution)/shard_map/while/body/eval_jaxpr/ppermute | solution.py:17
  232.1 18.3 %collective-permute-start.4 = (bf16[1,1,32,64]{3,2,1,0:T(8,128)(2,1)S(1)}, bf16[1,1,32,64]{3,2,1,0:T(8,128)(2,1)S(1)}, u32[]{:S(2)}, u32[]{:S(2)}) collective-permute-start(bf16[1,1,32,64]{3,2,1,0:T(8,128)(2,1)S(1)} %get-tuple-element.1611), channel_id=1, source_target_pairs={{0,1},{1,2},{2,3},{3,4},{4,5},{5,6},{6,7},{7,8},{8,9},{9,10},{10,1... | collective-permute-start | bytes 12296 | tf_op jit(solution)/shard_map/while/body/eval_jaxpr/ppermute | solution.py:17
  234.0 16.8 %collective-permute-start.10 = (bf16[1,1,32,64]{3,2,1,0:T(8,128)(2,1)S(1)}, bf16[1,1,32,64]{3,2,1,0:T(8,128)(2,1)S(1)}, u32[]{:S(2)}, u32[]{:S(2)}) collective-permute-start(bf16[1,1,32,64]{3,2,1,0:T(8,128)(2,1)S(1)} %get-tuple-element.1624), channel_id=1, source_target_pairs={{1,0},{2,1},{3,2},{4,3},{5,4},{6,5},{7,6},{8,7},{9,8},{10,9},{11,1... | collective-permute-start | bytes 12296 | tf_op jit(solution)/shard_map/while/body/eval_jaxpr/ppermute | solution.py:19
  241.0 12.8 %collective-permute-start.9 = (bf16[1,1,32,64]{3,2,1,0:T(8,128)(2,1)S(1)}, bf16[1,1,32,64]{3,2,1,0:T(8,128)(2,1)S(1)}, u32[]{:S(2)}, u32[]{:S(2)}) collective-permute-start(bf16[1,1,32,64]{3,2,1,0:T(8,128)(2,1)S(1)} %get-tuple-element.1622), channel_id=1, source_target_pairs={{1,0},{2,1},{3,2},{4,3},{5,4},{6,5},{7,6},{8,7},{9,8},{10,9},{11,1... | collective-permute-start | bytes 12296 | tf_op jit(solution)/shard_map/while/body/eval_jaxpr/ppermute | solution.py:19
  248.0 8.8 %collective-permute-start.5 = (bf16[1,1,32,64]{3,2,1,0:T(8,128)(2,1)S(1)}, bf16[1,1,32,64]{3,2,1,0:T(8,128)(2,1)S(1)}, u32[]{:S(2)}, u32[]{:S(2)}) collective-permute-start(bf16[1,1,32,64]{3,2,1,0:T(8,128)(2,1)S(1)} %get-tuple-element.1613), channel_id=1, source_target_pairs={{1,0},{2,1},{3,2},{4,3},{5,4},{6,5},{7,6},{8,7},{9,8},{10,9},{11,1... | collective-permute-start | bytes 12296 | tf_op jit(solution)/shard_map/while/body/eval_jaxpr/ppermute | solution.py:19
  261.6 13.6 %collective-permute-start.6 = (bf16[1,64,32,64]{3,2,1,0:T(8,128)(2,1)S(1)}, bf16[1,64,32,64]{3,2,1,0:T(8,128)(2,1)S(1)}, u32[]{:S(2)}, u32[]{:S(2)}) collective-permute-start(bf16[1,64,32,64]{3,2,1,0:T(8,128)(2,1)S(1)} %fusion.298), channel_id=1, source_target_pairs={{0,128},{128,256},{256,384},{1,129},{129,257},{257,385},{2,130},{1... | collective-permute-start | bytes 786440 | tf_op jit(solution)/shard_map/while/body/eval_jaxpr/ppermute | solution.py:29
  265.6 19.4 %copy-start.6 = (bf16[1,64,32,64]{3,2,1,0:T(8,128)(2,1)}, bf16[1,64,32,64]{3,2,1,0:T(8,128)(2,1)S(1)}, u32[]{:S(2)}) copy-start(bf16[1,64,32,64]{3,2,1,0:T(8,128)(2,1)S(1)} %fusion.301) | copy-start | bytes 786436 | tf_op jit(solution)/shard_map/while
  275.2 7.9 %copy-start.8 = (f32[9,64,64]{2,1,0:T(8,128)S(1)}, f32[9,64,64]{2,1,0:T(8,128)}, u32[]{:S(2)}) copy-start(f32[9,64,64]{2,1,0:T(8,128)} %copy-done.7) | copy-start | bytes 442372 | tf_op jit(solution)/shard_map/while
  275.2 7.9 %copy-start.10 = (f32[9,64,64]{2,1,0:T(8,128)S(1)}, f32[9,64,64]{2,1,0:T(8,128)}, u32[]{:S(2)}) copy-start(f32[9,64,64]{2,1,0:T(8,128)} %copy-done.9) | copy-start | bytes 442372 | tf_op jit(solution)/shard_map/while
  276.6 6.8 %collective-permute-start.7 = (f32[1,1,24,64]{3,1,2,0:T(1,128)S(1)}, f32[1,1,24,64]{3,1,2,0:T(1,128)S(1)}, u32[]{:S(2)}, u32[]{:S(2)}) collective-permute-start(f32[1,1,24,64]{3,1,2,0:T(1,128)S(1)} %slice.546), channel_id=1, source_target_pairs={{1,0},{2,1},{3,2},{4,3},{5,4},{6,5},{7,6},{8,7},{9,8},{10,9},{11,1... | collective-permute-start | bytes 18440 | tf_op jit(solution)/shard_map/while/body/eval_jaxpr/ppermute | solution.py:19
  281.2 3.5 collective-permute-start.8
  286.1 13.8 %collective-permute-start = (bf16[1,1,32,64]{3,2,1,0:T(8,128)(2,1)S(1)}, bf16[1,1,32,64]{3,2,1,0:T(8,128)(2,1)S(1)}, u32[]{:S(2)}, u32[]{:S(2)}) collective-permute-start(bf16[1,1,32,64]{3,2,1,0:T(8,128)(2,1)S(1)} %get-tuple-element.1604), channel_id=1, source_target_pairs={{0,1},{1,2},{2,3},{3,4},{4,5},{5,6},{6,7},{7,8},{8,9},{9,10},{10,1... | collective-permute-start | bytes 12296 | tf_op jit(solution)/shard_map/while/body/eval_jaxpr/ppermute | solution.py:17
  289.5 10.6 %collective-permute-start.1 = (bf16[1,1,32,64]{3,2,1,0:T(8,128)(2,1)S(1)}, bf16[1,1,32,64]{3,2,1,0:T(8,128)(2,1)S(1)}, u32[]{:S(2)}, u32[]{:S(2)}) collective-permute-start(bf16[1,1,32,64]{3,2,1,0:T(8,128)(2,1)S(1)} %get-tuple-element.1605), channel_id=1, source_target_pairs={{1,0},{2,1},{3,2},{4,3},{5,4},{6,5},{7,6},{8,7},{9,8},{10,9},{11,1... | collective-permute-start | bytes 12296 | tf_op jit(solution)/shard_map/while/body/eval_jaxpr/ppermute | solution.py:19
  306.5 19.8 %collective-permute-start.2 = (bf16[1,1,32,64]{3,2,1,0:T(8,128)(2,1)S(1)}, bf16[1,1,32,64]{3,2,1,0:T(8,128)(2,1)S(1)}, u32[]{:S(2)}, u32[]{:S(2)}) collective-permute-start(bf16[1,1,32,64]{3,2,1,0:T(8,128)(2,1)S(1)} %get-tuple-element.1607), channel_id=1, source_target_pairs={{0,1},{1,2},{2,3},{3,4},{4,5},{5,6},{6,7},{7,8},{8,9},{9,10},{10,1... | collective-permute-start | bytes 12296 | tf_op jit(solution)/shard_map/while/body/eval_jaxpr/ppermute | solution.py:17
  308.5 20.3 %collective-permute-start.3 = (bf16[1,1,32,64]{3,2,1,0:T(8,128)(2,1)S(1)}, bf16[1,1,32,64]{3,2,1,0:T(8,128)(2,1)S(1)}, u32[]{:S(2)}, u32[]{:S(2)}) collective-permute-start(bf16[1,1,32,64]{3,2,1,0:T(8,128)(2,1)S(1)} %get-tuple-element.1609), channel_id=1, source_target_pairs={{0,1},{1,2},{2,3},{3,4},{4,5},{5,6},{6,7},{7,8},{8,9},{9,10},{10,1... | collective-permute-start | bytes 12296 | tf_op jit(solution)/shard_map/while/body/eval_jaxpr/ppermute | solution.py:17
  310.4 18.3 %collective-permute-start.4 = (bf16[1,1,32,64]{3,2,1,0:T(8,128)(2,1)S(1)}, bf16[1,1,32,64]{3,2,1,0:T(8,128)(2,1)S(1)}, u32[]{:S(2)}, u32[]{:S(2)}) collective-permute-start(bf16[1,1,32,64]{3,2,1,0:T(8,128)(2,1)S(1)} %get-tuple-element.1611), channel_id=1, source_target_pairs={{0,1},{1,2},{2,3},{3,4},{4,5},{5,6},{6,7},{7,8},{8,9},{9,10},{10,1... | collective-permute-start | bytes 12296 | tf_op jit(solution)/shard_map/while/body/eval_jaxpr/ppermute | solution.py:17
  312.3 16.8 %collective-permute-start.10 = (bf16[1,1,32,64]{3,2,1,0:T(8,128)(2,1)S(1)}, bf16[1,1,32,64]{3,2,1,0:T(8,128)(2,1)S(1)}, u32[]{:S(2)}, u32[]{:S(2)}) collective-permute-start(bf16[1,1,32,64]{3,2,1,0:T(8,128)(2,1)S(1)} %get-tuple-element.1624), channel_id=1, source_target_pairs={{1,0},{2,1},{3,2},{4,3},{5,4},{6,5},{7,6},{8,7},{9,8},{10,9},{11,1... | collective-permute-start | bytes 12296 | tf_op jit(solution)/shard_map/while/body/eval_jaxpr/ppermute | solution.py:19
  319.3 12.8 %collective-permute-start.9 = (bf16[1,1,32,64]{3,2,1,0:T(8,128)(2,1)S(1)}, bf16[1,1,32,64]{3,2,1,0:T(8,128)(2,1)S(1)}, u32[]{:S(2)}, u32[]{:S(2)}) collective-permute-start(bf16[1,1,32,64]{3,2,1,0:T(8,128)(2,1)S(1)} %get-tuple-element.1622), channel_id=1, source_target_pairs={{1,0},{2,1},{3,2},{4,3},{5,4},{6,5},{7,6},{8,7},{9,8},{10,9},{11,1... | collective-permute-start | bytes 12296 | tf_op jit(solution)/shard_map/while/body/eval_jaxpr/ppermute | solution.py:19
  326.3 8.8 %collective-permute-start.5 = (bf16[1,1,32,64]{3,2,1,0:T(8,128)(2,1)S(1)}, bf16[1,1,32,64]{3,2,1,0:T(8,128)(2,1)S(1)}, u32[]{:S(2)}, u32[]{:S(2)}) collective-permute-start(bf16[1,1,32,64]{3,2,1,0:T(8,128)(2,1)S(1)} %get-tuple-element.1613), channel_id=1, source_target_pairs={{1,0},{2,1},{3,2},{4,3},{5,4},{6,5},{7,6},{8,7},{9,8},{10,9},{11,1... | collective-permute-start | bytes 12296 | tf_op jit(solution)/shard_map/while/body/eval_jaxpr/ppermute | solution.py:19
  339.9 13.6 %collective-permute-start.6 = (bf16[1,64,32,64]{3,2,1,0:T(8,128)(2,1)S(1)}, bf16[1,64,32,64]{3,2,1,0:T(8,128)(2,1)S(1)}, u32[]{:S(2)}, u32[]{:S(2)}) collective-permute-start(bf16[1,64,32,64]{3,2,1,0:T(8,128)(2,1)S(1)} %fusion.298), channel_id=1, source_target_pairs={{0,128},{128,256},{256,384},{1,129},{129,257},{257,385},{2,130},{1... | collective-permute-start | bytes 786440 | tf_op jit(solution)/shard_map/while/body/eval_jaxpr/ppermute | solution.py:29
  343.9 19.5 %copy-start.6 = (bf16[1,64,32,64]{3,2,1,0:T(8,128)(2,1)}, bf16[1,64,32,64]{3,2,1,0:T(8,128)(2,1)S(1)}, u32[]{:S(2)}) copy-start(bf16[1,64,32,64]{3,2,1,0:T(8,128)(2,1)S(1)} %fusion.301) | copy-start | bytes 786436 | tf_op jit(solution)/shard_map/while
  353.5 7.9 %copy-start.8 = (f32[9,64,64]{2,1,0:T(8,128)S(1)}, f32[9,64,64]{2,1,0:T(8,128)}, u32[]{:S(2)}) copy-start(f32[9,64,64]{2,1,0:T(8,128)} %copy-done.7) | copy-start | bytes 442372 | tf_op jit(solution)/shard_map/while
  353.5 7.9 %copy-start.10 = (f32[9,64,64]{2,1,0:T(8,128)S(1)}, f32[9,64,64]{2,1,0:T(8,128)}, u32[]{:S(2)}) copy-start(f32[9,64,64]{2,1,0:T(8,128)} %copy-done.9) | copy-start | bytes 442372 | tf_op jit(solution)/shard_map/while
  354.9 6.8 %collective-permute-start.7 = (f32[1,1,24,64]{3,1,2,0:T(1,128)S(1)}, f32[1,1,24,64]{3,1,2,0:T(1,128)S(1)}, u32[]{:S(2)}, u32[]{:S(2)}) collective-permute-start(f32[1,1,24,64]{3,1,2,0:T(1,128)S(1)} %slice.546), channel_id=1, source_target_pairs={{1,0},{2,1},{3,2},{4,3},{5,4},{6,5},{7,6},{8,7},{9,8},{10,9},{11,1... | collective-permute-start | bytes 18440 | tf_op jit(solution)/shard_map/while/body/eval_jaxpr/ppermute | solution.py:19
  359.5 3.5 collective-permute-start.8
  (37 other events, 81.4 us)
Sparse Core Ops, SparseCore 0:
  363.6 190.1 all-reduce.4
where the time goes:
time: 629 us; the launch traced here: 627 us
  blocking collectives  252 us (40%)
  starting transfers between devices  178 us (28%)
  waiting for transfers between devices  43.6 us (7%)
  matrix products  43.2 us (7%)
  other arithmetic  42.8 us (7%)
  local copies, waits for them, and re-layouts  41.2 us (7%)
  between operations  23.6 us (4%)
    psum x1, blocking collectives, local(): kernel_sum, bias_sum = lax.psum((final_state[2], final_state[3]), 'strip')  252 us
    ppermute x22, starting transfers between devices, extended_2(): lax.ppermute(head, axis, [((i + 1) % count, i) for i in range(ends)])  115 us
    ppermute x22, starting transfers between devices, extended_2(): lax.ppermute(tail, axis, [(i, (i + 1) % count) for i in range(ends)])  50.2 us
    ppermute x4, waiting for transfers between devices, shifted_2(): return lax.ppermute(x, axis, pairs)  38.1 us
    dot_general x72, matrix products, weight_taps(): lax.dot_general(window, error, (((0, 1, 2), (0, 1, 2)), ((), ())), prefer...  22.9 us
    conv_general_dilated x10, matrix products, conv_rows(): lax.conv_general_dilated(field_in, kernel, (1, 1), ((0, 0), (1, 1)), dime...  15 us
    while x104, local copies, waits for them, and re-layouts  14.7 us
  transfers between devices with their start and end apart: 49, of which 8 were waited for; matrix products, arithmetic and copies ran while one was open for 9% of the time, Pallas kernels for 0%

commit v1 on v0

--- a/solution.py
+++ b/solution.py
@@ -1,6 +1,8 @@
 import jax
 import jax.numpy as jnp
 from jax import lax
+from jax.experimental import pallas as pl
+from jax.experimental.pallas import tpu as pltpu
 from jax.sharding import PartitionSpec as P
 
 LEAK = 0.05
@@ -84,6 +86,151 @@
     filler = jnp.zeros_like(upper_rows)
     joined = jnp.concatenate([upper_rows, field_in, filler], axis=1)
     return lax.dynamic_update_slice_in_dim(joined, lower_rows, live_rows + rim_depth, 1)
+
+
+RING = 8
+PIECE = 40
+HALF = RING * PIECE
+PACKED = 2 * HALF
+MESH = pl.DeviceIdType.MESH
+
+
+def reduce_body(
+    src, out, pair_in, y_sum, y_in, z_out, z_in, gathered,
+    pair_send, pair_recv, y_send, y_recv, z_send, z_recv, g_send, g_recv, p_send, p_recv,
+):
+    strip = lax.axis_index("strip")
+    core = lax.rem(strip, 2)
+    row = lax.rem(lax.div(strip, 2), RING)
+    deep = lax.div(strip, 2 * RING)
+    partner = strip + 1 - 2 * core
+
+    def y_peer(step):
+        return (deep * RING + lax.rem(row + step, RING)) * 2 + core
+
+    def z_peer(step):
+        return (lax.rem(deep + step, RING) * RING + row) * 2 + core
+
+    def remote(src_ref, dst_ref, send, recv, strip_id):
+        return pltpu.make_async_remote_copy(
+            src_ref=src_ref,
+            dst_ref=dst_ref,
+            send_sem=send,
+            recv_sem=recv,
+            device_id=(lax.axis_index("section"), strip_id),
+            device_id_type=MESH,
+        )
+
+    barrier = pltpu.get_barrier_semaphore()
+    peers = [partner]
+    peers += [y_peer(step) for step in range(1, RING)]
+    peers += [z_peer(step) for step in range(1, RING)]
+    for peer in peers:
+        pl.semaphore_signal(
+            barrier,
+            inc=1,
+            device_id=(lax.axis_index("section"), peer),
+            device_id_type=MESH,
+        )
+    pl.semaphore_wait(barrier, len(peers))
+
+    mine = pl.multiple_of(core * HALF, 8)
+    other = pl.multiple_of((1 - core) * HALF, 8)
+    swap = remote(src.at[pl.ds(other, HALF)], pair_in, pair_send, pair_recv, partner)
+    swap.start()
+    swap.wait()
+    y_sum[...] = src[pl.ds(mine, HALF), :] + pair_in[...]
+
+    def piece(ref, index):
+        return ref.at[pl.ds(pl.multiple_of(index * PIECE, 8), PIECE)]
+
+    scatter = []
+    for step in range(1, RING):
+        copy = remote(
+            piece(y_sum, lax.rem(row + step, RING)),
+            y_in.at[step - 1],
+            y_send.at[step - 1],
+            y_recv.at[step - 1],
+            y_peer(step),
+        )
+        copy.start()
+        scatter.append(copy)
+    total = y_sum[pl.ds(pl.multiple_of(row * PIECE, 8), PIECE), :]
+    for step in range(1, RING):
+        scatter[step - 1].wait_recv()
+        total = total + y_in[step - 1]
+    z_out[...] = total
+    z_in[deep] = total
+    trade = []
+    for step in range(1, RING):
+        copy = remote(
+            z_out, z_in.at[deep], z_send.at[step - 1], z_recv.at[step - 1], z_peer(step)
+        )
+        copy.start()
+        trade.append(copy)
+    for copy in trade:
+        copy.wait_recv()
+    total = z_in[0]
+    for index in range(1, RING):
+        total = total + z_in[index]
+    own = core * RING + row
+    gathered[pl.ds(pl.multiple_of(own * PIECE, 8), PIECE), :] = total
+    gather = []
+    for step in range(1, RING):
+        copy = remote(
+            piece(gathered, own),
+            piece(gathered, own),
+            g_send.at[step - 1],
+            g_recv.at[step - 1],
+            y_peer(step),
+        )
+        copy.start()
+        gather.append(copy)
+    passed = []
+    copy = remote(piece(gathered, own), piece(gathered, own), p_send.at[0], p_recv.at[0], partner)
+    copy.start()
+    passed.append(copy)
+    for step in range(1, RING):
+        gather[step - 1].wait_recv()
+        came = core * RING + lax.rem(row + RING - step, RING)
+        copy = remote(
+            piece(gathered, came),
+            piece(gathered, came),
+            p_send.at[step],
+            p_recv.at[step],
+            partner,
+        )
+        copy.start()
+        passed.append(copy)
+    for copy in passed:
+        copy.wait_recv()
+    out[...] = gathered[...]
+    for copy in scatter + trade + gather + passed:
+        copy.wait_send()
+
+
+def strip_sum(packed):
+    dma = pltpu.SemaphoreType.DMA
+    return pl.pallas_call(
+        reduce_body,
+        out_shape=jax.ShapeDtypeStruct((PACKED, 128), jnp.float32),
+        in_specs=[pl.BlockSpec(memory_space=pltpu.VMEM)],
+        out_specs=pl.BlockSpec(memory_space=pltpu.VMEM),
+        scratch_shapes=[
+            pltpu.VMEM((HALF, 128), jnp.float32),
+            pltpu.VMEM((HALF, 128), jnp.float32),
+            pltpu.VMEM((RING - 1, PIECE, 128), jnp.float32),
+            pltpu.VMEM((PIECE, 128), jnp.float32),
+            pltpu.VMEM((RING, PIECE, 128), jnp.float32),
+            pltpu.VMEM((PACKED, 128), jnp.float32),
+            dma, dma,
+            dma((RING - 1,)), dma((RING - 1,)),
+            dma((RING - 1,)), dma((RING - 1,)),
+            dma((RING - 1,)), dma((RING - 1,)),
+            dma((RING,)), dma((RING,)),
+        ],
+        compiler_params=pltpu.CompilerParams(collective_id=1, has_side_effects=True),
+    )(packed)
 
 
 def local(cotangent, activations, weights, biases):
@@ -248,7 +395,12 @@
     )
     final_state = lax.fori_loop(0, tick_count, one_tick, initial)
     noise_acc = final_state[1]
-    kernel_sum, bias_sum = lax.psum((final_state[2], final_state[3]), "strip")
+    flat = jnp.concatenate([final_state[2].reshape(-1), final_state[3].reshape(-1)])
+    taps = flat.shape[0]
+    flat = jnp.pad(flat, (0, PACKED * 128 - taps)).reshape(PACKED, 128)
+    flat = strip_sum(flat).reshape(-1)
+    kernel_sum = flat[: taps - 2 * channels].reshape(final_state[2].shape)
+    bias_sum = flat[taps - 2 * channels : taps].reshape(2, channels)
     pixel_count = (samples * strip_count * live_rows * live_cols).astype(jnp.float32)
     scale_back = 1.0 / jnp.sqrt(pixel_count)
     return (

time: 629 us -> 414 us (0.66)
  the two profiles are of different devices: /device:TPU:259 before, /device:TPU:7 now
where the time goes in v1:
time: 414 us; the launch traced here: 411 us
  starting transfers between devices  141 us (34%)
  Pallas kernels  68.5 us (17%)
  local copies, waits for them, and re-layouts  49.7 us (12%)
  matrix products  48.6 us (12%)
  waiting for transfers between devices  48.2 us (12%)
  other arithmetic  42.6 us (10%)
  between operations  10 us (2%)
    ppermute x22, starting transfers between devices, extended_2(): lax.ppermute(tail, axis, [(i, (i + 1) % count) for i in range(ends)])  93.1 us
    pallas_call x1, Pallas kernels, strip_sum(): pl.pallas_call(reduce_body, out_shape=jax.ShapeDtypeStruct((PACKED, 128),...  68.5 us
    ppermute x22, starting transfers between devices, extended_2(): lax.ppermute(head, axis, [((i + 1) % count, i) for i in range(ends)])  42.9 us
    ppermute x4, waiting for transfers between devices, shifted_2(): return lax.ppermute(x, axis, pairs)  42.4 us
    dot_general x72, matrix products, weight_taps(): lax.dot_general(window, error, (((0, 1, 2), (0, 1, 2)), ((), ())), prefer...  22.9 us
    conv_general_dilated x10, matrix products, conv_rows(): lax.conv_general_dilated(field_in, kernel, (1, 1), ((0, 0), (1, 1)), dime...  20.3 us
    while x104, local copies, waits for them, and re-layouts  16.4 us
    dynamic_update_slice x28, local copies, waits for them, and re-layouts, attach(): lax.dynamic_update_slice_in_dim(joined, lower_rows, live_rows + rim_depth...  12.6 us
  transfers between devices with their start and end apart: 48, of which 11 were waited for; matrix products, arithmetic and copies ran while one was open for 12% of the time, Pallas kernels for 0%

profile of v1, /device:TPU:7, one launch (start us, length us, event | category | flops | bytes accessed | tf_op | source)
XLA Modules:
  0.0 411.3 jit_solution(17911914802000865595)
XLA Ops:
  6.6 3.8 collective-permute-start.11
  10.3 1.9 collective-permute-start.12
  15.6 3.8 dynamic_update_slice.57
  20.6 3.5 fusion.168
  25.9 3.3 collective-permute-start.13
  38.5 2.1 collective-permute-start.14
  41.3 2.2 collective-permute-done.14
  43.8 3.8 dynamic_update_slice.58
  47.7 2.3 copy.158
  50.0 4.7 %fusion.169 = f32[1,64,32,64]{3,0,2,1:T(1,128)S(1)} fusion(bf16[1,66,32,64]{3,0,2,1:T(2,128)(2,1)} %copy.158, bf16[3,3,64,64]{3,2,1,0:T(8,128)(2,1)S(1)} %get-tuple-element.1370), kind=kOutput, calls=%fused_computation.256 | convolution fusion | flops 147849216 | bytes 868352 | tf_op jit(solution)/shard_map/while/body/eval_jaxpr/conv_general_dilated | solution.py:43
  54.8 281.5 %while.25 = (s32[]{:T(128)}, bf16[1,64,32,64]{3,1,2,0:T(8,128)(2,1)S(1)}, bf16[1,64,32,64]{3,2,1,0:T(8,128)(2,1)}, f32[2,3,3,64,64]{4,3,2,1,0:T(8,128)}, f32[2,6...) while((s32[]{:T(128)}, ...), condition=%wide.region_3.4_spmd.clone.clone, body=%wide.region_0.3_spmd.clone.clone.sunk | while | flops 787387328 | bytes 55671280 | solution.py:396
  55.8 1.9 collective-permute-start
  57.8 2.4 collective-permute-start.1
  65.8 2.0 convolution_select_fusion.4
  69.3 1.5 convert_reduce_fusion.5
  70.8 3.2 collective-permute-start.2
  74.1 2.3 collective-permute-start.3
  76.4 4.0 collective-permute-start.4
  80.5 1.9 collective-permute-start.10
  82.4 1.9 collective-permute-start.9
  84.3 1.9 collective-permute-start.5
  99.7 10.6 %collective-permute-done.6 = bf16[1,64,32,64]{3,2,1,0:T(8,128)(2,1)S(1)} collective-permute-done((bf16[1,64,32,64]{3,2,1,0:T(8,128)(2,1)S(1)}, bf16[1,64,32,64]{3,2,1,0:T(8,128)(2,1)S(1)}, u32[]{:S(2)}, u32[]{:S(2)}) %collective-permute-start.6) | collective-permute-done | bytes 262176 | tf_op jit(solution)/shard_map/while/body/eval_jaxpr/ppermute | solution.py:31
  111.6 1.9 collective-permute-start.7
  113.6 5.8 %collective-permute-start.8 = (f32[1,1,24,64]{3,2,1,0:T(8,128)S(1)}, f32[1,1,24,64]{3,2,1,0:T(8,128)S(1)}, u32[]{:S(2)}, u32[]{:S(2)}) collective-permute-start(f32[1,1,24,64]{3,2,1,0:T(8,128)S(1)} %bitcast.472), channel_id=1, source_target_pairs={{0,1},{1,2},{2,3},{3,4},{4,5},{5,6},{6,7},{7,8},{8,9},{9,10},{10,1... | collective-permute-start | bytes 18440 | tf_op jit(solution)/shard_map/while/body/eval_jaxpr/ppermute | solution.py:19
  122.0 3.8 collective-permute-start
  125.8 1.9 collective-permute-start.1
  134.4 2.0 convolution_select_fusion.4
  137.9 1.5 convert_reduce_fusion.5
  139.4 4.9 %collective-permute-start.2 = (bf16[1,1,32,64]{3,2,1,0:T(8,128)(2,1)S(1)}, bf16[1,1,32,64]{3,2,1,0:T(8,128)(2,1)S(1)}, u32[]{:S(2)}, u32[]{:S(2)}) collective-permute-start(bf16[1,1,32,64]{3,2,1,0:T(8,128)(2,1)S(1)} %get-tuple-element.1607), channel_id=1, source_target_pairs={{0,1},{1,2},{2,3},{3,4},{4,5},{5,6},{6,7},{7,8},{8,9},{9,10},{10,1... | collective-permute-start | bytes 12296 | tf_op jit(solution)/shard_map/while/body/eval_jaxpr/ppermute | solution.py:19
  144.3 3.8 collective-permute-start.3
  148.1 3.6 collective-permute-start.4
  151.8 1.9 collective-permute-start.10
  153.7 1.9 collective-permute-start.9
  155.7 1.9 collective-permute-start.5
  171.0 10.7 %collective-permute-done.6 = bf16[1,64,32,64]{3,2,1,0:T(8,128)(2,1)S(1)} collective-permute-done((bf16[1,64,32,64]{3,2,1,0:T(8,128)(2,1)S(1)}, bf16[1,64,32,64]{3,2,1,0:T(8,128)(2,1)S(1)}, u32[]{:S(2)}, u32[]{:S(2)}) %collective-permute-start.6) | collective-permute-done | bytes 262176 | tf_op jit(solution)/shard_map/while/body/eval_jaxpr/ppermute | solution.py:31
  183.0 1.9 collective-permute-start.7
  184.9 7.4 %collective-permute-start.8 = (f32[1,1,24,64]{3,2,1,0:T(8,128)S(1)}, f32[1,1,24,64]{3,2,1,0:T(8,128)S(1)}, u32[]{:S(2)}, u32[]{:S(2)}) collective-permute-start(f32[1,1,24,64]{3,2,1,0:T(8,128)S(1)} %bitcast.472), channel_id=1, source_target_pairs={{0,1},{1,2},{2,3},{3,4},{4,5},{5,6},{6,7},{7,8},{8,9},{9,10},{10,1... | collective-permute-start | bytes 18440 | tf_op jit(solution)/shard_map/while/body/eval_jaxpr/ppermute | solution.py:19
  195.0 3.8 collective-permute-start
  198.8 1.9 collective-permute-start.1
  206.4 2.0 convolution_select_fusion.4
  209.8 1.5 convert_reduce_fusion.5
  211.4 3.6 collective-permute-start.2
  215.0 2.8 collective-permute-start.3
  217.9 4.9 %collective-permute-start.4 = (bf16[1,1,32,64]{3,2,1,0:T(8,128)(2,1)S(1)}, bf16[1,1,32,64]{3,2,1,0:T(8,128)(2,1)S(1)}, u32[]{:S(2)}, u32[]{:S(2)}) collective-permute-start(bf16[1,1,32,64]{3,2,1,0:T(8,128)(2,1)S(1)} %get-tuple-element.1611), channel_id=1, source_target_pairs={{0,1},{1,2},{2,3},{3,4},{4,5},{5,6},{6,7},{7,8},{8,9},{9,10},{10,1... | collective-permute-start | bytes 12296 | tf_op jit(solution)/shard_map/while/body/eval_jaxpr/ppermute | solution.py:19
  222.8 1.9 collective-permute-start.10
  224.7 1.9 collective-permute-start.9
  226.6 1.9 collective-permute-start.5
  242.0 10.6 %collective-permute-done.6 = bf16[1,64,32,64]{3,2,1,0:T(8,128)(2,1)S(1)} collective-permute-done((bf16[1,64,32,64]{3,2,1,0:T(8,128)(2,1)S(1)}, bf16[1,64,32,64]{3,2,1,0:T(8,128)(2,1)S(1)}, u32[]{:S(2)}, u32[]{:S(2)}) %collective-permute-start.6) | collective-permute-done | bytes 262176 | tf_op jit(solution)/shard_map/while/body/eval_jaxpr/ppermute | solution.py:31
  253.9 1.9 collective-permute-start.7
  255.9 6.9 %collective-permute-start.8 = (f32[1,1,24,64]{3,2,1,0:T(8,128)S(1)}, f32[1,1,24,64]{3,2,1,0:T(8,128)S(1)}, u32[]{:S(2)}, u32[]{:S(2)}) collective-permute-start(f32[1,1,24,64]{3,2,1,0:T(8,128)S(1)} %bitcast.472), channel_id=1, source_target_pairs={{0,1},{1,2},{2,3},{3,4},{4,5},{5,6},{6,7},{7,8},{8,9},{9,10},{10,1... | collective-permute-start | bytes 18440 | tf_op jit(solution)/shard_map/while/body/eval_jaxpr/ppermute | solution.py:19
  265.5 3.8 collective-permute-start
  269.2 1.9 collective-permute-start.1
  276.8 2.0 convolution_select_fusion.4
  280.3 1.5 convert_reduce_fusion.5
  281.8 3.6 collective-permute-start.2
  285.5 4.1 %collective-permute-start.3 = (bf16[1,1,32,64]{3,2,1,0:T(8,128)(2,1)S(1)}, bf16[1,1,32,64]{3,2,1,0:T(8,128)(2,1)S(1)}, u32[]{:S(2)}, u32[]{:S(2)}) collective-permute-start(bf16[1,1,32,64]{3,2,1,0:T(8,128)(2,1)S(1)} %get-tuple-element.1609), channel_id=1, source_target_pairs={{0,1},{1,2},{2,3},{3,4},{4,5},{5,6},{6,7},{7,8},{8,9},{9,10},{10,1... | collective-permute-start | bytes 12296 | tf_op jit(solution)/shard_map/while/body/eval_jaxpr/ppermute | solution.py:19
  289.7 4.9 %collective-permute-start.4 = (bf16[1,1,32,64]{3,2,1,0:T(8,128)(2,1)S(1)}, bf16[1,1,32,64]{3,2,1,0:T(8,128)(2,1)S(1)}, u32[]{:S(2)}, u32[]{:S(2)}) collective-permute-start(bf16[1,1,32,64]{3,2,1,0:T(8,128)(2,1)S(1)} %get-tuple-element.1611), channel_id=1, source_target_pairs={{0,1},{1,2},{2,3},{3,4},{4,5},{5,6},{6,7},{7,8},{8,9},{9,10},{10,1... | collective-permute-start | bytes 12296 | tf_op jit(solution)/shard_map/while/body/eval_jaxpr/ppermute | solution.py:19
  294.6 1.9 collective-permute-start.10
  296.5 1.9 collective-permute-start.9
  298.5 1.9 collective-permute-start.5
  313.8 10.6 %collective-permute-done.6 = bf16[1,64,32,64]{3,2,1,0:T(8,128)(2,1)S(1)} collective-permute-done((bf16[1,64,32,64]{3,2,1,0:T(8,128)(2,1)S(1)}, bf16[1,64,32,64]{3,2,1,0:T(8,128)(2,1)S(1)}, u32[]{:S(2)}, u32[]{:S(2)}) %collective-permute-start.6) | collective-permute-done | bytes 262176 | tf_op jit(solution)/shard_map/while/body/eval_jaxpr/ppermute | solution.py:31
  325.7 1.9 collective-permute-start.7
  327.7 6.9 %collective-permute-start.8 = (f32[1,1,24,64]{3,2,1,0:T(8,128)S(1)}, f32[1,1,24,64]{3,2,1,0:T(8,128)S(1)}, u32[]{:S(2)}, u32[]{:S(2)}) collective-permute-start(f32[1,1,24,64]{3,2,1,0:T(8,128)S(1)} %bitcast.472), channel_id=1, source_target_pairs={{0,1},{1,2},{2,3},{3,4},{4,5},{5,6},{6,7},{7,8},{8,9},{9,10},{10,1... | collective-permute-start | bytes 18440 | tf_op jit(solution)/shard_map/while/body/eval_jaxpr/ppermute | solution.py:19
  338.3 68.5 %shard_map.85 = f32[640,128]{1,0:T(8,128)} custom-call(f32[640,128]{1,0:T(8,128)} %fusion.156.src), custom_call_target="tpu_custom_call" | custom-call | tf_op jit(solution)/shard_map/pallas_call | solution.py:214
  (452 shorter events, 117.5 us)
Async XLA Ops:
  0.6 11.6 %copy-start.13 = (bf16[1,2,3,3,64,64]{5,4,3,2,1,0:T(8,128)(2,1)S(1)}, bf16[1,2,3,3,64,64]{5,4,3,2,1,0:T(8,128)(2,1)}, u32[]{:S(2)}) copy-start(bf16[1,2,3,3,64,64]{5,4,3,2,1,0:T(8,128)(2,1)} %param.10) | copy-start | bytes 442372
  0.6 11.7 %copy-start.16 = (f32[1,2,64]{2,1,0:T(2,128)S(1)}, f32[1,2,64]{2,1,0:T(2,128)}, u32[]{:S(2)}) copy-start(f32[1,2,64]{2,1,0:T(2,128)} %param.11) | copy-start | bytes 1540
  6.6 7.8 %collective-permute-start.11 = (bf16[1,1,32,64]{3,2,1,0:T(8,128)(2,1)S(1)}, bf16[1,1,32,64]{3,2,1,0:T(8,128)(2,1)S(1)}, u32[]{:S(2)}, u32[]{:S(2)}) collective-permute-start(bf16[1,1,32,64]{3,2,1,0:T(8,128)(2,1)S(1)} %get-tuple-element.1369), channel_id=1, source_target_pairs={{0,1},{1,2},{2,3},{3,4},{4,5},{5,6},{6,7},{7,8},{8,9},{9,10},{10,1... | collective-permute-start | bytes 12296 | tf_op jit(solution)/shard_map/while/body/eval_jaxpr/ppermute | solution.py:19
  10.3 5.0 %collective-permute-start.12 = (bf16[1,1,32,64]{3,2,1,0:T(8,128)(2,1)S(1)}, bf16[1,1,32,64]{3,2,1,0:T(8,128)(2,1)S(1)}, u32[]{:S(2)}, u32[]{:S(2)}) collective-permute-start(bf16[1,1,32,64]{3,2,1,0:T(8,128)(2,1)S(1)} %get-tuple-element.1368), channel_id=1, source_target_pairs={{1,0},{2,1},{3,2},{4,3},{5,4},{6,5},{7,6},{8,7},{9,8},{10,9},{11,1... | collective-permute-start | bytes 12296 | tf_op jit(solution)/shard_map/while/body/eval_jaxpr/ppermute | solution.py:21
  25.1 11.0 %copy-start.14 = (bf16[1,64,2048]{2,1,0:T(8,128)(2,1)S(1)}, bf16[1,64,2048]{2,1,0:T(8,128)(2,1)}, u32[]{:S(2)}) copy-start(bf16[1,64,2048]{2,1,0:T(8,128)(2,1)} %param.8) | copy-start | bytes 786436
  25.9 14.7 %collective-permute-start.13 = (bf16[1,1,32,64]{3,2,1,0:T(8,128)(2,1)S(1)}, bf16[1,1,32,64]{3,2,1,0:T(8,128)(2,1)S(1)}, u32[]{:S(2)}, u32[]{:S(2)}) collective-permute-start(bf16[1,1,32,64]{3,2,1,0:T(8,128)(2,1)S(1)} %get-tuple-element.1367), channel_id=1, source_target_pairs={{0,1},{1,2},{2,3},{3,4},{4,5},{5,6},{6,7},{7,8},{8,9},{9,10},{10,1... | collective-permute-start | bytes 12296 | tf_op jit(solution)/shard_map/while/body/eval_jaxpr/ppermute | solution.py:19
  38.5 5.0 %collective-permute-start.14 = (bf16[1,1,32,64]{3,2,1,0:T(8,128)(2,1)S(1)}, bf16[1,1,32,64]{3,2,1,0:T(8,128)(2,1)S(1)}, u32[]{:S(2)}, u32[]{:S(2)}) collective-permute-start(bf16[1,1,32,64]{3,2,1,0:T(8,128)(2,1)S(1)} %get-tuple-element.1366), channel_id=1, source_target_pairs={{1,0},{2,1},{3,2},{4,3},{5,4},{6,5},{7,6},{8,7},{9,8},{10,9},{11,1... | collective-permute-start | bytes 12296 | tf_op jit(solution)/shard_map/while/body/eval_jaxpr/ppermute | solution.py:21
  55.8 8.4 %collective-permute-start = (bf16[1,1,32,64]{3,2,1,0:T(8,128)(2,1)S(1)}, bf16[1,1,32,64]{3,2,1,0:T(8,128)(2,1)S(1)}, u32[]{:S(2)}, u32[]{:S(2)}) collective-permute-start(bf16[1,1,32,64]{3,2,1,0:T(8,128)(2,1)S(1)} %get-tuple-element.1604), channel_id=1, source_target_pairs={{0,1},{1,2},{2,3},{3,4},{4,5},{5,6},{6,7},{7,8},{8,9},{9,10},{10,1... | collective-permute-start | bytes 12296 | tf_op jit(solution)/shard_map/while/body/eval_jaxpr/ppermute | solution.py:19
  57.8 6.6 %collective-permute-start.1 = (bf16[1,1,32,64]{3,2,1,0:T(8,128)(2,1)S(1)}, bf16[1,1,32,64]{3,2,1,0:T(8,128)(2,1)S(1)}, u32[]{:S(2)}, u32[]{:S(2)}) collective-permute-start(bf16[1,1,32,64]{3,2,1,0:T(8,128)(2,1)S(1)} %get-tuple-element.1605), channel_id=1, source_target_pairs={{1,0},{2,1},{3,2},{4,3},{5,4},{6,5},{7,6},{8,7},{9,8},{10,9},{11,1... | collective-permute-start | bytes 12296 | tf_op jit(solution)/shard_map/while/body/eval_jaxpr/ppermute | solution.py:21
  70.8 13.5 %collective-permute-start.2 = (bf16[1,1,32,64]{3,2,1,0:T(8,128)(2,1)S(1)}, bf16[1,1,32,64]{3,2,1,0:T(8,128)(2,1)S(1)}, u32[]{:S(2)}, u32[]{:S(2)}) collective-permute-start(bf16[1,1,32,64]{3,2,1,0:T(8,128)(2,1)S(1)} %get-tuple-element.1607), channel_id=1, source_target_pairs={{0,1},{1,2},{2,3},{3,4},{4,5},{5,6},{6,7},{7,8},{8,9},{9,10},{10,1... | collective-permute-start | bytes 12296 | tf_op jit(solution)/shard_map/while/body/eval_jaxpr/ppermute | solution.py:19
  74.1 12.2 %collective-permute-start.3 = (bf16[1,1,32,64]{3,2,1,0:T(8,128)(2,1)S(1)}, bf16[1,1,32,64]{3,2,1,0:T(8,128)(2,1)S(1)}, u32[]{:S(2)}, u32[]{:S(2)}) collective-permute-start(bf16[1,1,32,64]{3,2,1,0:T(8,128)(2,1)S(1)} %get-tuple-element.1609), channel_id=1, source_target_pairs={{0,1},{1,2},{2,3},{3,4},{4,5},{5,6},{6,7},{7,8},{8,9},{9,10},{10,1... | collective-permute-start | bytes 12296 | tf_op jit(solution)/shard_map/while/body/eval_jaxpr/ppermute | solution.py:19
  76.4 9.9 %collective-permute-start.4 = (bf16[1,1,32,64]{3,2,1,0:T(8,128)(2,1)S(1)}, bf16[1,1,32,64]{3,2,1,0:T(8,128)(2,1)S(1)}, u32[]{:S(2)}, u32[]{:S(2)}) collective-permute-start(bf16[1,1,32,64]{3,2,1,0:T(8,128)(2,1)S(1)} %get-tuple-element.1611), channel_id=1, source_target_pairs={{0,1},{1,2},{2,3},{3,4},{4,5},{5,6},{6,7},{7,8},{8,9},{9,10},{10,1... | collective-permute-start | bytes 12296 | tf_op jit(solution)/shard_map/while/body/eval_jaxpr/ppermute | solution.py:19
  80.5 6.2 %collective-permute-start.10 = (bf16[1,1,32,64]{3,2,1,0:T(8,128)(2,1)S(1)}, bf16[1,1,32,64]{3,2,1,0:T(8,128)(2,1)S(1)}, u32[]{:S(2)}, u32[]{:S(2)}) collective-permute-start(bf16[1,1,32,64]{3,2,1,0:T(8,128)(2,1)S(1)} %get-tuple-element.1624), channel_id=1, source_target_pairs={{1,0},{2,1},{3,2},{4,3},{5,4},{6,5},{7,6},{8,7},{9,8},{10,9},{11,1... | collective-permute-start | bytes 12296 | tf_op jit(solution)/shard_map/while/body/eval_jaxpr/ppermute | solution.py:21
  82.4 7.3 %collective-permute-start.9 = (bf16[1,1,32,64]{3,2,1,0:T(8,128)(2,1)S(1)}, bf16[1,1,32,64]{3,2,1,0:T(8,128)(2,1)S(1)}, u32[]{:S(2)}, u32[]{:S(2)}) collective-permute-start(bf16[1,1,32,64]{3,2,1,0:T(8,128)(2,1)S(1)} %get-tuple-element.1622), channel_id=1, source_target_pairs={{1,0},{2,1},{3,2},{4,3},{5,4},{6,5},{7,6},{8,7},{9,8},{10,9},{11,1... | collective-permute-start | bytes 12296 | tf_op jit(solution)/shard_map/while/body/eval_jaxpr/ppermute | solution.py:21
  84.3 8.3 %collective-permute-start.5 = (bf16[1,1,32,64]{3,2,1,0:T(8,128)(2,1)S(1)}, bf16[1,1,32,64]{3,2,1,0:T(8,128)(2,1)S(1)}, u32[]{:S(2)}, u32[]{:S(2)}) collective-permute-start(bf16[1,1,32,64]{3,2,1,0:T(8,128)(2,1)S(1)} %get-tuple-element.1613), channel_id=1, source_target_pairs={{1,0},{2,1},{3,2},{4,3},{5,4},{6,5},{7,6},{8,7},{9,8},{10,9},{11,1... | collective-permute-start | bytes 12296 | tf_op jit(solution)/shard_map/while/body/eval_jaxpr/ppermute | solution.py:21
  97.4 12.8 %collective-permute-start.6 = (bf16[1,64,32,64]{3,2,1,0:T(8,128)(2,1)S(1)}, bf16[1,64,32,64]{3,2,1,0:T(8,128)(2,1)S(1)}, u32[]{:S(2)}, u32[]{:S(2)}) collective-permute-start(bf16[1,64,32,64]{3,2,1,0:T(8,128)(2,1)S(1)} %fusion.284), channel_id=1, source_target_pairs={{0,128},{128,256},{256,384},{1,129},{129,257},{257,385},{2,130},{1... | collective-permute-start | bytes 786440 | tf_op jit(solution)/shard_map/while/body/eval_jaxpr/ppermute | solution.py:31
  99.7 20.9 %copy-start.7 = (bf16[1,64,32,64]{3,2,1,0:T(8,128)(2,1)}, bf16[1,64,32,64]{3,2,1,0:T(8,128)(2,1)S(1)}, u32[]{:S(2)}) copy-start(bf16[1,64,32,64]{3,2,1,0:T(8,128)(2,1)S(1)} %fusion.287) | copy-start | bytes 786436 | tf_op jit(solution)/shard_map/while
  111.6 8.0 %collective-permute-start.7 = (f32[1,1,24,64]{3,1,2,0:T(1,128)S(1)}, f32[1,1,24,64]{3,1,2,0:T(1,128)S(1)}, u32[]{:S(2)}, u32[]{:S(2)}) collective-permute-start(f32[1,1,24,64]{3,1,2,0:T(1,128)S(1)} %slice.537), channel_id=1, source_target_pairs={{1,0},{2,1},{3,2},{4,3},{5,4},{6,5},{7,6},{8,7},{9,8},{10,9},{11,1... | collective-permute-start | bytes 18440 | tf_op jit(solution)/shard_map/while/body/eval_jaxpr/ppermute | solution.py:21
  113.6 6.6 %collective-permute-start.8 = (f32[1,1,24,64]{3,2,1,0:T(8,128)S(1)}, f32[1,1,24,64]{3,2,1,0:T(8,128)S(1)}, u32[]{:S(2)}, u32[]{:S(2)}) collective-permute-start(f32[1,1,24,64]{3,2,1,0:T(8,128)S(1)} %bitcast.472), channel_id=1, source_target_pairs={{0,1},{1,2},{2,3},{3,4},{4,5},{5,6},{6,7},{7,8},{8,9},{9,10},{10,1... | collective-permute-start | bytes 18440 | tf_op jit(solution)/shard_map/while/body/eval_jaxpr/ppermute | solution.py:19
  122.0 9.8 %collective-permute-start = (bf16[1,1,32,64]{3,2,1,0:T(8,128)(2,1)S(1)}, bf16[1,1,32,64]{3,2,1,0:T(8,128)(2,1)S(1)}, u32[]{:S(2)}, u32[]{:S(2)}) collective-permute-start(bf16[1,1,32,64]{3,2,1,0:T(8,128)(2,1)S(1)} %get-tuple-element.1604), channel_id=1, source_target_pairs={{0,1},{1,2},{2,3},{3,4},{4,5},{5,6},{6,7},{7,8},{8,9},{9,10},{10,1... | collective-permute-start | bytes 12296 | tf_op jit(solution)/shard_map/while/body/eval_jaxpr/ppermute | solution.py:19
  125.8 7.2 %collective-permute-start.1 = (bf16[1,1,32,64]{3,2,1,0:T(8,128)(2,1)S(1)}, bf16[1,1,32,64]{3,2,1,0:T(8,128)(2,1)S(1)}, u32[]{:S(2)}, u32[]{:S(2)}) collective-permute-start(bf16[1,1,32,64]{3,2,1,0:T(8,128)(2,1)S(1)} %get-tuple-element.1605), channel_id=1, source_target_pairs={{1,0},{2,1},{3,2},{4,3},{5,4},{6,5},{7,6},{8,7},{9,8},{10,9},{11,1... | collective-permute-start | bytes 12296 | tf_op jit(solution)/shard_map/while/body/eval_jaxpr/ppermute | solution.py:21
  139.4 16.2 %collective-permute-start.2 = (bf16[1,1,32,64]{3,2,1,0:T(8,128)(2,1)S(1)}, bf16[1,1,32,64]{3,2,1,0:T(8,128)(2,1)S(1)}, u32[]{:S(2)}, u32[]{:S(2)}) collective-permute-start(bf16[1,1,32,64]{3,2,1,0:T(8,128)(2,1)S(1)} %get-tuple-element.1607), channel_id=1, source_target_pairs={{0,1},{1,2},{2,3},{3,4},{4,5},{5,6},{6,7},{7,8},{8,9},{9,10},{10,1... | collective-permute-start | bytes 12296 | tf_op jit(solution)/shard_map/while/body/eval_jaxpr/ppermute | solution.py:19
  144.3 13.3 %collective-permute-start.3 = (bf16[1,1,32,64]{3,2,1,0:T(8,128)(2,1)S(1)}, bf16[1,1,32,64]{3,2,1,0:T(8,128)(2,1)S(1)}, u32[]{:S(2)}, u32[]{:S(2)}) collective-permute-start(bf16[1,1,32,64]{3,2,1,0:T(8,128)(2,1)S(1)} %get-tuple-element.1609), channel_id=1, source_target_pairs={{0,1},{1,2},{2,3},{3,4},{4,5},{5,6},{6,7},{7,8},{8,9},{9,10},{10,1... | collective-permute-start | bytes 12296 | tf_op jit(solution)/shard_map/while/body/eval_jaxpr/ppermute | solution.py:19
  148.1 9.5 %collective-permute-start.4 = (bf16[1,1,32,64]{3,2,1,0:T(8,128)(2,1)S(1)}, bf16[1,1,32,64]{3,2,1,0:T(8,128)(2,1)S(1)}, u32[]{:S(2)}, u32[]{:S(2)}) collective-permute-start(bf16[1,1,32,64]{3,2,1,0:T(8,128)(2,1)S(1)} %get-tuple-element.1611), channel_id=1, source_target_pairs={{0,1},{1,2},{2,3},{3,4},{4,5},{5,6},{6,7},{7,8},{8,9},{9,10},{10,1... | collective-permute-start | bytes 12296 | tf_op jit(solution)/shard_map/while/body/eval_jaxpr/ppermute | solution.py:19
  151.8 6.2 %collective-permute-start.10 = (bf16[1,1,32,64]{3,2,1,0:T(8,128)(2,1)S(1)}, bf16[1,1,32,64]{3,2,1,0:T(8,128)(2,1)S(1)}, u32[]{:S(2)}, u32[]{:S(2)}) collective-permute-start(bf16[1,1,32,64]{3,2,1,0:T(8,128)(2,1)S(1)} %get-tuple-element.1624), channel_id=1, source_target_pairs={{1,0},{2,1},{3,2},{4,3},{5,4},{6,5},{7,6},{8,7},{9,8},{10,9},{11,1... | collective-permute-start | bytes 12296 | tf_op jit(solution)/shard_map/while/body/eval_jaxpr/ppermute | solution.py:21
  153.7 7.3 %collective-permute-start.9 = (bf16[1,1,32,64]{3,2,1,0:T(8,128)(2,1)S(1)}, bf16[1,1,32,64]{3,2,1,0:T(8,128)(2,1)S(1)}, u32[]{:S(2)}, u32[]{:S(2)}) collective-permute-start(bf16[1,1,32,64]{3,2,1,0:T(8,128)(2,1)S(1)} %get-tuple-element.1622), channel_id=1, source_target_pairs={{1,0},{2,1},{3,2},{4,3},{5,4},{6,5},{7,6},{8,7},{9,8},{10,9},{11,1... | collective-permute-start | bytes 12296 | tf_op jit(solution)/shard_map/while/body/eval_jaxpr/ppermute | solution.py:21
  155.7 8.3 %collective-permute-start.5 = (bf16[1,1,32,64]{3,2,1,0:T(8,128)(2,1)S(1)}, bf16[1,1,32,64]{3,2,1,0:T(8,128)(2,1)S(1)}, u32[]{:S(2)}, u32[]{:S(2)}) collective-permute-start(bf16[1,1,32,64]{3,2,1,0:T(8,128)(2,1)S(1)} %get-tuple-element.1613), channel_id=1, source_target_pairs={{1,0},{2,1},{3,2},{4,3},{5,4},{6,5},{7,6},{8,7},{9,8},{10,9},{11,1... | collective-permute-start | bytes 12296 | tf_op jit(solution)/shard_map/while/body/eval_jaxpr/ppermute | solution.py:21
  168.7 12.9 %collective-permute-start.6 = (bf16[1,64,32,64]{3,2,1,0:T(8,128)(2,1)S(1)}, bf16[1,64,32,64]{3,2,1,0:T(8,128)(2,1)S(1)}, u32[]{:S(2)}, u32[]{:S(2)}) collective-permute-start(bf16[1,64,32,64]{3,2,1,0:T(8,128)(2,1)S(1)} %fusion.284), channel_id=1, source_target_pairs={{0,128},{128,256},{256,384},{1,129},{129,257},{257,385},{2,130},{1... | collective-permute-start | bytes 786440 | tf_op jit(solution)/shard_map/while/body/eval_jaxpr/ppermute | solution.py:31
  171.0 22.6 %copy-start.7 = (bf16[1,64,32,64]{3,2,1,0:T(8,128)(2,1)}, bf16[1,64,32,64]{3,2,1,0:T(8,128)(2,1)S(1)}, u32[]{:S(2)}) copy-start(bf16[1,64,32,64]{3,2,1,0:T(8,128)(2,1)S(1)} %fusion.287) | copy-start | bytes 786436 | tf_op jit(solution)/shard_map/while
  181.6 10.7 %copy-start.4 = (f32[2,3,3,64,64]{4,3,2,1,0:T(8,128)S(1)}, f32[2,3,3,64,64]{4,3,2,1,0:T(8,128)}, u32[]{:S(2)}) copy-start(f32[2,3,3,64,64]{4,3,2,1,0:T(8,128)} %get-tuple-element.1667) | copy-start | bytes 884740 | tf_op jit(solution)/shard_map/while
  181.6 10.7 %copy-start.10 = (f32[9,64,64]{2,1,0:T(8,128)S(1)}, f32[9,64,64]{2,1,0:T(8,128)}, u32[]{:S(2)}) copy-start(f32[9,64,64]{2,1,0:T(8,128)} %copy-done.9) | copy-start | bytes 442372 | tf_op jit(solution)/shard_map/while
  181.6 10.7 %copy-start.12 = (f32[9,64,64]{2,1,0:T(8,128)S(1)}, f32[9,64,64]{2,1,0:T(8,128)}, u32[]{:S(2)}) copy-start(f32[9,64,64]{2,1,0:T(8,128)} %copy-done.11) | copy-start | bytes 442372 | tf_op jit(solution)/shard_map/while
  183.0 9.6 %collective-permute-start.7 = (f32[1,1,24,64]{3,1,2,0:T(1,128)S(1)}, f32[1,1,24,64]{3,1,2,0:T(1,128)S(1)}, u32[]{:S(2)}, u32[]{:S(2)}) collective-permute-start(f32[1,1,24,64]{3,1,2,0:T(1,128)S(1)} %slice.537), channel_id=1, source_target_pairs={{1,0},{2,1},{3,2},{4,3},{5,4},{6,5},{7,6},{8,7},{9,8},{10,9},{11,1... | collective-permute-start | bytes 18440 | tf_op jit(solution)/shard_map/while/body/eval_jaxpr/ppermute | solution.py:21
  184.9 8.2 %collective-permute-start.8 = (f32[1,1,24,64]{3,2,1,0:T(8,128)S(1)}, f32[1,1,24,64]{3,2,1,0:T(8,128)S(1)}, u32[]{:S(2)}, u32[]{:S(2)}) collective-permute-start(f32[1,1,24,64]{3,2,1,0:T(8,128)S(1)} %bitcast.472), channel_id=1, source_target_pairs={{0,1},{1,2},{2,3},{3,4},{4,5},{5,6},{6,7},{7,8},{8,9},{9,10},{10,1... | collective-permute-start | bytes 18440 | tf_op jit(solution)/shard_map/while/body/eval_jaxpr/ppermute | solution.py:19
  195.0 9.8 %collective-permute-start = (bf16[1,1,32,64]{3,2,1,0:T(8,128)(2,1)S(1)}, bf16[1,1,32,64]{3,2,1,0:T(8,128)(2,1)S(1)}, u32[]{:S(2)}, u32[]{:S(2)}) collective-permute-start(bf16[1,1,32,64]{3,2,1,0:T(8,128)(2,1)S(1)} %get-tuple-element.1604), channel_id=1, source_target_pairs={{0,1},{1,2},{2,3},{3,4},{4,5},{5,6},{6,7},{7,8},{8,9},{9,10},{10,1... | collective-permute-start | bytes 12296 | tf_op jit(solution)/shard_map/while/body/eval_jaxpr/ppermute | solution.py:19
  198.8 6.2 %collective-permute-start.1 = (bf16[1,1,32,64]{3,2,1,0:T(8,128)(2,1)S(1)}, bf16[1,1,32,64]{3,2,1,0:T(8,128)(2,1)S(1)}, u32[]{:S(2)}, u32[]{:S(2)}) collective-permute-start(bf16[1,1,32,64]{3,2,1,0:T(8,128)(2,1)S(1)} %get-tuple-element.1605), channel_id=1, source_target_pairs={{1,0},{2,1},{3,2},{4,3},{5,4},{6,5},{7,6},{8,7},{9,8},{10,9},{11,1... | collective-permute-start | bytes 12296 | tf_op jit(solution)/shard_map/while/body/eval_jaxpr/ppermute | solution.py:21
  211.4 15.3 %collective-permute-start.2 = (bf16[1,1,32,64]{3,2,1,0:T(8,128)(2,1)S(1)}, bf16[1,1,32,64]{3,2,1,0:T(8,128)(2,1)S(1)}, u32[]{:S(2)}, u32[]{:S(2)}) collective-permute-start(bf16[1,1,32,64]{3,2,1,0:T(8,128)(2,1)S(1)} %get-tuple-element.1607), channel_id=1, source_target_pairs={{0,1},{1,2},{2,3},{3,4},{4,5},{5,6},{6,7},{7,8},{8,9},{9,10},{10,1... | collective-permute-start | bytes 12296 | tf_op jit(solution)/shard_map/while/body/eval_jaxpr/ppermute | solution.py:19
  215.0 13.5 %collective-permute-start.3 = (bf16[1,1,32,64]{3,2,1,0:T(8,128)(2,1)S(1)}, bf16[1,1,32,64]{3,2,1,0:T(8,128)(2,1)S(1)}, u32[]{:S(2)}, u32[]{:S(2)}) collective-permute-start(bf16[1,1,32,64]{3,2,1,0:T(8,128)(2,1)S(1)} %get-tuple-element.1609), channel_id=1, source_target_pairs={{0,1},{1,2},{2,3},{3,4},{4,5},{5,6},{6,7},{7,8},{8,9},{9,10},{10,1... | collective-permute-start | bytes 12296 | tf_op jit(solution)/shard_map/while/body/eval_jaxpr/ppermute | solution.py:19
  217.9 10.7 %collective-permute-start.4 = (bf16[1,1,32,64]{3,2,1,0:T(8,128)(2,1)S(1)}, bf16[1,1,32,64]{3,2,1,0:T(8,128)(2,1)S(1)}, u32[]{:S(2)}, u32[]{:S(2)}) collective-permute-start(bf16[1,1,32,64]{3,2,1,0:T(8,128)(2,1)S(1)} %get-tuple-element.1611), channel_id=1, source_target_pairs={{0,1},{1,2},{2,3},{3,4},{4,5},{5,6},{6,7},{7,8},{8,9},{9,10},{10,1... | collective-permute-start | bytes 12296 | tf_op jit(solution)/shard_map/while/body/eval_jaxpr/ppermute | solution.py:19
  222.8 6.2 %collective-permute-start.10 = (bf16[1,1,32,64]{3,2,1,0:T(8,128)(2,1)S(1)}, bf16[1,1,32,64]{3,2,1,0:T(8,128)(2,1)S(1)}, u32[]{:S(2)}, u32[]{:S(2)}) collective-permute-start(bf16[1,1,32,64]{3,2,1,0:T(8,128)(2,1)S(1)} %get-tuple-element.1624), channel_id=1, source_target_pairs={{1,0},{2,1},{3,2},{4,3},{5,4},{6,5},{7,6},{8,7},{9,8},{10,9},{11,1... | collective-permute-start | bytes 12296 | tf_op jit(solution)/shard_map/while/body/eval_jaxpr/ppermute | solution.py:21
  224.7 7.3 %collective-permute-start.9 = (bf16[1,1,32,64]{3,2,1,0:T(8,128)(2,1)S(1)}, bf16[1,1,32,64]{3,2,1,0:T(8,128)(2,1)S(1)}, u32[]{:S(2)}, u32[]{:S(2)}) collective-permute-start(bf16[1,1,32,64]{3,2,1,0:T(8,128)(2,1)S(1)} %get-tuple-element.1622), channel_id=1, source_target_pairs={{1,0},{2,1},{3,2},{4,3},{5,4},{6,5},{7,6},{8,7},{9,8},{10,9},{11,1... | collective-permute-start | bytes 12296 | tf_op jit(solution)/shard_map/while/body/eval_jaxpr/ppermute | solution.py:21
  226.6 8.3 %collective-permute-start.5 = (bf16[1,1,32,64]{3,2,1,0:T(8,128)(2,1)S(1)}, bf16[1,1,32,64]{3,2,1,0:T(8,128)(2,1)S(1)}, u32[]{:S(2)}, u32[]{:S(2)}) collective-permute-start(bf16[1,1,32,64]{3,2,1,0:T(8,128)(2,1)S(1)} %get-tuple-element.1613), channel_id=1, source_target_pairs={{1,0},{2,1},{3,2},{4,3},{5,4},{6,5},{7,6},{8,7},{9,8},{10,9},{11,1... | collective-permute-start | bytes 12296 | tf_op jit(solution)/shard_map/while/body/eval_jaxpr/ppermute | solution.py:21
  239.7 12.8 %collective-permute-start.6 = (bf16[1,64,32,64]{3,2,1,0:T(8,128)(2,1)S(1)}, bf16[1,64,32,64]{3,2,1,0:T(8,128)(2,1)S(1)}, u32[]{:S(2)}, u32[]{:S(2)}) collective-permute-start(bf16[1,64,32,64]{3,2,1,0:T(8,128)(2,1)S(1)} %fusion.284), channel_id=1, source_target_pairs={{0,128},{128,256},{256,384},{1,129},{129,257},{257,385},{2,130},{1... | collective-permute-start | bytes 786440 | tf_op jit(solution)/shard_map/while/body/eval_jaxpr/ppermute | solution.py:31
  242.0 22.0 %copy-start.7 = (bf16[1,64,32,64]{3,2,1,0:T(8,128)(2,1)}, bf16[1,64,32,64]{3,2,1,0:T(8,128)(2,1)S(1)}, u32[]{:S(2)}) copy-start(bf16[1,64,32,64]{3,2,1,0:T(8,128)(2,1)S(1)} %fusion.287) | copy-start | bytes 786436 | tf_op jit(solution)/shard_map/while
  252.6 10.2 %copy-start.10 = (f32[9,64,64]{2,1,0:T(8,128)S(1)}, f32[9,64,64]{2,1,0:T(8,128)}, u32[]{:S(2)}) copy-start(f32[9,64,64]{2,1,0:T(8,128)} %copy-done.9) | copy-start | bytes 442372 | tf_op jit(solution)/shard_map/while
  252.6 10.2 %copy-start.12 = (f32[9,64,64]{2,1,0:T(8,128)S(1)}, f32[9,64,64]{2,1,0:T(8,128)}, u32[]{:S(2)}) copy-start(f32[9,64,64]{2,1,0:T(8,128)} %copy-done.11) | copy-start | bytes 442372 | tf_op jit(solution)/shard_map/while
  253.9 9.1 %collective-permute-start.7 = (f32[1,1,24,64]{3,1,2,0:T(1,128)S(1)}, f32[1,1,24,64]{3,1,2,0:T(1,128)S(1)}, u32[]{:S(2)}, u32[]{:S(2)}) collective-permute-start(f32[1,1,24,64]{3,1,2,0:T(1,128)S(1)} %slice.537), channel_id=1, source_target_pairs={{1,0},{2,1},{3,2},{4,3},{5,4},{6,5},{7,6},{8,7},{9,8},{10,9},{11,1... | collective-permute-start | bytes 18440 | tf_op jit(solution)/shard_map/while/body/eval_jaxpr/ppermute | solution.py:21
  255.9 7.7 %collective-permute-start.8 = (f32[1,1,24,64]{3,2,1,0:T(8,128)S(1)}, f32[1,1,24,64]{3,2,1,0:T(8,128)S(1)}, u32[]{:S(2)}, u32[]{:S(2)}) collective-permute-start(f32[1,1,24,64]{3,2,1,0:T(8,128)S(1)} %bitcast.472), channel_id=1, source_target_pairs={{0,1},{1,2},{2,3},{3,4},{4,5},{5,6},{6,7},{7,8},{8,9},{9,10},{10,1... | collective-permute-start | bytes 18440 | tf_op jit(solution)/shard_map/while/body/eval_jaxpr/ppermute | solution.py:19
  265.5 9.8 %collective-permute-start = (bf16[1,1,32,64]{3,2,1,0:T(8,128)(2,1)S(1)}, bf16[1,1,32,64]{3,2,1,0:T(8,128)(2,1)S(1)}, u32[]{:S(2)}, u32[]{:S(2)}) collective-permute-start(bf16[1,1,32,64]{3,2,1,0:T(8,128)(2,1)S(1)} %get-tuple-element.1604), channel_id=1, source_target_pairs={{0,1},{1,2},{2,3},{3,4},{4,5},{5,6},{6,7},{7,8},{8,9},{9,10},{10,1... | collective-permute-start | bytes 12296 | tf_op jit(solution)/shard_map/while/body/eval_jaxpr/ppermute | solution.py:19
  269.2 6.2 %collective-permute-start.1 = (bf16[1,1,32,64]{3,2,1,0:T(8,128)(2,1)S(1)}, bf16[1,1,32,64]{3,2,1,0:T(8,128)(2,1)S(1)}, u32[]{:S(2)}, u32[]{:S(2)}) collective-permute-start(bf16[1,1,32,64]{3,2,1,0:T(8,128)(2,1)S(1)} %get-tuple-element.1605), channel_id=1, source_target_pairs={{1,0},{2,1},{3,2},{4,3},{5,4},{6,5},{7,6},{8,7},{9,8},{10,9},{11,1... | collective-permute-start | bytes 12296 | tf_op jit(solution)/shard_map/while/body/eval_jaxpr/ppermute | solution.py:21
  281.8 16.6 %collective-permute-start.2 = (bf16[1,1,32,64]{3,2,1,0:T(8,128)(2,1)S(1)}, bf16[1,1,32,64]{3,2,1,0:T(8,128)(2,1)S(1)}, u32[]{:S(2)}, u32[]{:S(2)}) collective-permute-start(bf16[1,1,32,64]{3,2,1,0:T(8,128)(2,1)S(1)} %get-tuple-element.1607), channel_id=1, source_target_pairs={{0,1},{1,2},{2,3},{3,4},{4,5},{5,6},{6,7},{7,8},{8,9},{9,10},{10,1... | collective-permute-start | bytes 12296 | tf_op jit(solution)/shard_map/while/body/eval_jaxpr/ppermute | solution.py:19
  285.5 14.9 %collective-permute-start.3 = (bf16[1,1,32,64]{3,2,1,0:T(8,128)(2,1)S(1)}, bf16[1,1,32,64]{3,2,1,0:T(8,128)(2,1)S(1)}, u32[]{:S(2)}, u32[]{:S(2)}) collective-permute-start(bf16[1,1,32,64]{3,2,1,0:T(8,128)(2,1)S(1)} %get-tuple-element.1609), channel_id=1, source_target_pairs={{0,1},{1,2},{2,3},{3,4},{4,5},{5,6},{6,7},{7,8},{8,9},{9,10},{10,1... | collective-permute-start | bytes 12296 | tf_op jit(solution)/shard_map/while/body/eval_jaxpr/ppermute | solution.py:19
  289.7 10.7 %collective-permute-start.4 = (bf16[1,1,32,64]{3,2,1,0:T(8,128)(2,1)S(1)}, bf16[1,1,32,64]{3,2,1,0:T(8,128)(2,1)S(1)}, u32[]{:S(2)}, u32[]{:S(2)}) collective-permute-start(bf16[1,1,32,64]{3,2,1,0:T(8,128)(2,1)S(1)} %get-tuple-element.1611), channel_id=1, source_target_pairs={{0,1},{1,2},{2,3},{3,4},{4,5},{5,6},{6,7},{7,8},{8,9},{9,10},{10,1... | collective-permute-start | bytes 12296 | tf_op jit(solution)/shard_map/while/body/eval_jaxpr/ppermute | solution.py:19
  294.6 6.2 %collective-permute-start.10 = (bf16[1,1,32,64]{3,2,1,0:T(8,128)(2,1)S(1)}, bf16[1,1,32,64]{3,2,1,0:T(8,128)(2,1)S(1)}, u32[]{:S(2)}, u32[]{:S(2)}) collective-permute-start(bf16[1,1,32,64]{3,2,1,0:T(8,128)(2,1)S(1)} %get-tuple-element.1624), channel_id=1, source_target_pairs={{1,0},{2,1},{3,2},{4,3},{5,4},{6,5},{7,6},{8,7},{9,8},{10,9},{11,1... | collective-permute-start | bytes 12296 | tf_op jit(solution)/shard_map/while/body/eval_jaxpr/ppermute | solution.py:21
  296.5 7.3 %collective-permute-start.9 = (bf16[1,1,32,64]{3,2,1,0:T(8,128)(2,1)S(1)}, bf16[1,1,32,64]{3,2,1,0:T(8,128)(2,1)S(1)}, u32[]{:S(2)}, u32[]{:S(2)}) collective-permute-start(bf16[1,1,32,64]{3,2,1,0:T(8,128)(2,1)S(1)} %get-tuple-element.1622), channel_id=1, source_target_pairs={{1,0},{2,1},{3,2},{4,3},{5,4},{6,5},{7,6},{8,7},{9,8},{10,9},{11,1... | collective-permute-start | bytes 12296 | tf_op jit(solution)/shard_map/while/body/eval_jaxpr/ppermute | solution.py:21
  298.5 8.3 %collective-permute-start.5 = (bf16[1,1,32,64]{3,2,1,0:T(8,128)(2,1)S(1)}, bf16[1,1,32,64]{3,2,1,0:T(8,128)(2,1)S(1)}, u32[]{:S(2)}, u32[]{:S(2)}) collective-permute-start(bf16[1,1,32,64]{3,2,1,0:T(8,128)(2,1)S(1)} %get-tuple-element.1613), channel_id=1, source_target_pairs={{1,0},{2,1},{3,2},{4,3},{5,4},{6,5},{7,6},{8,7},{9,8},{10,9},{11,1... | collective-permute-start | bytes 12296 | tf_op jit(solution)/shard_map/while/body/eval_jaxpr/ppermute | solution.py:21
  311.5 12.8 %collective-permute-start.6 = (bf16[1,64,32,64]{3,2,1,0:T(8,128)(2,1)S(1)}, bf16[1,64,32,64]{3,2,1,0:T(8,128)(2,1)S(1)}, u32[]{:S(2)}, u32[]{:S(2)}) collective-permute-start(bf16[1,64,32,64]{3,2,1,0:T(8,128)(2,1)S(1)} %fusion.284), channel_id=1, source_target_pairs={{0,128},{128,256},{256,384},{1,129},{129,257},{257,385},{2,130},{1... | collective-permute-start | bytes 786440 | tf_op jit(solution)/shard_map/while/body/eval_jaxpr/ppermute | solution.py:31
  313.8 22.0 %copy-start.7 = (bf16[1,64,32,64]{3,2,1,0:T(8,128)(2,1)}, bf16[1,64,32,64]{3,2,1,0:T(8,128)(2,1)S(1)}, u32[]{:S(2)}) copy-start(bf16[1,64,32,64]{3,2,1,0:T(8,128)(2,1)S(1)} %fusion.287) | copy-start | bytes 786436 | tf_op jit(solution)/shard_map/while
  324.4 10.2 %copy-start.4 = (f32[2,3,3,64,64]{4,3,2,1,0:T(8,128)S(1)}, f32[2,3,3,64,64]{4,3,2,1,0:T(8,128)}, u32[]{:S(2)}) copy-start(f32[2,3,3,64,64]{4,3,2,1,0:T(8,128)} %get-tuple-element.1667) | copy-start | bytes 884740 | tf_op jit(solution)/shard_map/while
  324.4 10.2 %copy-start.10 = (f32[9,64,64]{2,1,0:T(8,128)S(1)}, f32[9,64,64]{2,1,0:T(8,128)}, u32[]{:S(2)}) copy-start(f32[9,64,64]{2,1,0:T(8,128)} %copy-done.9) | copy-start | bytes 442372 | tf_op jit(solution)/shard_map/while
  324.4 10.2 %copy-start.12 = (f32[9,64,64]{2,1,0:T(8,128)S(1)}, f32[9,64,64]{2,1,0:T(8,128)}, u32[]{:S(2)}) copy-start(f32[9,64,64]{2,1,0:T(8,128)} %copy-done.11) | copy-start | bytes 442372 | tf_op jit(solution)/shard_map/while
  325.7 9.1 %collective-permute-start.7 = (f32[1,1,24,64]{3,1,2,0:T(1,128)S(1)}, f32[1,1,24,64]{3,1,2,0:T(1,128)S(1)}, u32[]{:S(2)}, u32[]{:S(2)}) collective-permute-start(f32[1,1,24,64]{3,1,2,0:T(1,128)S(1)} %slice.537), channel_id=1, source_target_pairs={{1,0},{2,1},{3,2},{4,3},{5,4},{6,5},{7,6},{8,7},{9,8},{10,9},{11,1... | collective-permute-start | bytes 18440 | tf_op jit(solution)/shard_map/while/body/eval_jaxpr/ppermute | solution.py:21
  327.7 7.7 %collective-permute-start.8 = (f32[1,1,24,64]{3,2,1,0:T(8,128)S(1)}, f32[1,1,24,64]{3,2,1,0:T(8,128)S(1)}, u32[]{:S(2)}, u32[]{:S(2)}) collective-permute-start(f32[1,1,24,64]{3,2,1,0:T(8,128)S(1)} %bitcast.472), channel_id=1, source_target_pairs={{0,1},{1,2},{2,3},{3,4},{4,5},{5,6},{6,7},{7,8},{8,9},{9,10},{10,1... | collective-permute-start | bytes 18440 | tf_op jit(solution)/shard_map/while/body/eval_jaxpr/ppermute | solution.py:19
  337.6 72.5 %copy-start.8 = (bf16[1,64,32,64]{3,2,1,0:T(8,128)(2,1)S(1)}, bf16[1,64,32,64]{3,2,1,0:T(8,128)(2,1)}, u32[]{:S(2)}) copy-start(bf16[1,64,32,64]{3,2,1,0:T(8,128)(2,1)} %get-tuple-element.967) | copy-start | bytes 786436
  (38 other events, 80.6 us)

commit v2 on v1

v2 whole, which is shorter than its diff:
```python
import functools
import math

import jax
import jax.numpy as jnp
from jax import lax
from jax.experimental import pallas as pl
from jax.experimental.pallas import tpu as pltpu
from jax.sharding import PartitionSpec as P

LEAK = 0.05
RING = 8
PIECE = 40
HALF = RING * PIECE
PACKED = 2 * HALF
MESH = pl.DeviceIdType.MESH


def reduce_body(
    src, out, pair_in, y_sum, y_in, z_out, z_in, gathered,
    pair_send, pair_recv, y_send, y_recv, z_send, z_recv, g_send, g_recv, p_send, p_recv,
):
    strip = lax.axis_index("strip")
    core = lax.rem(strip, 2)
    row = lax.rem(lax.div(strip, 2), RING)
    deep = lax.div(strip, 2 * RING)
    partner = strip + 1 - 2 * core

    def y_peer(step):
        return (deep * RING + lax.rem(row + step, RING)) * 2 + core

    def z_peer(step):
        return (lax.rem(deep + step, RING) * RING + row) * 2 + core

    def remote(src_ref, dst_ref, send, recv, strip_id):
        return pltpu.make_async_remote_copy(
            src_ref=src_ref,
            dst_ref=dst_ref,
            send_sem=send,
            recv_sem=recv,
            device_id=(lax.axis_index("section"), strip_id),
            device_id_type=MESH,
        )

    barrier = pltpu.get_barrier_semaphore()
    peers = [partner]
    peers += [y_peer(step) for step in range(1, RING)]
    peers += [z_peer(step) for step in range(1, RING)]
    for peer in peers:
        pl.semaphore_signal(
            barrier,
            inc=1,
            device_id=(lax.axis_index("section"), peer),
            device_id_type=MESH,
        )
    pl.semaphore_wait(barrier, len(peers))

    mine = pl.multiple_of(core * HALF, 8)
    other = pl.multiple_of((1 - core) * HALF, 8)
    swap = remote(src.at[pl.ds(other, HALF)], pair_in, pair_send, pair_recv, partner)
    swap.start()
    swap.wait()
    y_sum[...] = src[pl.ds(mine, HALF), :] + pair_in[...]

    def piece(ref, index):
        return ref.at[pl.ds(pl.multiple_of(index * PIECE, 8), PIECE)]

    scatter = []
    for step in range(1, RING):
        copy = remote(
            piece(y_sum, lax.rem(row + step, RING)),
            y_in.at[step - 1],
            y_send.at[step - 1],
            y_recv.at[step - 1],
            y_peer(step),
        )
        copy.start()
        scatter.append(copy)
    total = y_sum[pl.ds(pl.multiple_of(row * PIECE, 8), PIECE), :]
    for step in range(1, RING):
        scatter[step - 1].wait_recv()
        total = total + y_in[step - 1]
    z_out[...] = total
    z_in[deep] = total
    trade = []
    for step in range(1, RING):
        copy = remote(
            z_out, z_in.at[deep], z_send.at[step - 1], z_recv.at[step - 1], z_peer(step)
        )
        copy.start()
        trade.append(copy)
    for copy in trade:
        copy.wait_recv()
    total = z_in[0]
    for index in range(1, RING):
        total = total + z_in[index]
    own = core * RING + row
    gathered[pl.ds(pl.multiple_of(own * PIECE, 8), PIECE), :] = total
    gather = []
    for step in range(1, RING):
        copy = remote(
            piece(gathered, own),
            piece(gathered, own),
            g_send.at[step - 1],
            g_recv.at[step - 1],
            y_peer(step),
        )
        copy.start()
        gather.append(copy)
    passed = []
    copy = remote(piece(gathered, own), piece(gathered, own), p_send.at[0], p_recv.at[0], partner)
    copy.start()
    passed.append(copy)
    for step in range(1, RING):
        gather[step - 1].wait_recv()
        came = core * RING + lax.rem(row + RING - step, RING)
        copy = remote(
            piece(gathered, came),
            piece(gathered, came),
            p_send.at[step],
            p_recv.at[step],
            partner,
        )
        copy.start()
        passed.append(copy)
    for copy in passed:
        copy.wait_recv()
    out[...] = gathered[...]
    for copy in scatter + trade + gather + passed:
        copy.wait_send()


def strip_sum(packed):
    dma = pltpu.SemaphoreType.DMA
    return pl.pallas_call(
        reduce_body,
        out_shape=jax.ShapeDtypeStruct((PACKED, 128), jnp.float32),
        in_specs=[pl.BlockSpec(memory_space=pltpu.VMEM)],
        out_specs=pl.BlockSpec(memory_space=pltpu.VMEM),
        scratch_shapes=[
            pltpu.VMEM((HALF, 128), jnp.float32),
            pltpu.VMEM((HALF, 128), jnp.float32),
            pltpu.VMEM((RING - 1, PIECE, 128), jnp.float32),
            pltpu.VMEM((PIECE, 128), jnp.float32),
            pltpu.VMEM((RING, PIECE, 128), jnp.float32),
            pltpu.VMEM((PACKED, 128), jnp.float32),
            dma, dma,
            dma((RING - 1,)), dma((RING - 1,)),
            dma((RING - 1,)), dma((RING - 1,)),
            dma((RING - 1,)), dma((RING - 1,)),
            dma((RING,)), dma((RING,)),
        ],
        compiler_params=pltpu.CompilerParams(collective_id=1, has_side_effects=True),
    )(packed)


SECTIONS = 4
ROWS = 64
COLS = 32
CH = 64
GROUP = 4 * CH
SIDE = 2 * CH
BLOCK = 32
NARROW = 16


def plans():
    reach = [0] * SECTIONS
    for level in reversed(range(SECTIONS - 1)):
        reach[level] = (8 * (reach[level + 1] + 2) + 7) // 6
    result = []
    for level in range(SECTIONS):
        rows = ROWS * 3**level // 4**level
        cols = COLS * 3**level // 4**level
        halo = reach[level] + 4
        lead = -(-halo // 8) * 8
        tall = -(-(lead + rows + halo) // 16) * 16
        first = max(0, (rows - halo) // 16 * 16)
        first = min(first, ROWS - BLOCK)
        if rows - first > BLOCK:
            first += 16
        result.append(
            dict(
                rows=rows,
                cols=cols,
                reach=reach[level],
                halo=halo,
                lead=lead,
                tall=tall,
                groups=-(-cols // 4),
                first=first,
            )
        )
    return result


PLANS = plans()
TALL = max(plan["tall"] for plan in PLANS)
WIDE = max(plan["groups"] for plan in PLANS) * GROUP
NEXT_TALL = max(plan["tall"] for plan in PLANS[1:])
NEXT_WIDE = max(plan["groups"] for plan in PLANS[1:]) * GROUP
DEEP = max(plan["tall"] * plan["groups"] for plan in PLANS)


def column_weights(level):
    fine, coarse = PLANS[level]["cols"], PLANS[level + 1]["cols"]
    table = {}
    for col in range(fine):
        num = max((2 * col + 1) * coarse - fine, 0)
        low = num // (2 * fine)
        frac = (num - 2 * fine * low) / (2 * fine)
        high = min(low + 1, coarse - 1)
        table[col, low] = table.get((col, low), 0.0) + 1.0 - frac
        table[col, high] = table.get((col, high), 0.0) + frac
    return {key: value for key, value in table.items() if value != 0.0}


def column_windows(level):
    table = column_weights(level)
    limit = PLANS[level]["groups"] * 4 - 8
    starts = []
    for group in range(PLANS[level + 1]["groups"]):
        used = [fine for fine, coarse in table if coarse // 4 == group]
        start = min(min(used) // 2 * 2, limit)
        assert max(used) < start + 8
        starts.append(start)
    return starts


def iota(shape, axis):
    return lax.broadcasted_iota(jnp.int32, shape, axis)


def mat(left, right):
    return jnp.dot(left, right, preferred_element_type=jnp.float32)


def one_hot(cond):
    return jnp.where(cond, 1.0, 0.0).astype(jnp.bfloat16)


def each_group(count, body):
    step = 2 if count % 2 == 0 else 1

    def run(index, carry):
        for extra in range(step):
            body(index * step + extra)
        return carry

    lax.fori_loop(0, count // step, run, 0)


def lanes(start, size):
    return pl.ds(pl.multiple_of(start, 128), size)


def chain_body(
    x, cot, taps, bias, noise, packed,
    stack, stack_g, bands, x_b, h_b, eo_b, ei_b, slope_in, slope_out, g_b, back_b, up_b,
    row_b, g_out, g_in, cols_m, tall_x, tall_e, grid_a, bias_acc,
    x_send, x_recv, c_send, c_recv, g_send, g_recv,
):
    section = lax.axis_index("section")
    strip = lax.axis_index("strip")
    strips = lax.axis_size("strip")
    below = lax.rem(strip + 1, strips)
    above = lax.rem(strip + strips - 1, strips)
    coarser = lax.rem(section + 1, SECTIONS)
    finer = lax.rem(section + SECTIONS - 1, SECTIONS)

    barrier = pltpu.get_barrier_semaphore()
    for peer in ((section, below), (section, above), (coarser, strip), (finer, strip)):
        pl.semaphore_signal(barrier, inc=1, device_id=peer, device_id_type=MESH)
    pl.semaphore_wait(barrier, 4)

    def remote(src_ref, dst_ref, send, recv, peer):
        return pltpu.make_async_remote_copy(
            src_ref=src_ref,
            dst_ref=dst_ref,
            send_sem=send,
            recv_sem=recv,
            device_id=peer,
            device_id_type=MESH,
        )

    first = PLANS[0]["first"]
    for level in range(1, SECTIONS):
        first = jnp.where(section >= level, PLANS[level]["first"], first)
    x_down = remote(
        x.at[pl.ds(pl.multiple_of(first, 16), BLOCK)],
        stack.at[pl.ds(0, BLOCK)],
        x_send.at[0],
        x_recv.at[0],
        (section, below),
    )
    x_up = remote(
        x.at[pl.ds(0, BLOCK)],
        stack.at[pl.ds(BLOCK + ROWS, BLOCK)],
        x_send.at[1],
        x_recv.at[1],
        (section, above),
    )
    c_down = remote(
        cot.at[pl.ds(ROWS - NARROW, NARROW)],
        stack_g.at[pl.ds(0, NARROW)],
        c_send.at[0],
        c_recv.at[0],
        (section, below),
    )
    c_up = remote(
        cot.at[pl.ds(0, NARROW)],
        stack_g.at[pl.ds(NARROW + ROWS, NARROW)],
        c_send.at[1],
        c_recv.at[1],
        (section, above),
    )
    x_down.start()
    x_up.start()

    @pl.when(section == 0)
    def _():
        c_down.start()
        c_up.start()

    stack[BLOCK : BLOCK + ROWS, :] = x[...]
    stack_g[NARROW : NARROW + ROWS, :] = cot[...]
    bands[...] = jnp.zeros_like(bands)
    for which in range(4):
        for dy in range(3):
            for half in range(2):
                bands[
                    which,
                    SIDE * half + CH : SIDE * half + CH + 4 * CH,
                    GROUP * dy + SIDE * half : GROUP * dy + SIDE * half + SIDE,
                ] = taps[which, dy]

    def hop(level):
        tall = PLANS[level]["tall"]
        width = PLANS[level]["groups"] * GROUP
        part = (pl.ds(0, tall), pl.ds(0, width))
        return g_out.at[part], g_in.at[part], g_send, g_recv

    def run_section(level):
        plan = PLANS[level]
        rows, cols, lead, tall = plan["rows"], plan["cols"], plan["lead"], plan["tall"]
        groups = plan["groups"]
        image = iota((tall, GROUP), 0) - lead
        keep_rows = ((image >= 0) | (strip > 0)) & ((image < rows) | (strip < strips - 1))
        inner_rows = (image >= 0) & (image < rows)
        lane = iota((tall, GROUP), 1)

        def live(group):
            return lane + group * GROUP < cols * CH

        def put(ref, group, value):
            ref[0:tall, lanes(SIDE + group * GROUP, GROUP)] = value.astype(jnp.bfloat16)

        for ref in (x_b, h_b, eo_b, ei_b):
            zero = jnp.zeros((tall, SIDE), jnp.bfloat16)
            ref[0:tall, 0:SIDE] = zero
            ref[0:tall, SIDE + groups * GROUP : 2 * SIDE + groups * GROUP] = zero

        if level + 1 < SECTIONS:
            table = column_weights(level)
            across = iota((CH, SIDE), 1) - iota((CH, SIDE), 0)
            for group, start in enumerate(column_windows(level)):
                for fine in range(8):
                    for half in range(2):
                        coarse = 4 * group + 2 * half
                        low = table.get((start + fine, coarse), 0.0)
                        high = table.get((start + fine, coarse + 1), 0.0)
                        block = jnp.where(across == 0, low, 0.0) + jnp.where(
                            across == CH, high, 0.0
                        )
                        cols_m[
                            group,
                            CH * fine : CH * fine + CH,
                            SIDE * half : SIDE * half + SIDE,
                        ] = block.astype(jnp.bfloat16)

        def conv(ref, which, group):
            window = ref[0:tall, lanes(group * GROUP, 2 * GROUP)]
            three = mat(window, bands[which])
            return (
                pltpu.roll(three[:, :GROUP], 1, 0)
                + three[:, GROUP : 2 * GROUP]
                + pltpu.roll(three[:, 2 * GROUP :], tall - 1, 0)
            )

        x_down.wait_recv()
        x_up.wait_recv()
        span = 2 * BLOCK + ROWS
        at = iota((tall, span), 0) - lead
        slot = iota((tall, span), 1)
        want = jnp.where(
            at < 0,
            at + rows - plan["first"],
            jnp.where(at < rows, at + BLOCK, at - rows + BLOCK + ROWS),
        )
        near = (at >= -plan["halo"]) & (at < rows + plan["halo"])
        near = near & ((at >= 0) | (strip > 0)) & ((at < rows) | (strip < strips - 1))
        pick = one_hot((slot == want) & near)

        def load_x(group):
            value = mat(pick, stack[:, lanes(group * GROUP, GROUP)])
            put(x_b, group, jnp.where(live(group), value, 0.0))

        each_group(groups, load_x)

        def forward_in(group):
            value = conv(x_b, 0, group) + bias[0:1, :]
            small = jnp.exp(-jnp.abs(value))
            soft = jnp.maximum(value, 0.0) + jnp.log1p(small)
            sigmoid = jnp.where(value >= 0.0, 1.0, small) / (1.0 + small)
            hidden = LEAK * value + (1.0 - LEAK) * soft
            keep = keep_rows & live(group)
            put(h_b, group, jnp.where(keep, hidden, 0.0))
            slope = jnp.where(keep, LEAK + (1.0 - LEAK) * sigmoid, 0.0)
            slope_in[0:tall, lanes(group * GROUP, GROUP)] = slope

        each_group(groups, forward_in)

        def forward_out(group):
            value = conv(h_b, 1, group) + bias[1:2, :]
            small = jnp.exp(-jnp.abs(value))
            sigmoid = jnp.where(value >= 0.0, 1.0, small) / (1.0 + small)
            slope = jnp.where(live(group), LEAK + (1.0 - LEAK) * sigmoid, 0.0)
            slope_out[0:tall, lanes(group * GROUP, GROUP)] = slope

        each_group(groups, forward_out)

        if level == 0:
            c_down.wait_recv()
            c_up.wait_recv()
            span_g = 2 * NARROW + ROWS
            at_g = iota((tall, span_g), 0) - lead
            near_g = ((at_g >= 0) | (strip > 0)) & ((at_g < rows) | (strip < strips - 1))
            pick_g = one_hot((iota((tall, span_g), 1) == at_g + NARROW) & near_g)

            def load_g(group):
                span_lanes = lanes(group * GROUP, GROUP)
                g_b[0:tall, span_lanes] = mat(pick_g, stack_g[:, span_lanes])

            each_group(groups, load_g)
        else:
            remote(*hop(level), (finer, strip)).wait_recv()

            def load_g(group):
                span_lanes = lanes(group * GROUP, GROUP)
                g_b[0:tall, span_lanes] = g_in[0:tall, span_lanes].astype(jnp.float32)

            each_group(groups, load_g)

        def error_out(group):
            span_lanes = lanes(group * GROUP, GROUP)
            put(eo_b, group, g_b[0:tall, span_lanes] * slope_out[0:tall, span_lanes])

        each_group(groups, error_out)

        def error_in(group):
            value = conv(eo_b, 2, group)
            put(ei_b, group, value * slope_in[0:tall, lanes(group * GROUP, GROUP)])

        each_group(groups, error_in)

        def back_input(group):
            span_lanes = lanes(group * GROUP, GROUP)
            value = jnp.where(live(group), conv(ei_b, 3, group), 0.0)
            back_b[0:tall, span_lanes] = value.astype(jnp.bfloat16)
            total = g_b[0:tall, span_lanes] + value
            up_b[0:tall, span_lanes] = total.astype(jnp.bfloat16)

        each_group(groups, back_input)

        if level + 1 < SECTIONS:
            after = PLANS[level + 1]
            shape = (after["tall"], tall)
            coarse_row = strip * after["rows"] + iota(shape, 0) - after["lead"]
            local_row = iota(shape, 1) - lead
            fine_row = strip * rows + local_row
            num = jnp.maximum(6 * fine_row - 1, 0)
            low = num >> 3
            frac = (num & 7).astype(jnp.float32) * 0.125
            high = jnp.minimum(low + 1, strips * after["rows"] - 1)
            real = (fine_row >= 0) & (fine_row < strips * rows)
            real = real & (local_row >= -plan["reach"]) & (local_row < rows + plan["reach"])
            real = real & (coarse_row >= 0) & (coarse_row < strips * after["rows"])
            row_m = jnp.where(coarse_row == low, 1.0 - frac, 0.0)
            row_m = row_m + jnp.where(coarse_row == high, frac, 0.0)
            row_m = jnp.where(real, row_m, 0.0).astype(jnp.bfloat16)

            def rows_down(group):
                span_lanes = lanes(group * GROUP, GROUP)
                value = mat(row_m, up_b[0:tall, span_lanes])
                row_b[0 : after["tall"], span_lanes] = value.astype(jnp.bfloat16)

            each_group(groups, rows_down)
            for group, start in enumerate(column_windows(level)):
                value = mat(
                    row_b[0 : after["tall"], CH * start : CH * start + 2 * GROUP],
                    cols_m[group],
                )
                g_out[0 : after["tall"], GROUP * group : GROUP * group + GROUP] = value.astype(
                    jnp.bfloat16
                )
            remote(*hop(level + 1), (coarser, strip)).start()

        choose = one_hot(
            (iota((ROWS, tall), 1) == iota((ROWS, tall), 0) + lead)
            & (iota((ROWS, tall), 0) < rows)
        )

        def save(group):
            span_lanes = lanes(group * GROUP, GROUP)
            noise[:, span_lanes] = mat(choose, back_b[0:tall, span_lanes]).astype(jnp.bfloat16)

        each_group(groups, save)
        if groups * GROUP < COLS * CH:
            noise[:, groups * GROUP :] = jnp.zeros(
                (ROWS, COLS * CH - groups * GROUP), jnp.bfloat16
            )

        for which, (field, error) in enumerate(((x_b, ei_b), (h_b, eo_b))):
            bias_acc[which : which + 1, :] = jnp.zeros((1, GROUP), jnp.float32)

            def pile(group):
                where_rows = pl.ds(pl.multiple_of(group * tall, 16), tall)
                tall_x[where_rows, :] = field[0:tall, lanes(group * GROUP, 2 * GROUP)]
                value = error[0:tall, lanes(SIDE + group * GROUP, GROUP)].astype(jnp.float32)
                value = jnp.where(inner_rows, value, 0.0)
                bias_acc[which : which + 1, :] += jnp.sum(value, axis=0, keepdims=True)
                tall_e[where_rows, 0:GROUP] = pltpu.roll(value, tall - 1, 0).astype(jnp.bfloat16)
                tall_e[where_rows, GROUP : 2 * GROUP] = value.astype(jnp.bfloat16)
                tall_e[where_rows, 2 * GROUP :] = pltpu.roll(value, 1, 0).astype(jnp.bfloat16)

            each_group(groups, pile)
            grid_a[which] = lax.dot_general(
                tall_x[0 : groups * tall, :],
                tall_e[0 : groups * tall, :],
                (((0,), (0,)), ((), ())),
                preferred_element_type=jnp.float32,
            )

    for level in range(SECTIONS):
        pl.when(section == level)(functools.partial(run_section, level))

    def folded(which, tap):
        dy, dx = tap // 3, tap % 3
        low, high = 0.0, 0.0
        for half in range(2):
            span_lanes = slice(GROUP * dy + SIDE * half, GROUP * dy + SIDE * half + SIDE)
            row = CH * (2 * half + dx + 1)
            low = low + grid_a[which, row : row + CH, span_lanes]
            high = high + grid_a[which, row + CH : row + 2 * CH, span_lanes]
        return low, high

    left = iota((CH, SIDE), 1) < CH
    for pair in range(9):
        low_a, high_a = folded((2 * pair) // 9, (2 * pair) % 9)
        low_b, high_b = folded((2 * pair + 1) // 9, (2 * pair + 1) % 9)
        packed[CH * pair : CH * pair + CH, :] = jnp.where(
            left, low_a + pltpu.roll(high_a, CH, 1), high_b + pltpu.roll(low_b, CH, 1)
        )
    sums = bias_acc[:, 0:SIDE] + bias_acc[:, SIDE:]
    sums = sums + pltpu.roll(sums, CH, 1)
    tail = jnp.where(iota((8, SIDE), 1) < CH, sums[0:1, :], sums[1:2, :])
    packed[9 * CH : 9 * CH + 8, :] = jnp.where(iota((8, SIDE), 0) == 0, tail, 0.0)
    packed[9 * CH + 8 :, :] = jnp.zeros((PACKED - 9 * CH - 8, SIDE), jnp.float32)

    x_down.wait_send()
    x_up.wait_send()

    @pl.when(section == 0)
    def _():
        c_down.wait_send()
        c_up.wait_send()

    for level in range(1, SECTIONS):

        @pl.when(section == level - 1)
        def _():
            remote(*hop(level), (coarser, strip)).wait_send()


def chain(x, cot, taps, bias):
    dma = pltpu.SemaphoreType.DMA
    half, full = jnp.bfloat16, jnp.float32
    padded = WIDE + 2 * SIDE
    in_vmem = pl.BlockSpec(memory_space=pltpu.VMEM)
    return pl.pallas_call(
        chain_body,
        out_shape=(
            jax.ShapeDtypeStruct((ROWS, COLS * CH), half),
            jax.ShapeDtypeStruct((PACKED, 128), full),
        ),
        in_specs=[in_vmem] * 4,
        out_specs=(in_vmem, in_vmem),
        scratch_shapes=[
            pltpu.VMEM((2 * BLOCK + ROWS, COLS * CH), half),
            pltpu.VMEM((2 * NARROW + ROWS, COLS * CH), half),
            pltpu.VMEM((4, 2 * GROUP, 3 * GROUP), half),
            pltpu.VMEM((TALL, padded), half),
            pltpu.VMEM((TALL, padded), half),
            pltpu.VMEM((TALL, padded), half),
            pltpu.VMEM((TALL, padded), half),
            pltpu.VMEM((TALL, WIDE), full),
            pltpu.VMEM((TALL, WIDE), full),
            pltpu.VMEM((TALL, WIDE), full),
            pltpu.VMEM((TALL, WIDE), half),
            pltpu.VMEM((TALL, WIDE), half),
            pltpu.VMEM((NEXT_TALL, WIDE), half),
            pltpu.VMEM((NEXT_TALL, NEXT_WIDE), half),
            pltpu.VMEM((NEXT_TALL, NEXT_WIDE), half),
            pltpu.VMEM((NEXT_WIDE // GROUP, 2 * GROUP, GROUP), half),
            pltpu.VMEM((DEEP, 2 * GROUP), half),
            pltpu.VMEM((DEEP, 3 * GROUP), half),
            pltpu.VMEM((2, 2 * GROUP, 3 * GROUP), full),
            pltpu.VMEM((2, GROUP), full),
            dma((2,)), dma((2,)), dma((2,)), dma((2,)), dma, dma,
        ],
        compiler_params=pltpu.CompilerParams(
            collective_id=0, has_side_effects=True, vmem_limit_bytes=48 << 20
        ),
    )(x, cot, taps, bias)


def flipped(kernel):
    return jnp.transpose(kernel[::-1, ::-1], (0, 1, 3, 2))


def local(cotangent, activations, weights, biases):
    section = lax.axis_index("section")
    strips = lax.axis_size("strip")
    kernel_in, kernel_out = weights[0, 0], weights[0, 1]
    taps = jnp.stack([kernel_in, kernel_out, flipped(kernel_out), flipped(kernel_in)])
    taps = taps.reshape(4, 3, 3 * CH, CH)
    edge = ((0, 0), (0, 0))
    taps = jnp.concatenate(
        [
            jnp.pad(taps, edge + ((0, CH), (0, 0))),
            jnp.pad(taps, edge + ((CH, 0), (0, 0))),
        ],
        axis=-1,
    )
    bias = jnp.tile(biases[0], (1, 4))
    noise, packed = chain(activations[0, 0], cotangent[0], taps, bias)
    total = strip_sum(packed)
    scales = jnp.array(
        [1.0 / math.sqrt(strips * plan["rows"] * plan["cols"]) for plan in PLANS], jnp.float32
    )
    total = total * scales[section]
    kernel_grads = total[: 9 * CH].reshape(9, CH, 2, CH).transpose(0, 2, 1, 3)
    return (
        noise[None, None],
        kernel_grads.reshape(1, 2, 3, 3, CH, CH),
        total[9 * CH].reshape(1, 2, CH),
    )

def solution(mesh):
    return jax.shard_map(
        local,
        mesh=mesh,
        in_specs=(
            P(None, "strip", None),
            P("section", None, "strip", None),
            P("section", None, None, None, None, None),
            P("section", None, None),
        ),
        out_specs=(
            P("section", None, "strip", None),
            P("section", None, None, None, None, None),
            P("section", None, None),
        ),
        check_vma=False,
    )
```

time: 414 us -> 89.3 us (0.22)
  starting transfers between devices: 141 us -> 0 us
  matrix products: 48.6 us -> 0 us
  waiting for transfers between devices: 48.2 us -> 0 us
  local copies, waits for them, and re-layouts: 49.7 us -> 7.34 us
  other arithmetic: 42.6 us -> 2.27 us
  Pallas kernels: 68.5 us -> 78.7 us
  between operations: 10 us -> 0.73 us
    ppermute x48 -> x0, starting transfers between devices: 141 us -> none  [the longest x22 93.1 us: extended_2(): lax.ppermute(tail, axis, [(i, (i + 1) % count) for i in range(ends)])]
    ppermute x48 -> x0, waiting for transfers between devices: 48.2 us -> none  [the longest x4 42.4 us: shifted_2(): return lax.ppermute(x, axis, pairs)]
    pallas_call x0 -> x1, Pallas kernels: none -> 43 us  [chain(): pl.pallas_call(chain_body, out_shape=(jax.ShapeDtypeStruct((ROWS, COLS *...]
    pallas_call x1, Pallas kernels: 68.5 us -> 35.7 us  [strip_sum(): pl.pallas_call(reduce_body, out_shape=jax.ShapeDtypeStruct((PACKED, 128),...]
    dot_general x80 -> x0, matrix products: 28.2 us -> none  [the longest x72 22.9 us: weight_taps(): lax.dot_general(window, error, (((0, 1, 2), (0, 1, 2)), ((), ())), prefer...]
    conv_general_dilated x10 -> x0, matrix products: 20.3 us -> none  [conv_rows(): lax.conv_general_dilated(field_in, kernel, (1, 1), ((0, 0), (1, 1)), dime...]
    while x104 -> x0, local copies, waits for them, and re-layouts: 16.4 us -> none
    dynamic_update_slice x28 -> x0, local copies, waits for them, and re-layouts: 12.6 us -> none  [attach(): lax.dynamic_update_slice_in_dim(joined, lower_rows, live_rows + rim_depth...]
  transfers between devices with their start and end apart: 48 -> 0, of which waited for: 11 -> 0; matrix products, arithmetic and copies ran while one was open for 12% -> 0% of each run, Pallas kernels for 0% -> 0%
where the time goes in v2:
time: 89.3 us; the launch traced here: 89 us
  Pallas kernels  78.7 us (88%)
  local copies, waits for them, and re-layouts  7.34 us (8%)
  other arithmetic  2.27 us (3%)
    pallas_call x1, Pallas kernels, chain(): pl.pallas_call(chain_body, out_shape=(jax.ShapeDtypeStruct((ROWS, COLS *...  43 us
    pallas_call x1, Pallas kernels, strip_sum(): pl.pallas_call(reduce_body, out_shape=jax.ShapeDtypeStruct((PACKED, 128),...  35.7 us
    unnamed x7, local copies, waits for them, and re-layouts  1.97 us

profile of v2, /device:TPU:7, one launch (start us, length us, event | category | flops | bytes accessed | tf_op | source)
XLA Modules:
  0.0 89.0 jit_solution(611213503178723317)
XLA Ops:
  0.6 1.2 %dynamic_slice.3 = f32[1]{0:T(128)} dynamic-slice(f32[4]{0:T(128)} %constant.14.clone, s32[]{:T(128)S(6)} %select_n.3), dynamic_slice_sizes={1} | dynamic-slice | bytes 12 | tf_op jit(solution)/shard_map/dynamic_slice | solution.py:651
  1.9 0.7 tile.11
  2.6 0.1 tile.12.bias
  2.6 1.1 %fusion.3 = (bf16[1,1,3,3,64,64]{5,4,3,2,1,0:T(8,128)(2,1)S(1)}, bf16[3,3,64,64]{3,2,1,0:T(8,128)(2,1)S(1)}, bf16[3,3,64,64]{3,2,1,0:T(8,128)(2,1)S(1)}, bf16[1,1,3,3,64,64]{5,4,3,2,1,0:T(8,128)(2,1)S(1)}) fusion(bf16[1,2,3,3,64,64]{5,4,3,2,1,0:T(8,128)(2,1)} %param.7), kind=kLoop, calls=%fused_computation.12 | loop fusion | bytes 442368 | tf_op jit(solution)/shard_map/slice | solution.py:634
  3.8 0.2 copy.9
  3.9 0.2 copy.8
  4.1 0.2 pad_maximum_fusion
  4.3 0.0 copy-start.1
  4.3 0.0 copy-start.2
  4.3 0.5 fusion.2.taps
  4.8 0.5 copy-done.1
  5.2 0.1 copy-done.2
  5.3 43.0 %shard_map.76 = (bf16[64,2048]{1,0:T(8,128)(2,1)S(1)}, f32[640,128]{1,0:T(8,128)S(1)}) custom-call(bf16[64,2048]{1,0:T(8,128)(2,1)S(1)} %bitcast.19, bf16[64,2048]{1,0:T(8,128)(2,1)S(1)} %bitcast.20, bf16[4,3,256,128]{3,2,1,0:T(8,128)(2,1)S(1)} %fusion.2.taps, f32[2,256]{1,0:T(2,128)S(1)} %tile.12.bias), custom_call_target="tpu_custom_call" | custom-call | tf_op jit(solution)/shard_map/pallas_call | solution.py:590
  48.3 0.0 copy-start
  48.3 0.7 copy-done
  49.0 35.7 %shard_map.77 = f32[640,128]{1,0:T(8,128)} custom-call(f32[640,128]{1,0:T(8,128)} %copy-done), custom_call_target="tpu_custom_call" | custom-call | tf_op jit(solution)/shard_map/pallas_call | solution.py:135
  84.7 1.6 %broadcast_multiply_fusion = f32[640,128]{1,0:T(8,128)S(1)} fusion(f32[640,128]{1,0:T(8,128)} %shard_map.77, f32[]{:T(128)} %bitcast.12), kind=kLoop, calls=%fused_computation.6 | loop fusion | flops 81920 | bytes 655364 | tf_op jit(solution)/shard_map/mul | solution.py:651
  86.4 0.6 reshape_squeeze.3
  87.1 0.4 reshape.25
  87.4 0.9 copy.10
  88.3 0.7 copy.12
  (3 shorter events, 0.1 us)
Async XLA Ops:
  4.3 1.0 %copy-start.1 = (bf16[1,1,64,2048]{3,2,1,0:T(8,128)(2,1)S(1)}, bf16[1,1,64,2048]{3,2,1,0:T(8,128)(2,1)}, u32[]{:S(2)}) copy-start(bf16[1,1,64,2048]{3,2,1,0:T(8,128)(2,1)} %param.6) | copy-start | bytes 786436
  4.3 1.0 %copy-start.2 = (bf16[1,64,2048]{2,1,0:T(8,128)(2,1)S(1)}, bf16[1,64,2048]{2,1,0:T(8,128)(2,1)}, u32[]{:S(2)}) copy-start(bf16[1,64,2048]{2,1,0:T(8,128)(2,1)} %param.5) | copy-start | bytes 786436
  48.3 0.7 copy-start

commit v3 on v2

v3 whole, which is shorter than its diff:
```python
import math

import jax
import jax.numpy as jnp
from jax import lax
from jax.experimental import pallas as pl
from jax.experimental.pallas import tpu as pltpu
from jax.sharding import PartitionSpec as P

LEAK = 0.05
RING = 8
PIECE = 40
PIECES = 2 * RING
MESH = pl.DeviceIdType.MESH


def sum_peers(strip):
    core = lax.rem(strip, 2)
    row = lax.rem(lax.div(strip, 2), RING)
    deep = lax.div(strip, 2 * RING)
    partner = strip + 1 - 2 * core
    along_y = [(deep * RING + lax.rem(row + step, RING)) * 2 + core for step in range(1, RING)]
    along_z = [(lax.rem(deep + step, RING) * RING + row) * 2 + core for step in range(1, RING)]
    return core, row, deep, partner, along_y, along_z


def strip_sum(
    remote, strip, scale, meanwhile, src, pair_in, y_sum, y_out, y_in, z_out, z_in, gathered,
    pair_send, pair_recv, y_send, y_recv, z_send, z_recv, g_send, g_recv, p_send, p_recv,
):
    core, row, deep, partner, along_y, along_z = sum_peers(strip)
    mine = core * RING
    swap = remote(
        src.at[pl.ds((1 - core) * RING, RING)], pair_in, pair_send, pair_recv, partner
    )
    swap.start()
    swap.wait()
    both = src[pl.ds(mine, RING)] + pair_in[...]
    y_sum[...] = both
    y_out[...] = both.astype(jnp.bfloat16)
    scatter = []
    for step in range(1, RING):
        copy = remote(
            y_out.at[lax.rem(row + step, RING)],
            y_in.at[step - 1],
            y_send.at[step - 1],
            y_recv.at[step - 1],
            along_y[step - 1],
        )
        copy.start()
        scatter.append(copy)
    meanwhile()
    total = y_sum[row]
    for step in range(1, RING):
        scatter[step - 1].wait_recv()
        total = total + y_in[step - 1].astype(jnp.float32)
    z_out[...] = total.astype(jnp.bfloat16)
    z_in[deep] = total.astype(jnp.bfloat16)
    trade = []
    for step in range(1, RING):
        copy = remote(
            z_out, z_in.at[deep], z_send.at[step - 1], z_recv.at[step - 1], along_z[step - 1]
        )
        copy.start()
        trade.append(copy)
    for copy in trade:
        copy.wait_recv()
    total = z_in[0].astype(jnp.float32)
    for index in range(1, RING):
        total = total + z_in[index].astype(jnp.float32)
    own = mine + row
    gathered[own] = (total * scale).astype(jnp.bfloat16)
    gather = []
    for step in range(1, RING):
        copy = remote(
            gathered.at[own],
            gathered.at[own],
            g_send.at[step - 1],
            g_recv.at[step - 1],
            along_y[step - 1],
        )
        copy.start()
        gather.append(copy)
    passed = [
        remote(gathered.at[own], gathered.at[own], p_send.at[0], p_recv.at[0], partner)
    ]
    passed[0].start()
    for step in range(1, RING):
        gather[step - 1].wait_recv()
        came = mine + lax.rem(row + RING - step, RING)
        copy = remote(
            gathered.at[came], gathered.at[came], p_send.at[step], p_recv.at[step], partner
        )
        copy.start()
        passed.append(copy)
    for copy in passed:
        copy.wait_recv()
    for copy in scatter + trade + gather + passed:
        copy.wait_send()


SECTIONS = 4
ROWS = 64
COLS = 32
CH = 64
GROUP = 4 * CH
SIDE = 2 * CH
BLOCK = 32
NARROW = 16
CHUNKS = (4, 3, 5, 4)


def plans():
    reach = [0] * SECTIONS
    for level in reversed(range(SECTIONS - 1)):
        reach[level] = (8 * (reach[level + 1] + 2) + 7) // 6
    result = []
    for level in range(SECTIONS):
        rows = ROWS * 3**level // 4**level
        cols = COLS * 3**level // 4**level
        halo = reach[level] + 4
        lead = halo
        tall = -(-(lead + rows + halo) // 16) * 16
        first = max(0, (rows - halo) // 16 * 16)
        first = min(first, ROWS - BLOCK)
        if rows - first > BLOCK:
            first += 16
        result.append(
            dict(
                rows=rows,
                cols=cols,
                reach=reach[level],
                halo=halo,
                lead=lead,
                tall=tall,
                groups=-(-cols // 4),
                first=first,
                sent=-(-(lead + rows + reach[level] + 2) // 8) * 8,
                chunk=CHUNKS[level],
            )
        )
    return result


PLANS = plans()
TALL = max(plan["tall"] for plan in PLANS)
WIDE = max(plan["groups"] for plan in PLANS) * GROUP
NEXT_TALL = max(plan["tall"] for plan in PLANS[1:])
NEXT_WIDE = max(plan["groups"] for plan in PLANS[1:]) * GROUP
DEEP = max(plan["tall"] * plan["groups"] for plan in PLANS)


def column_weights(level):
    fine, coarse = PLANS[level]["cols"], PLANS[level + 1]["cols"]
    table = {}
    for col in range(fine):
        num = max((2 * col + 1) * coarse - fine, 0)
        low = num // (2 * fine)
        frac = (num - 2 * fine * low) / (2 * fine)
        high = min(low + 1, coarse - 1)
        table[col, low] = table.get((col, low), 0.0) + 1.0 - frac
        table[col, high] = table.get((col, high), 0.0) + frac
    return {key: value for key, value in table.items() if value != 0.0}


def column_windows(level):
    table = column_weights(level)
    limit = PLANS[level]["groups"] * 4 - 8
    starts = []
    for group in range(PLANS[level + 1]["groups"]):
        used = [fine for fine, coarse in table if coarse // 4 == group]
        start = min(min(used) // 2 * 2, limit)
        assert max(used) < start + 8
        starts.append(start)
    return starts


def iota(shape, axis):
    return lax.broadcasted_iota(jnp.int32, shape, axis)


def mat(left, right):
    return jnp.dot(left, right, preferred_element_type=jnp.float32)


def one_hot(cond):
    return jnp.where(cond, 1.0, 0.0).astype(jnp.bfloat16)


def each_group(count, body, step):
    def run(index, carry):
        body([index * step + extra for extra in range(step)])
        return carry

    if step == count:
        body(list(range(count)))
    else:
        lax.fori_loop(0, count // step, run, 0)


def lanes(start, size):
    if isinstance(start, int):
        return pl.ds(start, size)
    return pl.ds(pl.multiple_of(start, 128), size)


def chain_body(
    x, cot, taps, bias, noise, kernel_out, bias_out,
    stack, stack_g, bands, x_b, h_b, eo_b, ei_b, slope_in, slope_out, g_b, back_b, up_b,
    row_b, g_out, g_in, cols_m, tall_x, tall_e, grid_a, bias_acc,
    packed, final, x_send, x_recv, c_send, c_recv, g_send, g_recv, *sum_refs,
):
    section = lax.axis_index("section")
    strip = lax.axis_index("strip")
    strips = lax.axis_size("strip")
    below = lax.rem(strip + 1, strips)
    above = lax.rem(strip + strips - 1, strips)
    coarser = lax.rem(section + 1, SECTIONS)
    finer = lax.rem(section + SECTIONS - 1, SECTIONS)

    barrier = pltpu.get_barrier_semaphore()
    partner, along_y, along_z = sum_peers(strip)[3:]
    peers = [(section, below), (section, above), (coarser, strip), (finer, strip)]
    peers += [(section, peer) for peer in [partner] + along_y + along_z]
    for peer in peers:
        pl.semaphore_signal(barrier, inc=1, device_id=peer, device_id_type=MESH)
    pl.semaphore_wait(barrier, len(peers))

    def remote(src_ref, dst_ref, send, recv, peer):
        return pltpu.make_async_remote_copy(
            src_ref=src_ref,
            dst_ref=dst_ref,
            send_sem=send,
            recv_sem=recv,
            device_id=peer,
            device_id_type=MESH,
        )

    first = PLANS[0]["first"]
    for level in range(1, SECTIONS):
        first = jnp.where(section >= level, PLANS[level]["first"], first)
    x_down = remote(
        x.at[pl.ds(pl.multiple_of(first, 16), BLOCK)],
        stack.at[pl.ds(0, BLOCK)],
        x_send.at[0],
        x_recv.at[0],
        (section, below),
    )
    x_up = remote(
        x.at[pl.ds(0, BLOCK)],
        stack.at[pl.ds(BLOCK + ROWS, BLOCK)],
        x_send.at[1],
        x_recv.at[1],
        (section, above),
    )
    c_down = remote(
        cot.at[pl.ds(ROWS - NARROW, NARROW)],
        stack_g.at[pl.ds(0, NARROW)],
        c_send.at[0],
        c_recv.at[0],
        (section, below),
    )
    c_up = remote(
        cot.at[pl.ds(0, NARROW)],
        stack_g.at[pl.ds(NARROW + ROWS, NARROW)],
        c_send.at[1],
        c_recv.at[1],
        (section, above),
    )
    x_down.start()
    x_up.start()

    @pl.when(section == 0)
    def _():
        c_down.start()
        c_up.start()

    stack[BLOCK : BLOCK + ROWS, :] = x[...]
    stack_g[NARROW : NARROW + ROWS, :] = cot[...]
    bands[...] = jnp.zeros_like(bands)
    for which in range(4):
        for dy in range(3):
            for half in range(2):
                bands[
                    which,
                    SIDE * half + CH : SIDE * half + CH + 4 * CH,
                    GROUP * dy + SIDE * half : GROUP * dy + SIDE * half + SIDE,
                ] = taps[which, dy]

    bias_rows = jnp.concatenate([bias[...]] * 4, axis=1)

    def hop(level, group, peer):
        part = (pl.ds(0, PLANS[level]["sent"]), pl.ds(group * GROUP, GROUP))
        return remote(g_out.at[part], g_in.at[part], g_send.at[group], g_recv.at[group], peer)

    def live_of(level, group):
        lane = iota((PLANS[level]["tall"], GROUP), 1)
        return lane + group * GROUP < PLANS[level]["cols"] * CH

    def conv_of(tall, ref, which, group_list):
        windows = [ref[0:tall, lanes(group * GROUP, 2 * GROUP)] for group in group_list]
        three = mat(jnp.concatenate(windows, axis=0), bands[which])
        result = []
        for index in range(len(group_list)):
            part = three[index * tall : (index + 1) * tall]
            result.append(
                pltpu.roll(part[:, :GROUP], 1, 0)
                + part[:, GROUP : 2 * GROUP]
                + pltpu.roll(part[:, 2 * GROUP :], tall - 1, 0)
            )
        return zip(group_list, result)

    def save_noise(level):
        plan = PLANS[level]
        rows, tall, groups = plan["rows"], plan["tall"], plan["groups"]
        shape = (ROWS, tall)
        choose = one_hot(
            (iota(shape, 1) == iota(shape, 0) + plan["lead"]) & (iota(shape, 0) < rows)
        )

        def save(group_list):
            for group in group_list:
                span_lanes = lanes(group * GROUP, GROUP)
                noise[:, span_lanes] = mat(choose, back_b[0:tall, span_lanes]).astype(
                    jnp.bfloat16
                )

        each_group(groups, save, plan["chunk"])
        if groups * GROUP < COLS * CH:
            noise[:, groups * GROUP :] = jnp.zeros(
                (ROWS, COLS * CH - groups * GROUP), jnp.bfloat16
            )

    def finish_last():
        level = SECTIONS - 1
        tall = PLANS[level]["tall"]

        def back_last(group_list):
            for group, value in conv_of(tall, ei_b, 3, group_list):
                value = jnp.where(live_of(level, group), value, 0.0)
                back_b[0:tall, lanes(group * GROUP, GROUP)] = value.astype(jnp.bfloat16)

        each_group(PLANS[level]["groups"], back_last, PLANS[level]["chunk"])
        save_noise(level)

    def run_section(level):
        plan = PLANS[level]
        rows, lead, tall = plan["rows"], plan["lead"], plan["tall"]
        groups, chunk = plan["groups"], plan["chunk"]
        image = iota((tall, GROUP), 0) - lead
        keep_rows = ((image >= 0) | (strip > 0)) & ((image < rows) | (strip < strips - 1))
        inner_rows = (image >= 0) & (image < rows)

        def live(group):
            return live_of(level, group)

        def conv(ref, which, group_list):
            return conv_of(tall, ref, which, group_list)

        def put(ref, group, value):
            ref[0:tall, lanes(SIDE + group * GROUP, GROUP)] = value.astype(jnp.bfloat16)

        for ref in (x_b, h_b, eo_b, ei_b):
            zero = jnp.zeros((tall, SIDE), jnp.bfloat16)
            ref[0:tall, 0:SIDE] = zero
            ref[0:tall, SIDE + groups * GROUP : 2 * SIDE + groups * GROUP] = zero

        if level + 1 < SECTIONS:
            table = column_weights(level)
            across = iota((CH, SIDE), 1) - iota((CH, SIDE), 0)
            for group, start in enumerate(column_windows(level)):
                for fine in range(8):
                    for half in range(2):
                        coarse = 4 * group + 2 * half
                        low = table.get((start + fine, coarse), 0.0)
                        high = table.get((start + fine, coarse + 1), 0.0)
                        block = jnp.where(across == 0, low, 0.0) + jnp.where(
                            across == CH, high, 0.0
                        )
                        cols_m[
                            group,
                            CH * fine : CH * fine + CH,
                            SIDE * half : SIDE * half + SIDE,
                        ] = block.astype(jnp.bfloat16)

        x_down.wait_recv()
        x_up.wait_recv()
        span = 2 * BLOCK + ROWS
        at = iota((tall, span), 0) - lead
        slot = iota((tall, span), 1)
        want = jnp.where(
            at < 0,
            at + rows - plan["first"],
            jnp.where(at < rows, at + BLOCK, at - rows + BLOCK + ROWS),
        )
        near = (at >= -plan["halo"]) & (at < rows + plan["halo"])
        near = near & ((at >= 0) | (strip > 0)) & ((at < rows) | (strip < strips - 1))
        pick = one_hot((slot == want) & near)

        def load_x(group_list):
            for group in group_list:
                value = mat(pick, stack[:, lanes(group * GROUP, GROUP)])
                put(x_b, group, jnp.where(live(group), value, 0.0))

        each_group(groups, load_x, chunk)

        def forward_in(group_list):
            for group, value in conv(x_b, 0, group_list):
                value = value + bias_rows[0:1, :]
                small = jnp.exp(-jnp.abs(value))
                soft = jnp.maximum(value, 0.0) + jnp.log1p(small)
                sigmoid = jnp.where(value >= 0.0, 1.0, small) / (1.0 + small)
                hidden = LEAK * value + (1.0 - LEAK) * soft
                keep = keep_rows & live(group)
                put(h_b, group, jnp.where(keep, hidden, 0.0))
                slope = jnp.where(keep, LEAK + (1.0 - LEAK) * sigmoid, 0.0)
                slope_in[0:tall, lanes(group * GROUP, GROUP)] = slope

        each_group(groups, forward_in, chunk)

        def forward_out(group_list):
            for group, value in conv(h_b, 1, group_list):
                value = value + bias_rows[1:2, :]
                small = jnp.exp(-jnp.abs(value))
                sigmoid = jnp.where(value >= 0.0, 1.0, small) / (1.0 + small)
                slope = jnp.where(live(group), LEAK + (1.0 - LEAK) * sigmoid, 0.0)
                slope_out[0:tall, lanes(group * GROUP, GROUP)] = slope

        each_group(groups, forward_out, chunk)

        if level == 0:
            c_down.wait_recv()
            c_up.wait_recv()
            span_g = 2 * NARROW + ROWS
            at_g = iota((tall, span_g), 0) - lead
            near_g = ((at_g >= 0) | (strip > 0)) & ((at_g < rows) | (strip < strips - 1))
            pick_g = one_hot((iota((tall, span_g), 1) == at_g + NARROW) & near_g)

            def load_g(group_list):
                for group in group_list:
                    span_lanes = lanes(group * GROUP, GROUP)
                    value = mat(pick_g, stack_g[:, span_lanes])
                    g_b[0:tall, span_lanes] = value
                    put(eo_b, group, value * slope_out[0:tall, span_lanes])

            each_group(groups, load_g, chunk)
        else:
            sent = plan["sent"]
            for group in range(groups):
                hop(level, group, (finer, strip)).wait_recv()
                span_lanes = lanes(group * GROUP, GROUP)
                value = g_in[0:sent, span_lanes].astype(jnp.float32)
                if sent < tall:
                    rest = jnp.zeros((tall - sent, GROUP), jnp.float32)
                    value = jnp.concatenate([value, rest], axis=0)
                g_b[0:tall, span_lanes] = value
                put(eo_b, group, value * slope_out[0:tall, span_lanes])

        def error_in(group_list):
            for group, value in conv(eo_b, 2, group_list):
                put(ei_b, group, value * slope_in[0:tall, lanes(group * GROUP, GROUP)])

        each_group(groups, error_in, chunk)

        def back_input(group_list):
            for group, value in conv(ei_b, 3, group_list):
                span_lanes = lanes(group * GROUP, GROUP)
                value = jnp.where(live(group), value, 0.0)
                back_b[0:tall, span_lanes] = value.astype(jnp.bfloat16)
                total = g_b[0:tall, span_lanes] + value
                up_b[0:tall, span_lanes] = total.astype(jnp.bfloat16)

        if level + 1 < SECTIONS:
            after = PLANS[level + 1]
            shape = (after["tall"], tall)
            coarse_row = strip * after["rows"] + iota(shape, 0) - after["lead"]
            local_row = iota(shape, 1) - lead
            fine_row = strip * rows + local_row
            num = jnp.maximum(6 * fine_row - 1, 0)
            low = num >> 3
            frac = (num & 7).astype(jnp.float32) * 0.125
            high = jnp.minimum(low + 1, strips * after["rows"] - 1)
            real = (fine_row >= 0) & (fine_row < strips * rows)
            real = real & (local_row >= -plan["reach"]) & (local_row < rows + plan["reach"])
            real = real & (coarse_row >= 0) & (coarse_row < strips * after["rows"])
            row_m = jnp.where(coarse_row == low, 1.0 - frac, 0.0)
            row_m = row_m + jnp.where(coarse_row == high, frac, 0.0)
            row_m = jnp.where(real, row_m, 0.0).astype(jnp.bfloat16)

            windows = column_windows(level)
            ready = 0
            for begin in range(0, groups, chunk):
                part = list(range(begin, begin + chunk))
                back_input(part)
                for group in part:
                    span_lanes = lanes(group * GROUP, GROUP)
                    value = mat(row_m, up_b[0:tall, span_lanes])
                    row_b[0 : after["tall"], span_lanes] = value.astype(jnp.bfloat16)
                while ready < len(windows) and windows[ready] + 8 <= 4 * (begin + chunk):
                    start = CH * windows[ready]
                    value = mat(
                        row_b[0 : after["tall"], start : start + 2 * GROUP], cols_m[ready]
                    )
                    g_out[0 : after["tall"], GROUP * ready : GROUP * ready + GROUP] = (
                        value.astype(jnp.bfloat16)
                    )
                    hop(level + 1, ready, (coarser, strip)).start()
                    ready += 1
            assert ready == len(windows)

        if level + 1 < SECTIONS:
            save_noise(level)

        for which, (field, error) in enumerate(((x_b, ei_b), (h_b, eo_b))):
            bias_acc[which : which + 1, :] = jnp.zeros((1, GROUP), jnp.float32)

            def pile(group_list):
                for group in group_list:
                    if isinstance(group, int):
                        where_rows = pl.ds(group * tall, tall)
                    else:
                        where_rows = pl.ds(pl.multiple_of(group * tall, 16), tall)
                    tall_x[where_rows, :] = field[0:tall, lanes(group * GROUP, 2 * GROUP)]
                    value = error[0:tall, lanes(SIDE + group * GROUP, GROUP)]
                    value = jnp.where(inner_rows, value.astype(jnp.float32), 0.0)
                    bias_acc[which : which + 1, :] += jnp.sum(value, axis=0, keepdims=True)
                    tall_e[where_rows, 0:GROUP] = pltpu.roll(value, tall - 1, 0).astype(
                        jnp.bfloat16
                    )
                    tall_e[where_rows, GROUP : 2 * GROUP] = value.astype(jnp.bfloat16)
                    tall_e[where_rows, 2 * GROUP :] = pltpu.roll(value, 1, 0).astype(
                        jnp.bfloat16
                    )

            each_group(groups, pile, chunk)
            grid_a[which] = lax.dot_general(
                tall_x[0 : groups * tall, :],
                tall_e[0 : groups * tall, :],
                (((0,), (0,)), ((), ())),
                preferred_element_type=jnp.float32,
            )

    for level in range(SECTIONS):

        @pl.when(section == level)
        def _():
            run_section(level)

    def folded(which, tap):
        dy, dx = tap // 3, tap % 3
        low, high = 0.0, 0.0
        for half in range(2):
            span_lanes = slice(GROUP * dy + SIDE * half, GROUP * dy + SIDE * half + SIDE)
            row = CH * (2 * half + dx + 1)
            low = low + grid_a[which, row : row + CH, span_lanes]
            high = high + grid_a[which, row + CH : row + 2 * CH, span_lanes]
        return low, high

    left = iota((CH, SIDE), 1) < CH
    blocks = []
    for pair in range(9):
        low_a, high_a = folded((2 * pair) // 9, (2 * pair) % 9)
        low_b, high_b = folded((2 * pair + 1) // 9, (2 * pair + 1) % 9)
        blocks.append(
            jnp.where(left, low_a + pltpu.roll(high_a, CH, 1), high_b + pltpu.roll(low_b, CH, 1))
        )
    sums = bias_acc[:, 0:SIDE] + bias_acc[:, SIDE:]
    sums = sums + pltpu.roll(sums, CH, 1)
    tail = jnp.where(iota((8, SIDE), 1) < CH, sums[0:1, :], sums[1:2, :])
    blocks.append(jnp.where(iota((8, SIDE), 0) == 0, tail, 0.0))
    blocks.append(jnp.zeros((PIECES * PIECE - 9 * CH - 8, SIDE), jnp.float32))
    packed[...] = jnp.concatenate(blocks, axis=0).reshape(PIECES, PIECE, SIDE)

    scale = 0.0
    for level, plan in enumerate(PLANS):
        factor = 1.0 / math.sqrt(strips * plan["rows"] * plan["cols"])
        scale = jnp.where(section == level, jnp.float32(factor), scale)

    def meanwhile():
        @pl.when(section == SECTIONS - 1)
        def _():
            finish_last()

    strip_sum(
        lambda a, b, c, d, peer: remote(a, b, c, d, (section, peer)),
        strip,
        scale,
        meanwhile,
        packed,
        *sum_refs,
    )
    gathered = sum_refs[6]
    final[...] = gathered[...].astype(jnp.float32).reshape(PIECES * PIECE, SIDE)
    for pair in range(9):
        block = final[CH * pair : CH * pair + CH, :]
        kernel_out[2 * pair] = block[:, :CH]
        kernel_out[2 * pair + 1] = pltpu.roll(block, CH, 1)[:, :CH]
    sums = final[9 * CH : 9 * CH + 8, :]
    bias_out[0:1, :] = sums[0:1, :CH]
    bias_out[1:2, :] = pltpu.roll(sums, CH, 1)[0:1, :CH]

    x_down.wait_send()
    x_up.wait_send()

    @pl.when(section == 0)
    def _():
        c_down.wait_send()
        c_up.wait_send()

    for level in range(1, SECTIONS):

        @pl.when(section == level - 1)
        def _():
            for group in range(PLANS[level]["groups"]):
                hop(level, group, (coarser, strip)).wait_send()


def chain(x, cot, taps, bias):
    dma = pltpu.SemaphoreType.DMA
    half, full = jnp.bfloat16, jnp.float32
    padded = WIDE + 2 * SIDE
    in_vmem = pl.BlockSpec(memory_space=pltpu.VMEM)
    return pl.pallas_call(
        chain_body,
        out_shape=(
            jax.ShapeDtypeStruct((ROWS, COLS * CH), half),
            jax.ShapeDtypeStruct((18, CH, CH), full),
            jax.ShapeDtypeStruct((2, CH), full),
        ),
        in_specs=[in_vmem] * 4,
        out_specs=(in_vmem, in_vmem, in_vmem),
        scratch_shapes=[
            pltpu.VMEM((2 * BLOCK + ROWS, COLS * CH), half),
            pltpu.VMEM((2 * NARROW + ROWS, COLS * CH), half),
            pltpu.VMEM((4, 2 * GROUP, 3 * GROUP), half),
            pltpu.VMEM((TALL, padded), half),
            pltpu.VMEM((TALL, padded), half),
            pltpu.VMEM((TALL, padded), half),
            pltpu.VMEM((TALL, padded), half),
            pltpu.VMEM((TALL, WIDE), full),
            pltpu.VMEM((TALL, WIDE), full),
            pltpu.VMEM((TALL, WIDE), full),
            pltpu.VMEM((TALL, WIDE), half),
            pltpu.VMEM((TALL, WIDE), half),
            pltpu.VMEM((NEXT_TALL, WIDE), half),
            pltpu.VMEM((NEXT_TALL, NEXT_WIDE), half),
            pltpu.VMEM((NEXT_TALL, NEXT_WIDE), half),
            pltpu.VMEM((NEXT_WIDE // GROUP, 2 * GROUP, GROUP), half),
            pltpu.VMEM((DEEP, 2 * GROUP), half),
            pltpu.VMEM((DEEP, 3 * GROUP), half),
            pltpu.VMEM((2, 2 * GROUP, 3 * GROUP), full),
            pltpu.VMEM((2, GROUP), full),
            pltpu.VMEM((PIECES, PIECE, SIDE), full),
            pltpu.VMEM((PIECES * PIECE, SIDE), full),
            dma((2,)), dma((2,)), dma((2,)), dma((2,)),
            dma((NEXT_WIDE // GROUP,)), dma((NEXT_WIDE // GROUP,)),
            pltpu.VMEM((RING, PIECE, SIDE), full),
            pltpu.VMEM((RING, PIECE, SIDE), full),
            pltpu.VMEM((RING, PIECE, SIDE), half),
            pltpu.VMEM((RING - 1, PIECE, SIDE), half),
            pltpu.VMEM((PIECE, SIDE), half),
            pltpu.VMEM((RING, PIECE, SIDE), half),
            pltpu.VMEM((PIECES, PIECE, SIDE), half),
            dma, dma,
            dma((RING - 1,)), dma((RING - 1,)),
            dma((RING - 1,)), dma((RING - 1,)),
            dma((RING - 1,)), dma((RING - 1,)),
            dma((RING,)), dma((RING,)),
        ],
        compiler_params=pltpu.CompilerParams(
            collective_id=0, has_side_effects=True, vmem_limit_bytes=48 << 20
        ),
    )(x, cot, taps, bias)


def flipped(kernel):
    return jnp.transpose(kernel[::-1, ::-1], (0, 1, 3, 2))


def local(cotangent, activations, weights, biases):
    kernel_in, kernel_out = weights[0, 0], weights[0, 1]
    taps = jnp.stack([kernel_in, kernel_out, flipped(kernel_out), flipped(kernel_in)])
    taps = taps.reshape(4, 3, 3 * CH, CH)
    edge = ((0, 0), (0, 0))
    taps = jnp.concatenate(
        [
            jnp.pad(taps, edge + ((0, CH), (0, 0))),
            jnp.pad(taps, edge + ((CH, 0), (0, 0))),
        ],
        axis=-1,
    )
    noise, kernels, sums = chain(activations[0, 0], cotangent[0], taps, biases[0])
    return (
        noise[None, None],
        kernels.reshape(1, 2, 3, 3, CH, CH),
        sums[None],
    )


def solution(mesh):
    return jax.shard_map(
        local,
        mesh=mesh,
        in_specs=(
            P(None, "strip", None),
            P("section", None, "strip", None),
            P("section", None, None, None, None, None),
            P("section", None, None),
        ),
        out_specs=(
            P("section", None, "strip", None),
            P("section", None, None, None, None, None),
            P("section", None, None),
        ),
        check_vma=False,
    )
```

time: 89.3 us -> 63.9 us (0.72)
  Pallas kernels: 78.7 us -> 58.4 us
  local copies, waits for them, and re-layouts: 7.34 us -> 4.01 us
  other arithmetic: 2.27 us -> 0.63 us
    pallas_call x1 -> x0, Pallas kernels: 35.7 us -> none  [strip_sum(): pl.pallas_call(reduce_body, out_shape=jax.ShapeDtypeStruct((PACKED, 128),...]
    pallas_call x1, Pallas kernels: 43 us -> 58.4 us  [chain(): pl.pallas_call(chain_body, out_shape=(jax.ShapeDtypeStruct((ROWS, COLS *...]
    mul x1 -> x0, other arithmetic: 1.64 us -> none  [local(): total = total * scales[section]]
    another operation x3 -> x0, local copies, waits for them, and re-layouts: 1.41 us -> none  [the longest x2 0.76 us: local(): bias = jnp.tile(biases[0], (1, 4))]
    dynamic_slice x1 -> x0, local copies, waits for them, and re-layouts: 1.24 us -> none  [local(): total = total * scales[section]]
    unnamed x7 -> x9, local copies, waits for them, and re-layouts: 1.97 us -> 2.62 us
where the time goes in v3:
time: 63.9 us; the launch traced here: 63.7 us
  Pallas kernels  58.4 us (91%)
  local copies, waits for them, and re-layouts  4.01 us (6%)
  between operations  0.69 us (1%)
    pallas_call x1, Pallas kernels, chain(): pl.pallas_call(chain_body, out_shape=(jax.ShapeDtypeStruct((ROWS, COLS *...  58.4 us
    unnamed x9, local copies, waits for them, and re-layouts  2.62 us

profile of v3, /device:TPU:7, one launch (start us, length us, event | category | flops | bytes accessed | tf_op | source)
XLA Modules:
  0.0 63.7 jit_solution(6526463542986310308)
XLA Ops:
  0.6 1.1 %fusion.3 = (bf16[1,1,3,3,64,64]{5,4,3,2,1,0:T(8,128)(2,1)S(1)}, bf16[3,3,64,64]{3,2,1,0:T(8,128)(2,1)S(1)}, bf16[3,3,64,64]{3,2,1,0:T(8,128)(2,1)S(1)}, bf16[1,1,3,3,64,64]{5,4,3,2,1,0:T(8,128)(2,1)S(1)}) fusion(bf16[1,2,3,3,64,64]{5,4,3,2,1,0:T(8,128)(2,1)} %param.6), kind=kLoop, calls=%fused_computation.10 | loop fusion | bytes 442368 | tf_op jit(solution)/shard_map/slice | solution.py:681
  1.7 0.1 copy.8
  1.9 0.2 copy.7
  2.0 0.2 pad_maximum_fusion
  2.2 0.0 copy-start
  2.2 0.0 copy-start.1
  2.2 0.0 copy-start.2
  2.2 0.5 fusion.2.taps
  2.7 0.4 copy-done
  3.1 0.1 copy-done.1
  3.2 0.0 copy-done.2
  3.2 58.4 %shard_map.67 = (bf16[64,2048]{1,0:T(8,128)(2,1)S(1)}, f32[18,64,64]{2,1,0:T(8,128)S(1)}, f32[2,64]{1,0:T(2,128)S(1)}) custom-call(bf16[64,2048]{1,0:T(8,128)(2,1)S(1)} %bitcast.20, bf16[64,2048]{1,0:T(8,128)(2,1)S(1)} %bitcast.21, bf16[4,3,256,128]{3,2,1,0:T(8,128)(2,1)S(1)} %fusion.2.taps, f32[2,64]{1,0:T(2,128)S(1)} %bitcast.23), custom_call_target="tpu_custom_call" | custom-call | tf_op jit(solution)/shard_map/pallas_call | solution.py:623
  61.6 0.7 %copy.12 = bf16[1,1,64,2048]{3,2,1,0:T(8,128)(2,1)} copy(bf16[1,1,64,2048]{3,2,1,0:T(8,128)(2,1)S(1)} %bitcast.19) | data formatting | bytes 524288
  62.4 0.8 %copy.13 = f32[1,2,3,3,64,64]{5,4,3,2,1,0:T(8,128)} copy(f32[1,2,3,3,64,64]{5,4,3,2,1,0:T(8,128)S(1)} %bitcast.18) | data formatting | bytes 589824
  63.2 0.6 copy.14
  (1 shorter events, 0.0 us)
Async XLA Ops:
  2.2 1.0 %copy-start = (bf16[1,1,64,2048]{3,2,1,0:T(8,128)(2,1)S(1)}, bf16[1,1,64,2048]{3,2,1,0:T(8,128)(2,1)}, u32[]{:S(2)}) copy-start(bf16[1,1,64,2048]{3,2,1,0:T(8,128)(2,1)} %param.5) | copy-start | bytes 786436
  2.2 1.0 %copy-start.1 = (bf16[1,64,2048]{2,1,0:T(8,128)(2,1)S(1)}, bf16[1,64,2048]{2,1,0:T(8,128)(2,1)}, u32[]{:S(2)}) copy-start(bf16[1,64,2048]{2,1,0:T(8,128)(2,1)} %param.4) | copy-start | bytes 786436
  2.2 1.0 %copy-start.2 = (f32[1,2,64]{2,1,0:T(2,128)S(1)}, f32[1,2,64]{2,1,0:T(2,128)}, u32[]{:S(2)}) copy-start(f32[1,2,64]{2,1,0:T(2,128)} %param.7) | copy-start | bytes 1540

commit v4 on v3

--- a/solution.py
+++ b/solution.py
@@ -108,6 +108,7 @@
 BLOCK = 32
 NARROW = 16
 CHUNKS = (4, 3, 5, 4)
+LAST_CHUNKS = ((4, 2, 2), (3, 3), (5,))
 
 
 def plans():
@@ -137,6 +138,7 @@
                 first=first,
                 sent=-(-(lead + rows + reach[level] + 2) // 8) * 8,
                 chunk=CHUNKS[level],
+                back=-(-(rows + 2 * halo - 2) // 16) * 16,
             )
         )
     return result
@@ -147,7 +149,7 @@
 WIDE = max(plan["groups"] for plan in PLANS) * GROUP
 NEXT_TALL = max(plan["tall"] for plan in PLANS[1:])
 NEXT_WIDE = max(plan["groups"] for plan in PLANS[1:]) * GROUP
-DEEP = max(plan["tall"] * plan["groups"] for plan in PLANS)
+DEEP = max(plan["back"] * plan["groups"] for plan in PLANS)
 
 
 def column_weights(level):
@@ -183,6 +185,11 @@
     return jnp.dot(left, right, preferred_element_type=jnp.float32)
 
 
+def steepness(value):
+    half = 0.5 * (1.0 - LEAK)
+    return (LEAK + half) + half * jnp.tanh(0.5 * value)
+
+
 def one_hot(cond):
     return jnp.where(cond, 1.0, 0.0).astype(jnp.bfloat16)
 
@@ -205,10 +212,10 @@
 
 
 def chain_body(
-    x, cot, taps, bias, noise, kernel_out, bias_out,
+    x, cot, taps, bias, noise, sums_out,
     stack, stack_g, bands, x_b, h_b, eo_b, ei_b, slope_in, slope_out, g_b, back_b, up_b,
     row_b, g_out, g_in, cols_m, tall_x, tall_e, grid_a, bias_acc,
-    packed, final, x_send, x_recv, c_send, c_recv, g_send, g_recv, *sum_refs,
+    packed, x_send, x_recv, c_send, c_recv, g_send, g_recv, *sum_refs,
 ):
     section = lax.axis_index("section")
     strip = lax.axis_index("strip")
@@ -224,6 +231,28 @@
     peers += [(section, peer) for peer in [partner] + along_y + along_z]
     for peer in peers:
         pl.semaphore_signal(barrier, inc=1, device_id=peer, device_id_type=MESH)
+
+    bands[...] = jnp.zeros_like(bands)
+    blank = jnp.zeros((CH, CH), jnp.float32)
+    for which, (source, flip) in enumerate(((0, False), (1, False), (1, True), (0, True))):
+        for dy in range(3):
+            tap_list = []
+            for dx in range(3):
+                at = (2 - dy) * 3 + 2 - dx if flip else dy * 3 + dx
+                tap_list.append(taps[source, at].astype(jnp.float32))
+            tap_list.append(blank)
+            for index in range(4):
+                pair = (tap_list[index], tap_list[index - 1])
+                if flip:
+                    block = jnp.concatenate(pair, axis=0).T
+                else:
+                    block = jnp.concatenate(pair, axis=1)
+                block = block.astype(jnp.bfloat16)
+                for half in range(2):
+                    row = CH * (2 * half + 1 + index)
+                    col = GROUP * dy + SIDE * half
+                    bands[which, row : row + CH, col : col + SIDE] = block
+
     pl.semaphore_wait(barrier, len(peers))
 
     def remote(src_ref, dst_ref, send, recv, peer):
@@ -277,16 +306,6 @@
 
     stack[BLOCK : BLOCK + ROWS, :] = x[...]
     stack_g[NARROW : NARROW + ROWS, :] = cot[...]
-    bands[...] = jnp.zeros_like(bands)
-    for which in range(4):
-        for dy in range(3):
-            for half in range(2):
-                bands[
-                    which,
-                    SIDE * half + CH : SIDE * half + CH + 4 * CH,
-                    GROUP * dy + SIDE * half : GROUP * dy + SIDE * half + SIDE,
-                ] = taps[which, dy]
-
     bias_rows = jnp.concatenate([bias[...]] * 4, axis=1)
 
     def hop(level, group, peer):
@@ -312,8 +331,8 @@
 
     def save_noise(level):
         plan = PLANS[level]
-        rows, tall, groups = plan["rows"], plan["tall"], plan["groups"]
-        shape = (ROWS, tall)
+        rows, back, groups = plan["rows"], plan["back"], plan["groups"]
+        shape = (ROWS, back)
         choose = one_hot(
             (iota(shape, 1) == iota(shape, 0) + plan["lead"]) & (iota(shape, 0) < rows)
         )
@@ -321,7 +340,7 @@
         def save(group_list):
             for group in group_list:
                 span_lanes = lanes(group * GROUP, GROUP)
-                noise[:, span_lanes] = mat(choose, back_b[0:tall, span_lanes]).astype(
+                noise[:, span_lanes] = mat(choose, back_b[0:back, span_lanes]).astype(
                     jnp.bfloat16
                 )
 
@@ -333,12 +352,12 @@
 
     def finish_last():
         level = SECTIONS - 1
-        tall = PLANS[level]["tall"]
+        back = PLANS[level]["back"]
 
         def back_last(group_list):
-            for group, value in conv_of(tall, ei_b, 3, group_list):
-                value = jnp.where(live_of(level, group), value, 0.0)
-                back_b[0:tall, lanes(group * GROUP, GROUP)] = value.astype(jnp.bfloat16)
+            for group, value in conv_of(back, ei_b, 3, group_list):
+                value = jnp.where(live_of(level, group)[:back], value, 0.0)
+                back_b[0:back, lanes(group * GROUP, GROUP)] = value.astype(jnp.bfloat16)
 
         each_group(PLANS[level]["groups"], back_last, PLANS[level]["chunk"])
         save_noise(level)
@@ -346,19 +365,26 @@
     def run_section(level):
         plan = PLANS[level]
         rows, lead, tall = plan["rows"], plan["lead"], plan["tall"]
-        groups, chunk = plan["groups"], plan["chunk"]
+        groups, chunk, back = plan["groups"], plan["chunk"], plan["back"]
         image = iota((tall, GROUP), 0) - lead
         keep_rows = ((image >= 0) | (strip > 0)) & ((image < rows) | (strip < strips - 1))
-        inner_rows = (image >= 0) & (image < rows)
+        inner_rows = (image[:back] >= 0) & (image[:back] < rows)
 
         def live(group):
             return live_of(level, group)
 
+        def live_back(group):
+            return iota((back, GROUP), 1) + group * GROUP < plan["cols"] * CH
+
         def conv(ref, which, group_list):
             return conv_of(tall, ref, which, group_list)
 
+        def conv_back(ref, which, group_list):
+            return conv_of(back, ref, which, group_list)
+
         def put(ref, group, value):
-            ref[0:tall, lanes(SIDE + group * GROUP, GROUP)] = value.astype(jnp.bfloat16)
+            size = value.shape[0]
+            ref[0:size, lanes(SIDE + group * GROUP, GROUP)] = value.astype(jnp.bfloat16)
 
         for ref in (x_b, h_b, eo_b, ei_b):
             zero = jnp.zeros((tall, SIDE), jnp.bfloat16)
@@ -407,13 +433,11 @@
         def forward_in(group_list):
             for group, value in conv(x_b, 0, group_list):
                 value = value + bias_rows[0:1, :]
-                small = jnp.exp(-jnp.abs(value))
-                soft = jnp.maximum(value, 0.0) + jnp.log1p(small)
-                sigmoid = jnp.where(value >= 0.0, 1.0, small) / (1.0 + small)
+                soft = jnp.maximum(value, 0.0) + jnp.log(1.0 + jnp.exp(-jnp.abs(value)))
                 hidden = LEAK * value + (1.0 - LEAK) * soft
                 keep = keep_rows & live(group)
                 put(h_b, group, jnp.where(keep, hidden, 0.0))
-                slope = jnp.where(keep, LEAK + (1.0 - LEAK) * sigmoid, 0.0)
+                slope = jnp.where(keep, steepness(value), 0.0)
                 slope_in[0:tall, lanes(group * GROUP, GROUP)] = slope
 
         each_group(groups, forward_in, chunk)
@@ -421,9 +445,7 @@
         def forward_out(group_list):
             for group, value in conv(h_b, 1, group_list):
                 value = value + bias_rows[1:2, :]
-                small = jnp.exp(-jnp.abs(value))
-                sigmoid = jnp.where(value >= 0.0, 1.0, small) / (1.0 + small)
-                slope = jnp.where(live(group), LEAK + (1.0 - LEAK) * sigmoid, 0.0)
+                slope = jnp.where(live(group), steepness(value), 0.0)
                 slope_out[0:tall, lanes(group * GROUP, GROUP)] = slope
 
         each_group(groups, forward_out, chunk)
@@ -432,47 +454,47 @@
             c_down.wait_recv()
             c_up.wait_recv()
             span_g = 2 * NARROW + ROWS
-            at_g = iota((tall, span_g), 0) - lead
+            at_g = iota((back, span_g), 0) - lead
             near_g = ((at_g >= 0) | (strip > 0)) & ((at_g < rows) | (strip < strips - 1))
-            pick_g = one_hot((iota((tall, span_g), 1) == at_g + NARROW) & near_g)
+            pick_g = one_hot((iota((back, span_g), 1) == at_g + NARROW) & near_g)
 
             def load_g(group_list):
                 for group in group_list:
                     span_lanes = lanes(group * GROUP, GROUP)
                     value = mat(pick_g, stack_g[:, span_lanes])
-                    g_b[0:tall, span_lanes] = value
-                    put(eo_b, group, value * slope_out[0:tall, span_lanes])
+                    g_b[0:back, span_lanes] = value
+                    put(eo_b, group, value * slope_out[0:back, span_lanes])
 
             each_group(groups, load_g, chunk)
         else:
-            sent = plan["sent"]
+            sent = min(plan["sent"], back)
             for group in range(groups):
                 hop(level, group, (finer, strip)).wait_recv()
                 span_lanes = lanes(group * GROUP, GROUP)
                 value = g_in[0:sent, span_lanes].astype(jnp.float32)
-                if sent < tall:
-                    rest = jnp.zeros((tall - sent, GROUP), jnp.float32)
+                if sent < back:
+                    rest = jnp.zeros((back - sent, GROUP), jnp.float32)
                     value = jnp.concatenate([value, rest], axis=0)
-                g_b[0:tall, span_lanes] = value
-                put(eo_b, group, value * slope_out[0:tall, span_lanes])
+                g_b[0:back, span_lanes] = value
+                put(eo_b, group, value * slope_out[0:back, span_lanes])
 
         def error_in(group_list):
-            for group, value in conv(eo_b, 2, group_list):
-                put(ei_b, group, value * slope_in[0:tall, lanes(group * GROUP, GROUP)])
+            for group, value in conv_back(eo_b, 2, group_list):
+                put(ei_b, group, value * slope_in[0:back, lanes(group * GROUP, GROUP)])
 
         each_group(groups, error_in, chunk)
 
         def back_input(group_list):
-            for group, value in conv(ei_b, 3, group_list):
+            for group, value in conv_back(ei_b, 3, group_list):
                 span_lanes = lanes(group * GROUP, GROUP)
-                value = jnp.where(live(group), value, 0.0)
-                back_b[0:tall, span_lanes] = value.astype(jnp.bfloat16)
-                total = g_b[0:tall, span_lanes] + value
-                up_b[0:tall, span_lanes] = total.astype(jnp.bfloat16)
+                value = jnp.where(live_back(group), value, 0.0)
+                back_b[0:back, span_lanes] = value.astype(jnp.bfloat16)
+                total = g_b[0:back, span_lanes] + value
+                up_b[0:back, span_lanes] = total.astype(jnp.bfloat16)
 
         if level + 1 < SECTIONS:
             after = PLANS[level + 1]
-            shape = (after["tall"], tall)
+            shape = (after["tall"], back)
             coarse_row = strip * after["rows"] + iota(shape, 0) - after["lead"]
             local_row = iota(shape, 1) - lead
             fine_row = strip * rows + local_row
@@ -489,14 +511,16 @@
 
             windows = column_windows(level)
             ready = 0
-            for begin in range(0, groups, chunk):
-                part = list(range(begin, begin + chunk))
+            begin = 0
+            for size in LAST_CHUNKS[level]:
+                part = list(range(begin, begin + size))
+                begin += size
                 back_input(part)
                 for group in part:
                     span_lanes = lanes(group * GROUP, GROUP)
-                    value = mat(row_m, up_b[0:tall, span_lanes])
+                    value = mat(row_m, up_b[0:back, span_lanes])
                     row_b[0 : after["tall"], span_lanes] = value.astype(jnp.bfloat16)
-                while ready < len(windows) and windows[ready] + 8 <= 4 * (begin + chunk):
+                while ready < len(windows) and windows[ready] + 8 <= 4 * begin:
                     start = CH * windows[ready]
                     value = mat(
                         row_b[0 : after["tall"], start : start + 2 * GROUP], cols_m[ready]
@@ -517,14 +541,14 @@
             def pile(group_list):
                 for group in group_list:
                     if isinstance(group, int):
-                        where_rows = pl.ds(group * tall, tall)
+                        where_rows = pl.ds(group * back, back)
                     else:
-                        where_rows = pl.ds(pl.multiple_of(group * tall, 16), tall)
-                    tall_x[where_rows, :] = field[0:tall, lanes(group * GROUP, 2 * GROUP)]
-                    value = error[0:tall, lanes(SIDE + group * GROUP, GROUP)]
+                        where_rows = pl.ds(pl.multiple_of(group * back, 16), back)
+                    tall_x[where_rows, :] = field[0:back, lanes(group * GROUP, 2 * GROUP)]
+                    value = error[0:back, lanes(SIDE + group * GROUP, GROUP)]
                     value = jnp.where(inner_rows, value.astype(jnp.float32), 0.0)
                     bias_acc[which : which + 1, :] += jnp.sum(value, axis=0, keepdims=True)
-                    tall_e[where_rows, 0:GROUP] = pltpu.roll(value, tall - 1, 0).astype(
+                    tall_e[where_rows, 0:GROUP] = pltpu.roll(value, back - 1, 0).astype(
                         jnp.bfloat16
                     )
                     tall_e[where_rows, GROUP : 2 * GROUP] = value.astype(jnp.bfloat16)
@@ -534,8 +558,8 @@
 
             each_group(groups, pile, chunk)
             grid_a[which] = lax.dot_general(
-                tall_x[0 : groups * tall, :],
-                tall_e[0 : groups * tall, :],
+                tall_x[0 : groups * back, :],
+                tall_e[0 : groups * back, :],
                 (((0,), (0,)), ((), ())),
                 preferred_element_type=jnp.float32,
             )
@@ -589,15 +613,7 @@
         packed,
         *sum_refs,
     )
-    gathered = sum_refs[6]
-    final[...] = gathered[...].astype(jnp.float32).reshape(PIECES * PIECE, SIDE)
-    for pair in range(9):
-        block = final[CH * pair : CH * pair + CH, :]
-        kernel_out[2 * pair] = block[:, :CH]
-        kernel_out[2 * pair + 1] = pltpu.roll(block, CH, 1)[:, :CH]
-    sums = final[9 * CH : 9 * CH + 8, :]
-    bias_out[0:1, :] = sums[0:1, :CH]
-    bias_out[1:2, :] = pltpu.roll(sums, CH, 1)[0:1, :CH]
+    sums_out[...] = sum_refs[6][...]
 
     x_down.wait_send()
     x_up.wait_send()
@@ -624,11 +640,10 @@
         chain_body,
         out_shape=(
             jax.ShapeDtypeStruct((ROWS, COLS * CH), half),
-            jax.ShapeDtypeStruct((18, CH, CH), full),
-            jax.ShapeDtypeStruct((2, CH), full),
+            jax.ShapeDtypeStruct((PIECES, PIECE, SIDE), half),
         ),
         in_specs=[in_vmem] * 4,
-        out_specs=(in_vmem, in_vmem, in_vmem),
+        out_specs=(in_vmem, in_vmem),
         scratch_shapes=[
             pltpu.VMEM((2 * BLOCK + ROWS, COLS * CH), half),
             pltpu.VMEM((2 * NARROW + ROWS, COLS * CH), half),
@@ -651,7 +666,6 @@
             pltpu.VMEM((2, 2 * GROUP, 3 * GROUP), full),
             pltpu.VMEM((2, GROUP), full),
             pltpu.VMEM((PIECES, PIECE, SIDE), full),
-            pltpu.VMEM((PIECES * PIECE, SIDE), full),
             dma((2,)), dma((2,)), dma((2,)), dma((2,)),
             dma((NEXT_WIDE // GROUP,)), dma((NEXT_WIDE // GROUP,)),
             pltpu.VMEM((RING, PIECE, SIDE), full),
@@ -673,23 +687,39 @@
     )(x, cot, taps, bias)
 
 
-def flipped(kernel):
-    return jnp.transpose(kernel[::-1, ::-1], (0, 1, 3, 2))
+def write_body(noise_in, sums_in, noise, kernel_out, bias_out, final):
+    noise[...] = noise_in[...]
+    final[...] = sums_in[...].astype(jnp.float32).reshape(PIECES * PIECE, SIDE)
+    for pair in range(9):
+        block = final[CH * pair : CH * pair + CH, :]
+        kernel_out[2 * pair] = block[:, :CH]
+        kernel_out[2 * pair + 1] = pltpu.roll(block, CH, 1)[:, :CH]
+    sums = final[9 * CH : 9 * CH + 8, :]
+    bias_out[0:1, :] = sums[0:1, :CH]
+    bias_out[1:2, :] = pltpu.roll(sums, CH, 1)[0:1, :CH]
+
+
+def write_out(noise, sums):
+    in_vmem = pl.BlockSpec(memory_space=pltpu.VMEM)
+    full = jnp.float32
+    return pl.pallas_call(
+        write_body,
+        out_shape=(
+            jax.ShapeDtypeStruct(noise.shape, noise.dtype),
+            jax.ShapeDtypeStruct((18, CH, CH), full),
+            jax.ShapeDtypeStruct((2, CH), full),
+        ),
+        in_specs=[in_vmem] * 2,
+        out_specs=(in_vmem,) * 3,
+        scratch_shapes=[pltpu.VMEM((PIECES * PIECE, SIDE), full)],
+        compiler_params=pltpu.CompilerParams(vmem_limit_bytes=8 << 20),
+    )(noise, sums)
 
 
 def local(cotangent, activations, weights, biases):
-    kernel_in, kernel_out = weights[0, 0], weights[0, 1]
-    taps = jnp.stack([kernel_in, kernel_out, flipped(kernel_out), flipped(kernel_in)])
-    taps = taps.reshape(4, 3, 3 * CH, CH)
-    edge = ((0, 0), (0, 0))
-    taps = jnp.concatenate(
-        [
-            jnp.pad(taps, edge + ((0, CH), (0, 0))),
-            jnp.pad(taps, edge + ((CH, 0), (0, 0))),
-        ],
-        axis=-1,
-    )
-    noise, kernels, sums = chain(activations[0, 0], cotangent[0], taps, biases[0])
+    taps = weights.reshape(2, 9, CH, CH)
+    noise, sums = chain(activations[0, 0], cotangent[0], taps, biases[0])
+    noise, kernels, sums = write_out(noise, sums)
     return (
         noise[None, None],
         kernels.reshape(1, 2, 3, 3, CH, CH),

time: 63.9 us -> 62.7 us (0.981)
    slice x1 -> x0, local copies, waits for them, and re-layouts: 1.06 us -> none  [local(): kernel_in, kernel_out = (weights[0, 0], weights[0, 1])]
    pallas_call x1, Pallas kernels: 58.4 us -> 57.4 us  [chain(): pl.pallas_call(chain_body, out_shape=(jax.ShapeDtypeStruct((ROWS, COLS *...]
    pallas_call x0 -> x1, Pallas kernels: none -> 0.95 us  [write_out(): pl.pallas_call(write_body, out_shape=(jax.ShapeDtypeStruct(noise.shape, n...]
    unnamed x9 -> x8, local copies, waits for them, and re-layouts: 2.62 us -> 3.53 us
where the time goes in v4:
time: 62.7 us; the launch traced here: 62.5 us
  Pallas kernels  58.3 us (93%)
  local copies, waits for them, and re-layouts  3.53 us (6%)
  between operations  0.65 us (1%)
    pallas_call x1, Pallas kernels, chain(): pl.pallas_call(chain_body, out_shape=(jax.ShapeDtypeStruct((ROWS, COLS *...  57.4 us
    unnamed x8, local copies, waits for them, and re-layouts  3.53 us

profile of v4, /device:TPU:7, one launch (start us, length us, event | category | flops | bytes accessed | tf_op | source)
XLA Modules:
  0.0 62.5 jit_solution(11385319565432111338)
XLA Ops:
  0.6 0.0 copy-start.3
  0.6 0.7 %copy-done.3 = f32[1,2,64]{2,1,0:T(2,128)S(1)} copy-done((f32[1,2,64]{2,1,0:T(2,128)S(1)}, f32[1,2,64]{2,1,0:T(2,128)}, u32[]{:S(2)}) %copy-start.3) | copy-done | bytes 536
  1.3 0.0 copy-start
  1.3 1.0 %copy-done = bf16[1,2,3,3,64,64]{5,4,3,2,1,0:T(8,128)(2,1)S(1)} copy-done((bf16[1,2,3,3,64,64]{5,4,3,2,1,0:T(8,128)(2,1)S(1)}, bf16[1,2,3,3,64,64]{5,4,3,2,1,0:T(8,128)(2,1)}, u32[]{:S(2)}) %copy-start) | copy-done | bytes 147480
  2.3 0.0 copy-start.1
  2.3 0.9 %copy-done.1 = bf16[1,1,64,2048]{3,2,1,0:T(8,128)(2,1)S(1)} copy-done((bf16[1,1,64,2048]{3,2,1,0:T(8,128)(2,1)S(1)}, bf16[1,1,64,2048]{3,2,1,0:T(8,128)(2,1)}, u32[]{:S(2)}) %copy-start.1) | copy-done | bytes 262168
  3.2 0.0 copy-start.2
  3.2 0.9 %copy-done.2 = bf16[1,64,2048]{2,1,0:T(8,128)(2,1)S(1)} copy-done((bf16[1,64,2048]{2,1,0:T(8,128)(2,1)S(1)}, bf16[1,64,2048]{2,1,0:T(8,128)(2,1)}, u32[]{:S(2)}) %copy-start.2) | copy-done | bytes 262168
  4.2 57.4 %shard_map.67 = (bf16[64,2048]{1,0:T(8,128)(2,1)S(1)}, bf16[16,40,128]{2,1,0:T(8,128)(2,1)S(1)}) custom-call(bf16[64,2048]{1,0:T(8,128)(2,1)S(1)} %bitcast.8, bf16[64,2048]{1,0:T(8,128)(2,1)S(1)} %bitcast.9, bf16[2,9,64,64]{3,2,1,0:T(8,128)(2,1)S(1)} %bitcast.7, f32[2,64]{1,0:T(2,128)S(1)} %bitcast.10), custom_call_target="tpu_custom_call" | custom-call | tf_op jit(solution)/shard_map/pallas_call | solution.py:639
  61.5 0.9 %shard_map.68 = (bf16[64,2048]{1,0:T(8,128)(2,1)}, f32[18,64,64]{2,1,0:T(8,128)}, f32[2,64]{1,0:T(2,128)}) custom-call(bf16[64,2048]{1,0:T(8,128)(2,1)S(1)} %get-tuple-element.8.noise_in, bf16[16,40,128]{2,1,0:T(8,128)(2,1)S(1)} %get-tuple-element.9.sums_in), custom_call_target="tpu_custom_call" | custom-call | tf_op jit(solution)/shard_map/pallas_call | solution.py:705
Async XLA Ops:
  0.6 0.7 %copy-start.3 = (f32[1,2,64]{2,1,0:T(2,128)S(1)}, f32[1,2,64]{2,1,0:T(2,128)}, u32[]{:S(2)}) copy-start(f32[1,2,64]{2,1,0:T(2,128)} %param.7) | copy-start | bytes 1540
  1.3 1.0 %copy-start = (bf16[1,2,3,3,64,64]{5,4,3,2,1,0:T(8,128)(2,1)S(1)}, bf16[1,2,3,3,64,64]{5,4,3,2,1,0:T(8,128)(2,1)}, u32[]{:S(2)}) copy-start(bf16[1,2,3,3,64,64]{5,4,3,2,1,0:T(8,128)(2,1)} %param.6) | copy-start | bytes 442372
  2.3 0.9 %copy-start.1 = (bf16[1,1,64,2048]{3,2,1,0:T(8,128)(2,1)S(1)}, bf16[1,1,64,2048]{3,2,1,0:T(8,128)(2,1)}, u32[]{:S(2)}) copy-start(bf16[1,1,64,2048]{3,2,1,0:T(8,128)(2,1)} %param.5) | copy-start | bytes 786436
  3.2 0.9 %copy-start.2 = (bf16[1,64,2048]{2,1,0:T(8,128)(2,1)S(1)}, bf16[1,64,2048]{2,1,0:T(8,128)(2,1)}, u32[]{:S(2)}) copy-start(bf16[1,64,2048]{2,1,0:T(8,128)(2,1)} %param.4) | copy-start | bytes 786436

commit v5 on v4

--- a/solution.py
+++ b/solution.py
@@ -108,7 +108,13 @@
 BLOCK = 32
 NARROW = 16
 CHUNKS = (4, 3, 5, 4)
-LAST_CHUNKS = ((4, 2, 2), (3, 3), (5,))
+WAIT, INNER, OUTER = range(3)
+STEPS = (
+    ((INNER, 0, 4), (OUTER, 0, 3), (INNER, 4, 8), (OUTER, 3, 6), (OUTER, 6, 8)),
+    ((WAIT, 0, 4), (INNER, 0, 3), (OUTER, 0, 2), (WAIT, 4, 6), (INNER, 3, 6), (OUTER, 2, 6)),
+    ((WAIT, 0, 5), (INNER, 0, 5), (OUTER, 0, 5)),
+    ((WAIT, 0, 4), (INNER, 0, 4)),
+)
 
 
 def plans():
@@ -215,7 +221,7 @@
     x, cot, taps, bias, noise, sums_out,
     stack, stack_g, bands, x_b, h_b, eo_b, ei_b, slope_in, slope_out, g_b, back_b, up_b,
     row_b, g_out, g_in, cols_m, tall_x, tall_e, grid_a, bias_acc,
-    packed, x_send, x_recv, c_send, c_recv, g_send, g_recv, *sum_refs,
+    packed, taps_v, bias_v, local_sem, x_send, x_recv, c_send, c_recv, g_send, g_recv, *sum_refs,
 ):
     section = lax.axis_index("section")
     strip = lax.axis_index("strip")
@@ -225,6 +231,14 @@
     coarser = lax.rem(section + 1, SECTIONS)
     finer = lax.rem(section + SECTIONS - 1, SECTIONS)
 
+    fetches = [
+        pltpu.make_async_copy(taps, taps_v, local_sem.at[0]),
+        pltpu.make_async_copy(bias, bias_v, local_sem.at[1]),
+        pltpu.make_async_copy(x, stack.at[pl.ds(BLOCK, ROWS)], local_sem.at[2]),
+        pltpu.make_async_copy(cot, stack_g.at[pl.ds(NARROW, ROWS)], local_sem.at[3]),
+    ]
+    for fetch in fetches:
+        fetch.start()
     barrier = pltpu.get_barrier_semaphore()
     partner, along_y, along_z = sum_peers(strip)[3:]
     peers = [(section, below), (section, above), (coarser, strip), (finer, strip)]
@@ -233,13 +247,14 @@
         pl.semaphore_signal(barrier, inc=1, device_id=peer, device_id_type=MESH)
 
     bands[...] = jnp.zeros_like(bands)
+    fetches[0].wait()
     blank = jnp.zeros((CH, CH), jnp.float32)
     for which, (source, flip) in enumerate(((0, False), (1, False), (1, True), (0, True))):
         for dy in range(3):
             tap_list = []
             for dx in range(3):
                 at = (2 - dy) * 3 + 2 - dx if flip else dy * 3 + dx
-                tap_list.append(taps[source, at].astype(jnp.float32))
+                tap_list.append(taps_v[source, at].astype(jnp.float32))
             tap_list.append(blank)
             for index in range(4):
                 pair = (tap_list[index], tap_list[index - 1])
@@ -304,9 +319,9 @@
         c_down.start()
         c_up.start()
 
-    stack[BLOCK : BLOCK + ROWS, :] = x[...]
-    stack_g[NARROW : NARROW + ROWS, :] = cot[...]
-    bias_rows = jnp.concatenate([bias[...]] * 4, axis=1)
+    for fetch in fetches[1:]:
+        fetch.wait()
+    bias_rows = jnp.concatenate([bias_v[...]] * 4, axis=1)
 
     def hop(level, group, peer):
         part = (pl.ds(0, PLANS[level]["sent"]), pl.ds(group * GROUP, GROUP))
@@ -468,21 +483,21 @@
             each_group(groups, load_g, chunk)
         else:
             sent = min(plan["sent"], back)
-            for group in range(groups):
-                hop(level, group, (finer, strip)).wait_recv()
-                span_lanes = lanes(group * GROUP, GROUP)
-                value = g_in[0:sent, span_lanes].astype(jnp.float32)
-                if sent < back:
-                    rest = jnp.zeros((back - sent, GROUP), jnp.float32)
-                    value = jnp.concatenate([value, rest], axis=0)
-                g_b[0:back, span_lanes] = value
-                put(eo_b, group, value * slope_out[0:back, span_lanes])
+
+            def arrive(group_list):
+                for group in group_list:
+                    hop(level, group, (finer, strip)).wait_recv()
+                    span_lanes = lanes(group * GROUP, GROUP)
+                    value = g_in[0:sent, span_lanes].astype(jnp.float32)
+                    if sent < back:
+                        rest = jnp.zeros((back - sent, GROUP), jnp.float32)
+                        value = jnp.concatenate([value, rest], axis=0)
+                    g_b[0:back, span_lanes] = value
+                    put(eo_b, group, value * slope_out[0:back, span_lanes])
 
         def error_in(group_list):
             for group, value in conv_back(eo_b, 2, group_list):
                 put(ei_b, group, value * slope_in[0:back, lanes(group * GROUP, GROUP)])
-
-        each_group(groups, error_in, chunk)
 
         def back_input(group_list):
             for group, value in conv_back(ei_b, 3, group_list):
@@ -510,17 +525,21 @@
             row_m = jnp.where(real, row_m, 0.0).astype(jnp.bfloat16)
 
             windows = column_windows(level)
-            ready = 0
-            begin = 0
-            for size in LAST_CHUNKS[level]:
-                part = list(range(begin, begin + size))
-                begin += size
+
+        ready = 0
+        for kind, begin, end in STEPS[level]:
+            part = list(range(begin, end))
+            if kind == WAIT:
+                arrive(part)
+            elif kind == INNER:
+                error_in(part)
+            else:
                 back_input(part)
                 for group in part:
                     span_lanes = lanes(group * GROUP, GROUP)
                     value = mat(row_m, up_b[0:back, span_lanes])
                     row_b[0 : after["tall"], span_lanes] = value.astype(jnp.bfloat16)
-                while ready < len(windows) and windows[ready] + 8 <= 4 * begin:
+                while ready < len(windows) and windows[ready] + 8 <= 4 * end:
                     start = CH * windows[ready]
                     value = mat(
                         row_b[0 : after["tall"], start : start + 2 * GROUP], cols_m[ready]
@@ -530,7 +549,6 @@
                     )
                     hop(level + 1, ready, (coarser, strip)).start()
                     ready += 1
-            assert ready == len(windows)
 
         if level + 1 < SECTIONS:
             save_noise(level)
@@ -642,7 +660,7 @@
             jax.ShapeDtypeStruct((ROWS, COLS * CH), half),
             jax.ShapeDtypeStruct((PIECES, PIECE, SIDE), half),
         ),
-        in_specs=[in_vmem] * 4,
+        in_specs=[pl.BlockSpec(memory_space=pltpu.HBM)] * 4,
         out_specs=(in_vmem, in_vmem),
         scratch_shapes=[
             pltpu.VMEM((2 * BLOCK + ROWS, COLS * CH), half),
@@ -666,6 +684,9 @@
             pltpu.VMEM((2, 2 * GROUP, 3 * GROUP), full),
             pltpu.VMEM((2, GROUP), full),
             pltpu.VMEM((PIECES, PIECE, SIDE), full),
+            pltpu.VMEM((2, 9, CH, CH), half),
+            pltpu.VMEM((2, CH), full),
+            dma((4,)),
             dma((2,)), dma((2,)), dma((2,)), dma((2,)),
             dma((NEXT_WIDE // GROUP,)), dma((NEXT_WIDE // GROUP,)),
             pltpu.VMEM((RING, PIECE, SIDE), full),
@@ -682,7 +703,7 @@
             dma((RING,)), dma((RING,)),
         ],
         compiler_params=pltpu.CompilerParams(
-            collective_id=0, has_side_effects=True, vmem_limit_bytes=48 << 20
+            collective_id=0, has_side_effects=True, vmem_limit_bytes=67043328
         ),
     )(x, cot, taps, bias)
 
@@ -712,7 +733,7 @@
         in_specs=[in_vmem] * 2,
         out_specs=(in_vmem,) * 3,
         scratch_shapes=[pltpu.VMEM((PIECES * PIECE, SIDE), full)],
-        compiler_params=pltpu.CompilerParams(vmem_limit_bytes=8 << 20),
+        compiler_params=pltpu.CompilerParams(vmem_limit_bytes=67043328),
     )(noise, sums)
 
 

time: 62.7 us -> 60.8 us (0.970)
  local copies, waits for them, and re-layouts: 3.53 us -> 0 us
  Pallas kernels: 58.3 us -> 60 us
    unnamed x8 -> x0, local copies, waits for them, and re-layouts: 3.53 us -> none
    pallas_call x1, Pallas kernels: 0.95 us -> 1.94 us  [write_out(): pl.pallas_call(write_body, out_shape=(jax.ShapeDtypeStruct(noise.shape, n...]
    pallas_call x1, Pallas kernels: 57.4 us -> 58.1 us  [chain(): pl.pallas_call(chain_body, out_shape=(jax.ShapeDtypeStruct((ROWS, COLS *...]
where the time goes in v5:
time: 60.8 us; the launch traced here: 60.7 us
  Pallas kernels  60 us (99%)
  between operations  0.64 us (1%)
    pallas_call x1, Pallas kernels, chain(): pl.pallas_call(chain_body, out_shape=(jax.ShapeDtypeStruct((ROWS, COLS *...  58.1 us
    pallas_call x1, Pallas kernels, write_out(): pl.pallas_call(write_body, out_shape=(jax.ShapeDtypeStruct(noise.shape, n...  1.94 us

profile of v5, /device:TPU:7, one launch (start us, length us, event | category | flops | bytes accessed | tf_op | source)
XLA Modules:
  0.0 60.7 jit_solution(1492838185851564285)
XLA Ops:
  0.6 58.1 %shard_map.67 = (bf16[64,2048]{1,0:T(8,128)(2,1)}, bf16[16,40,128]{2,1,0:T(8,128)(2,1)}) custom-call(bf16[64,2048]{1,0:T(8,128)(2,1)} %bitcast.8, bf16[64,2048]{1,0:T(8,128)(2,1)} %bitcast.9, bf16[2,9,64,64]{3,2,1,0:T(8,128)(2,1)} %bitcast.7, f32[2,64]{1,0:T(2,128)} %bitcast.10), custom_call_target="tpu_custom_call" | custom-call | tf_op jit(solution)/shard_map/pallas_call | solution.py:657
  58.7 1.9 %shard_map.68 = (bf16[64,2048]{1,0:T(8,128)(2,1)}, f32[18,64,64]{2,1,0:T(8,128)}, f32[2,64]{1,0:T(2,128)}) custom-call(bf16[64,2048]{1,0:T(8,128)(2,1)} %get-tuple-element.8.noise_in, bf16[16,40,128]{2,1,0:T(8,128)(2,1)} %get-tuple-element.9.sums_in), custom_call_target="tpu_custom_call" | custom-call | tf_op jit(solution)/shard_map/pallas_call | solution.py:726

commit v6 on v5

--- a/solution.py
+++ b/solution.py
@@ -25,39 +25,54 @@
 
 
 def strip_sum(
-    remote, strip, scale, meanwhile, src, pair_in, y_sum, y_out, y_in, z_out, z_in, gathered,
+    remote, strip, scale, meanwhile, src, src_half, pair_in, y_sum, y_out, y_in, z_out, z_in, gathered,
     pair_send, pair_recv, y_send, y_recv, z_send, z_recv, g_send, g_recv, p_send, p_recv,
 ):
     core, row, deep, partner, along_y, along_z = sum_peers(strip)
     mine = core * RING
-    swap = remote(
-        src.at[pl.ds((1 - core) * RING, RING)], pair_in, pair_send, pair_recv, partner
-    )
-    swap.start()
-    swap.wait()
-    both = src[pl.ds(mine, RING)] + pair_in[...]
-    y_sum[...] = both
-    y_out[...] = both.astype(jnp.bfloat16)
-    scatter = []
-    for step in range(1, RING):
+    other = (1 - core) * RING
+    order = sorted(range(1, RING), key=lambda step: -min(step, RING - step))
+    pieces = [lax.rem(row + step, RING) for step in order] + [row]
+    swaps = []
+    for at, index in enumerate(pieces):
+        src_half[other + index] = src[other + index].astype(jnp.bfloat16)
+    for at, index in enumerate(pieces):
         copy = remote(
-            y_out.at[lax.rem(row + step, RING)],
+            src_half.at[other + index],
+            pair_in.at[index],
+            pair_send.at[at],
+            pair_recv.at[at],
+            partner,
+        )
+        copy.start()
+        swaps.append(copy)
+    scatter = [None] * (RING - 1)
+    for at, index in enumerate(pieces):
+        swaps[at].wait_recv()
+        both = src[mine + index] + pair_in[index].astype(jnp.float32)
+        if at == RING - 1:
+            y_sum[...] = both
+            break
+        step = order[at]
+        y_out[index] = both.astype(jnp.bfloat16)
+        copy = remote(
+            y_out.at[index],
             y_in.at[step - 1],
             y_send.at[step - 1],
             y_recv.at[step - 1],
             along_y[step - 1],
         )
         copy.start()
-        scatter.append(copy)
+        scatter[step - 1] = copy
     meanwhile()
-    total = y_sum[row]
+    total = y_sum[...]
     for step in range(1, RING):
         scatter[step - 1].wait_recv()
         total = total + y_in[step - 1].astype(jnp.float32)
     z_out[...] = total.astype(jnp.bfloat16)
     z_in[deep] = total.astype(jnp.bfloat16)
     trade = []
-    for step in range(1, RING):
+    for step in order:
         copy = remote(
             z_out, z_in.at[deep], z_send.at[step - 1], z_recv.at[step - 1], along_z[step - 1]
         )
@@ -70,8 +85,8 @@
         total = total + z_in[index].astype(jnp.float32)
     own = mine + row
     gathered[own] = (total * scale).astype(jnp.bfloat16)
-    gather = []
-    for step in range(1, RING):
+    gather = [None] * (RING - 1)
+    for step in order:
         copy = remote(
             gathered.at[own],
             gathered.at[own],
@@ -80,12 +95,12 @@
             along_y[step - 1],
         )
         copy.start()
-        gather.append(copy)
+        gather[step - 1] = copy
     passed = [
         remote(gathered.at[own], gathered.at[own], p_send.at[0], p_recv.at[0], partner)
     ]
     passed[0].start()
-    for step in range(1, RING):
+    for step in reversed(order):
         gather[step - 1].wait_recv()
         came = mine + lax.rem(row + RING - step, RING)
         copy = remote(
@@ -95,7 +110,7 @@
         passed.append(copy)
     for copy in passed:
         copy.wait_recv()
-    for copy in scatter + trade + gather + passed:
+    for copy in swaps + scatter + trade + gather + passed:
         copy.wait_send()
 
 
@@ -631,7 +646,7 @@
         packed,
         *sum_refs,
     )
-    sums_out[...] = sum_refs[6][...]
+    sums_out[...] = sum_refs[7][...]
 
     x_down.wait_send()
     x_up.wait_send()
@@ -689,14 +704,15 @@
             dma((4,)),
             dma((2,)), dma((2,)), dma((2,)), dma((2,)),
             dma((NEXT_WIDE // GROUP,)), dma((NEXT_WIDE // GROUP,)),
-            pltpu.VMEM((RING, PIECE, SIDE), full),
-            pltpu.VMEM((RING, PIECE, SIDE), full),
+            pltpu.VMEM((PIECES, PIECE, SIDE), half),
+            pltpu.VMEM((RING, PIECE, SIDE), half),
+            pltpu.VMEM((PIECE, SIDE), full),
             pltpu.VMEM((RING, PIECE, SIDE), half),
             pltpu.VMEM((RING - 1, PIECE, SIDE), half),
             pltpu.VMEM((PIECE, SIDE), half),
             pltpu.VMEM((RING, PIECE, SIDE), half),
             pltpu.VMEM((PIECES, PIECE, SIDE), half),
-            dma, dma,
+            dma((RING,)), dma((RING,)),
             dma((RING - 1,)), dma((RING - 1,)),
             dma((RING - 1,)), dma((RING - 1,)),
             dma((RING - 1,)), dma((RING - 1,)),

time: 60.8 us -> 58.3 us (0.959)
  Pallas kernels: 60 us -> 57.5 us
    pallas_call x1, Pallas kernels: 58.1 us -> 55.6 us  [chain(): pl.pallas_call(chain_body, out_shape=(jax.ShapeDtypeStruct((ROWS, COLS *...]
where the time goes in v6:
time: 58.3 us; the launch traced here: 58.2 us
  Pallas kernels  57.5 us (99%)
  between operations  0.64 us (1%)
    pallas_call x1, Pallas kernels, chain(): pl.pallas_call(chain_body, out_shape=(jax.ShapeDtypeStruct((ROWS, COLS *...  55.6 us
    pallas_call x1, Pallas kernels, write_out(): pl.pallas_call(write_body, out_shape=(jax.ShapeDtypeStruct(noise.shape, n...  1.94 us

profile of v6, /device:TPU:7, one launch (start us, length us, event | category | flops | bytes accessed | tf_op | source)
XLA Modules:
  0.0 58.2 jit_solution(13786624337017355390)
XLA Ops:
  0.6 55.6 %shard_map.67 = (bf16[64,2048]{1,0:T(8,128)(2,1)}, bf16[16,40,128]{2,1,0:T(8,128)(2,1)}) custom-call(bf16[64,2048]{1,0:T(8,128)(2,1)} %bitcast.8, bf16[64,2048]{1,0:T(8,128)(2,1)} %bitcast.9, bf16[2,9,64,64]{3,2,1,0:T(8,128)(2,1)} %bitcast.7, f32[2,64]{1,0:T(2,128)} %bitcast.10), custom_call_target="tpu_custom_call" | custom-call | tf_op jit(solution)/shard_map/pallas_call | solution.py:672
  56.2 1.9 %shard_map.68 = (bf16[64,2048]{1,0:T(8,128)(2,1)}, f32[18,64,64]{2,1,0:T(8,128)}, f32[2,64]{1,0:T(2,128)}) custom-call(bf16[64,2048]{1,0:T(8,128)(2,1)} %get-tuple-element.8.noise_in, bf16[16,40,128]{2,1,0:T(8,128)(2,1)} %get-tuple-element.9.sums_in), custom_call_target="tpu_custom_call" | custom-call | tf_op jit(solution)/shard_map/pallas_call | solution.py:742

commit v7 on v6

--- a/solution.py
+++ b/solution.py
@@ -126,8 +126,11 @@
 WAIT, INNER, OUTER = range(3)
 STEPS = (
     ((INNER, 0, 4), (OUTER, 0, 3), (INNER, 4, 8), (OUTER, 3, 6), (OUTER, 6, 8)),
-    ((WAIT, 0, 4), (INNER, 0, 3), (OUTER, 0, 2), (WAIT, 4, 6), (INNER, 3, 6), (OUTER, 2, 6)),
-    ((WAIT, 0, 5), (INNER, 0, 5), (OUTER, 0, 5)),
+    (
+        (WAIT, 0, 4), (INNER, 0, 3), (OUTER, 0, 2),
+        (WAIT, 4, 6), (INNER, 3, 6), (OUTER, 2, 4), (OUTER, 4, 6),
+    ),
+    ((WAIT, 0, 3), (INNER, 0, 2), (WAIT, 3, 5), (INNER, 2, 5), (OUTER, 0, 3), (OUTER, 3, 5)),
     ((WAIT, 0, 4), (INNER, 0, 4)),
 )
 

time: 58.3 us -> 58.7 us (level)
  no operation moved by 1% of the time
where the time goes in v7:
time: 58.7 us; the launch traced here: 58.5 us
  Pallas kernels  57.9 us (99%)
  between operations  0.64 us (1%)
    pallas_call x1, Pallas kernels, chain(): pl.pallas_call(chain_body, out_shape=(jax.ShapeDtypeStruct((ROWS, COLS *...  55.9 us
    pallas_call x1, Pallas kernels, write_out(): pl.pallas_call(write_body, out_shape=(jax.ShapeDtypeStruct(noise.shape, n...  1.94 us

profile of v7, /device:TPU:7, one launch (start us, length us, event | category | flops | bytes accessed | tf_op | source)
XLA Modules:
  0.0 58.5 jit_solution(8561670821908090673)
XLA Ops:
  0.6 55.9 %shard_map.67 = (bf16[64,2048]{1,0:T(8,128)(2,1)}, bf16[16,40,128]{2,1,0:T(8,128)(2,1)}) custom-call(bf16[64,2048]{1,0:T(8,128)(2,1)} %bitcast.8, bf16[64,2048]{1,0:T(8,128)(2,1)} %bitcast.9, bf16[2,9,64,64]{3,2,1,0:T(8,128)(2,1)} %bitcast.7, f32[2,64]{1,0:T(2,128)} %bitcast.10), custom_call_target="tpu_custom_call" | custom-call | tf_op jit(solution)/shard_map/pallas_call | solution.py:675
  56.6 1.9 %shard_map.68 = (bf16[64,2048]{1,0:T(8,128)(2,1)}, f32[18,64,64]{2,1,0:T(8,128)}, f32[2,64]{1,0:T(2,128)}) custom-call(bf16[64,2048]{1,0:T(8,128)(2,1)} %get-tuple-element.8.noise_in, bf16[16,40,128]{2,1,0:T(8,128)(2,1)} %get-tuple-element.9.sums_in), custom_call_target="tpu_custom_call" | custom-call | tf_op jit(solution)/shard_map/pallas_call | solution.py:745
